TPU v7x, 32 devices: a whole 2x2x4 slice. The times are simulated.
32 devices in a mesh: dp: 8 (over z, core), tensor: 4 (over y, x).
Axes of the slice: x: 2, y: 2, z: 4, core: 2. Of those that a mesh axis runs over, the one named last changes fastest.
Arguments:
- tokens: bfloat16 [8192, 2048], P(('dp', 'tensor')), may hold values from -6 to 6
- cotangent: bfloat16 [8192, 2048], P(('dp', 'tensor')), may hold values from -6 to 6
- lengths: int32 [8], P('dp'), may hold values from 256 to 1024, as said below
- norm_gain: bfloat16 [2048], P('dp'), may hold values from 0.5 to 1.5
- norm_bias: bfloat16 [2048], P('dp'), may hold values from -1.75 to 1.75
- query_weight: bfloat16 [2048, 2048], P('dp', 'tensor'), may hold values from -0.125 to 0.125
- key_weight: bfloat16 [2048, 2048], P('dp', 'tensor'), may hold values from -0.125 to 0.125
- value_weight: bfloat16 [2048, 2048], P('dp', 'tensor'), may hold values from -0.125 to 0.125
- qkv_bias: bfloat16 [3, 32, 64], P(None, 'tensor', 'dp'), may hold values from -1.75 to 1.75
- proj_weight: bfloat16 [2048, 2048], P('tensor', 'dp'), may hold values from -1.5 to 1.5
- proj_bias: bfloat16 [2048], P('dp'), may hold values from -1.75 to 1.75
- up_weight: bfloat16 [2048, 8192], P('dp', 'tensor'), may hold values from -0.125 to 0.125
- up_bias: bfloat16 [128, 64], P('tensor', 'dp'), may hold values from -3 to 3
- down_weight: bfloat16 [8192, 2048], P('tensor', 'dp'), may hold values from -0.0625 to 0.0625
- down_bias: bfloat16 [2048], P('dp'), may hold values from -1.75 to 1.75
Outputs:
- output: bfloat16 [8192, 2048], P(('dp', 'tensor'))
- input_grad: float32 [8192, 2048], P(('dp', 'tensor'))
- norm_gain_grad: float32 [2048], P('dp')
- norm_bias_grad: float32 [2048], P('dp')
- query_grad: float32 [2048, 2048], P('dp', 'tensor')
- key_grad: float32 [2048, 2048], P('dp', 'tensor')
- value_grad: float32 [2048, 2048], P('dp', 'tensor')
- qkv_bias_grad: float32 [3, 32, 64], P(None, 'tensor', 'dp')
- proj_grad: float32 [2048, 2048], P('tensor', 'dp')
- proj_bias_grad: float32 [2048], P('dp')
- up_grad: float32 [2048, 8192], P('dp', 'tensor')
- up_bias_grad: float32 [128, 64], P('tensor', 'dp')
- down_grad: float32 [8192, 2048], P('tensor', 'dp')
- down_bias_grad: float32 [2048], P('dp')
Inputs may be any that keep to these rules, and one draw needn't show every extreme that they name: `lengths`: each slot holds one sequence from its first row; in every draw some slot is full, of length 1024.
All inputs are finite; a program needn't handle non-finite values.
Results may differ from a plain program's by a relative error of at most 0.017.
Values may be sent and summed in bfloat16 or wider, within the bound.
No kernel may reach another device: no remote copies, remote signals or barrier semaphores. Data moves between devices by JAX's collectives and lax.ppermute only.
A program may use at most 192 MiB of HBM per device.

v0:
```python
import jax
import jax.numpy as jnp
from jax import lax
from jax.sharding import PartitionSpec as P

HEAD = 64
ROT = 32


norm_eps = 1e-05
masked_score = -1000000000.0


def layer_norm(rows, gain, shift):
    center = rows - jnp.mean(rows, axis=-1, keepdims=True)
    spread = jnp.mean(center * center, axis=-1, keepdims=True)
    return center * lax.rsqrt(spread + norm_eps) * gain + shift


def rotary_tables(count, rot_dims):
    half = rot_dims // 2
    freq = 1.0 / 10000.0 ** (jnp.arange(half, dtype=jnp.float32) * (2.0 / rot_dims))
    angle = jnp.arange(count, dtype=jnp.float32)[:, None] * freq[None, :]
    return (jnp.cos(angle), jnp.sin(angle))


def rotary(field, cosine, sine):
    half = cosine.shape[1]
    first = field[..., :half]
    second = field[..., half : 2 * half]
    cos_b = cosine[:, None, :]
    sin_b = sine[:, None, :]
    return jnp.concatenate(
        [first * cos_b - second * sin_b, second * cos_b + first * sin_b, field[..., 2 * half :]],
        axis=-1,
    )


def inner_rows(left, right):
    return lax.dot_general(
        left, right, (((0,), (0,)), ((), ())), preferred_element_type=jnp.float32
    )


def times_trans(left, right):
    return lax.dot_general(
        left, right, (((1,), (1,)), ((), ())), preferred_element_type=jnp.float32
    )


def product(left, right):
    return jnp.dot(left, right, preferred_element_type=jnp.float32)


def on_device(
    tokens,
    cotangent,
    lengths,
    norm_gain,
    norm_bias,
    query_weight,
    key_weight,
    value_weight,
    qkv_bias,
    proj_weight,
    proj_bias,
    up_weight,
    up_bias,
    down_weight,
    down_bias,
):
    tok_rows = tokens.shape[0]
    seq_rows = tok_rows * lax.axis_size("tensor")
    block_rows = min(512, seq_rows)
    blocks = seq_rows // block_rows
    scale = HEAD ** (-0.5)
    (
        n_gain,
        n_shift,
        w_query,
        w_key,
        w_value,
        b_heads,
        w_proj,
        b_proj,
        w_up,
        b_up,
        w_down,
        b_down,
    ) = (
        lax.all_gather(norm_gain, "dp", axis=0, tiled=True),
        lax.all_gather(norm_bias, "dp", axis=0, tiled=True),
        lax.all_gather(query_weight, "dp", axis=0, tiled=True),
        lax.all_gather(key_weight, "dp", axis=0, tiled=True),
        lax.all_gather(value_weight, "dp", axis=0, tiled=True),
        lax.all_gather(qkv_bias, "dp", axis=2, tiled=True),
        lax.all_gather(proj_weight, "dp", axis=1, tiled=True),
        lax.all_gather(proj_bias, "dp", axis=0, tiled=True),
        lax.all_gather(up_weight, "dp", axis=0, tiled=True),
        lax.all_gather(up_bias, "dp", axis=1, tiled=True),
        lax.all_gather(down_weight, "dp", axis=1, tiled=True),
        lax.all_gather(down_bias, "dp", axis=0, tiled=True),
    )
    heads_here = b_heads.shape[1]
    inputs = tokens.astype(jnp.float32)
    normed_low = layer_norm(inputs, n_gain, n_shift).astype(jnp.bfloat16)
    gathered = lax.all_gather(normed_low, "tensor", axis=0, tiled=True)
    q_pre = product(gathered, w_query) + b_heads[0].reshape(-1)
    k_pre = product(gathered, w_key) + b_heads[1].reshape(-1)
    v_pre = product(gathered, w_value) + b_heads[2].reshape(-1)
    cosine, sine = rotary_tables(seq_rows, ROT)
    q_rot = rotary(q_pre.reshape(seq_rows, heads_here, HEAD), cosine, sine).astype(jnp.bfloat16)
    k_rot = rotary(k_pre.reshape(seq_rows, heads_here, HEAD), cosine, sine).astype(jnp.bfloat16)
    v_low = v_pre.reshape(seq_rows, heads_here, HEAD).astype(jnp.bfloat16)
    slot_len = lengths[0]
    key_pos = jnp.arange(seq_rows)
    key_live = key_pos < slot_len

    def block_scores(q_block, start):
        logits = (
            jnp.einsum("qhe,khe->hqk", q_block, k_rot, preferred_element_type=jnp.float32) * scale
        )
        query_pos = start + jnp.arange(q_block.shape[0])
        allowed = key_live[None, :] & (key_pos[None, :] <= query_pos[:, None])
        return jnp.where(allowed[None], logits, masked_score)

    def forward_block(index):
        start = index * block_rows
        q_block = lax.dynamic_slice_in_dim(q_rot, start, block_rows, 0)
        logits = block_scores(q_block, start)
        top = jnp.max(logits, axis=-1, keepdims=True)
        expo = jnp.exp(logits - top)
        total = jnp.sum(expo, axis=-1, keepdims=True)
        probs_low = (expo / total).astype(jnp.bfloat16)
        mixed = jnp.einsum("hqk,khe->qhe", probs_low, v_low, preferred_element_type=jnp.float32)
        return (mixed.astype(jnp.bfloat16), top + jnp.log(total))

    mixed_blocks, log_totals = lax.map(forward_block, jnp.arange(blocks))
    mixed_low = mixed_blocks.reshape(seq_rows, heads_here * HEAD)
    attn_part = product(mixed_low, w_proj)
    up_pre = product(gathered, w_up) + b_up.reshape(-1)
    act_low = jax.nn.gelu(up_pre, approximate=True).astype(jnp.bfloat16)
    mlp_part = product(act_low, w_down)
    branch_total = lax.psum_scatter(
        (attn_part + mlp_part).astype(jnp.bfloat16), "tensor", scatter_dimension=0, tiled=True
    ).astype(jnp.float32)
    output = (inputs + branch_total + b_proj + b_down).astype(jnp.bfloat16)
    own_pos = lax.axis_index("tensor") * tok_rows + jnp.arange(tok_rows)
    live_rows = (own_pos < slot_len).astype(jnp.float32)[:, None]
    grad_local = cotangent.astype(jnp.float32) * live_rows
    grad_all = lax.all_gather(grad_local.astype(jnp.bfloat16), "tensor", axis=0, tiled=True)
    bw_gain, bw_query, bw_key, bw_value, bw_proj, bw_up, bw_down = (
        lax.all_gather(norm_gain, "dp", axis=0, tiled=True),
        lax.all_gather(query_weight, "dp", axis=0, tiled=True),
        lax.all_gather(key_weight, "dp", axis=0, tiled=True),
        lax.all_gather(value_weight, "dp", axis=0, tiled=True),
        lax.all_gather(proj_weight, "dp", axis=1, tiled=True),
        lax.all_gather(up_weight, "dp", axis=0, tiled=True),
        lax.all_gather(down_weight, "dp", axis=1, tiled=True),
    )
    out_bias_grad = jnp.sum(grad_all, axis=0, dtype=jnp.float32)
    down_grad = inner_rows(act_low, grad_all)
    proj_grad = inner_rows(mixed_low, grad_all)
    act_grad = times_trans(grad_all, bw_down)
    _, gelu_back = jax.vjp(lambda value: jax.nn.gelu(value, approximate=True), up_pre)
    up_pre_grad = gelu_back(act_grad)[0].astype(jnp.bfloat16)
    up_grad = inner_rows(gathered, up_pre_grad)
    up_bias_grad = jnp.sum(up_pre_grad, axis=0, dtype=jnp.float32).reshape(b_up.shape)
    mlp_input_grad = times_trans(up_pre_grad, bw_up)
    mixed_grad = (
        times_trans(grad_all, bw_proj).astype(jnp.bfloat16).reshape(seq_rows, heads_here, HEAD)
    )

    def backward_block(carry, index):
        key_acc, value_acc = carry
        start = index * block_rows
        q_block = lax.dynamic_slice_in_dim(q_rot, start, block_rows, 0)
        grad_block = lax.dynamic_slice_in_dim(mixed_grad, start, block_rows, 0)
        logits = block_scores(q_block, start)
        probs = jnp.exp(logits - log_totals[index])
        probs_low = probs.astype(jnp.bfloat16)
        prob_grad = jnp.einsum(
            "qhe,khe->hqk", grad_block, v_low, preferred_element_type=jnp.float32
        )
        row_dot = jnp.sum(probs * prob_grad, axis=-1, keepdims=True)
        score_grad = (probs * (prob_grad - row_dot)).astype(jnp.bfloat16)
        query_part = (
            jnp.einsum("hqk,khe->qhe", score_grad, k_rot, preferred_element_type=jnp.float32)
            * scale
        )
        key_acc = (
            key_acc
            + jnp.einsum("hqk,qhe->khe", score_grad, q_block, preferred_element_type=jnp.float32)
            * scale
        )
        value_acc = value_acc + jnp.einsum(
            "hqk,qhe->khe", probs_low, grad_block, preferred_element_type=jnp.float32
        )
        return ((key_acc, value_acc), query_part)

    zeros_heads = jnp.zeros((seq_rows, heads_here, HEAD), jnp.float32)
    (key_rot_grad, value_acc), query_parts = lax.scan(
        backward_block, (zeros_heads, zeros_heads), jnp.arange(blocks)
    )
    _, rotary_back = jax.vjp(lambda field: rotary(field, cosine, sine), zeros_heads)
    q_pre_grad = (
        rotary_back(query_parts.reshape(seq_rows, heads_here, HEAD))[0]
        .reshape(seq_rows, -1)
        .astype(jnp.bfloat16)
    )
    k_pre_grad = rotary_back(key_rot_grad)[0].reshape(seq_rows, -1).astype(jnp.bfloat16)
    v_pre_grad = value_acc.reshape(seq_rows, -1).astype(jnp.bfloat16)
    query_grad = inner_rows(gathered, q_pre_grad)
    key_grad = inner_rows(gathered, k_pre_grad)
    value_grad = inner_rows(gathered, v_pre_grad)
    head_bias_grad = jnp.stack(
        [
            jnp.sum(q_pre_grad, axis=0, dtype=jnp.float32),
            jnp.sum(k_pre_grad, axis=0, dtype=jnp.float32),
            jnp.sum(v_pre_grad, axis=0, dtype=jnp.float32),
        ]
    ).reshape(b_heads.shape)
    attn_input_grad = (
        times_trans(q_pre_grad, bw_query)
        + times_trans(k_pre_grad, bw_key)
        + times_trans(v_pre_grad, bw_value)
    )
    normed_grad = lax.psum_scatter(
        (attn_input_grad + mlp_input_grad).astype(jnp.bfloat16),
        "tensor",
        scatter_dimension=0,
        tiled=True,
    ).astype(jnp.float32)
    _, norm_back = jax.vjp(layer_norm, inputs, bw_gain, n_shift)
    input_part, gain_part, shift_part = norm_back(normed_grad)
    input_grad = grad_local + input_part
    gain_sum, shift_sum = lax.psum(
        (gain_part.astype(jnp.float32), shift_part.astype(jnp.float32)), "tensor"
    )
    (
        gain_grad,
        shift_grad,
        query_out,
        key_out,
        value_out,
        head_bias_out,
        proj_out,
        out_bias_out,
        up_out,
        up_bias_out,
        down_out,
    ) = (
        lax.psum_scatter(
            gain_sum.astype(jnp.bfloat16), "dp", scatter_dimension=0, tiled=True
        ).astype(jnp.float32),
        lax.psum_scatter(
            shift_sum.astype(jnp.bfloat16), "dp", scatter_dimension=0, tiled=True
        ).astype(jnp.float32),
        lax.psum_scatter(
            query_grad.astype(jnp.bfloat16), "dp", scatter_dimension=0, tiled=True
        ).astype(jnp.float32),
        lax.psum_scatter(
            key_grad.astype(jnp.bfloat16), "dp", scatter_dimension=0, tiled=True
        ).astype(jnp.float32),
        lax.psum_scatter(
            value_grad.astype(jnp.bfloat16), "dp", scatter_dimension=0, tiled=True
        ).astype(jnp.float32),
        lax.psum_scatter(
            head_bias_grad.astype(jnp.bfloat16), "dp", scatter_dimension=2, tiled=True
        ).astype(jnp.float32),
        lax.psum_scatter(
            proj_grad.astype(jnp.bfloat16), "dp", scatter_dimension=1, tiled=True
        ).astype(jnp.float32),
        lax.psum_scatter(
            out_bias_grad.astype(jnp.bfloat16), "dp", scatter_dimension=0, tiled=True
        ).astype(jnp.float32),
        lax.psum_scatter(
            up_grad.astype(jnp.bfloat16), "dp", scatter_dimension=0, tiled=True
        ).astype(jnp.float32),
        lax.psum_scatter(
            up_bias_grad.astype(jnp.bfloat16), "dp", scatter_dimension=1, tiled=True
        ).astype(jnp.float32),
        lax.psum_scatter(
            down_grad.astype(jnp.bfloat16), "dp", scatter_dimension=1, tiled=True
        ).astype(jnp.float32),
    )
    return (
        output,
        input_grad,
        gain_grad,
        shift_grad,
        query_out,
        key_out,
        value_out,
        head_bias_out,
        proj_out,
        out_bias_out,
        up_out,
        up_bias_out,
        down_out,
        out_bias_out,
    )


def solution(mesh):
    placed = (
        P(("dp", "tensor"), None),
        P(("dp", "tensor"), None),
        P("dp"),
        P("dp"),
        P("dp"),
        P("dp", "tensor"),
        P("dp", "tensor"),
        P("dp", "tensor"),
        P(None, "tensor", "dp"),
        P("tensor", "dp"),
        P("dp"),
        P("dp", "tensor"),
        P("tensor", "dp"),
        P("tensor", "dp"),
        P("dp"),
    )
    return jax.shard_map(
        on_device,
        mesh=mesh,
        in_specs=placed,
        out_specs=(
            P(("dp", "tensor"), None),
            P(("dp", "tensor"), None),
            P("dp"),
            P("dp"),
            P("dp", "tensor"),
            P("dp", "tensor"),
            P("dp", "tensor"),
            P(None, "tensor", "dp"),
            P("tensor", "dp"),
            P("dp"),
            P("dp", "tensor"),
            P("tensor", "dp"),
            P("tensor", "dp"),
            P("dp"),
        ),
        check_vma=False,
    )
```

profile of v0, /device:TPU:0, one launch (start us, length us, event | category | flops | bytes accessed | tf_op | source)
XLA Modules:
  0.0 881.5 jit_solution(469638515962775755)
XLA Ops:
  8.6 13.5 %all-gather = bf16[8,1,256]{2,1,0:T(2,128)(2,1)S(1)} all-gather(bf16[1,1,256]{2,1,0:T(2,128)(2,1)S(1)} %reshape.309), channel_id=1, replica_groups=mesh['dp'=8,'tensor'=4] {'dp'}, dimensions={0}, use_global_device_ids=true | all-gather | bytes 4608 | tf_op jit(solution)/shard_map/all_gather | solution.py:91
  22.8 9.1 %all-gather.1 = bf16[8,1,256]{2,1,0:T(2,128)(2,1)S(1)} all-gather(bf16[1,1,256]{2,1,0:T(2,128)(2,1)S(1)} %reshape.311), channel_id=1, replica_groups=mesh['dp'=8,'tensor'=4] {'dp'}, dimensions={0}, use_global_device_ids=true | all-gather | bytes 4608 | tf_op jit(solution)/shard_map/all_gather | solution.py:92
  44.9 14.0 %all_gather.53 = bf16[3,8,64]{1,0,2:T(4,128)(2,1)S(1)} all-gather(bf16[3,8,8]{1,0,2:T(4,128)(2,1)S(1)} %copy.54), channel_id=1, replica_groups=mesh['dp'=8,'tensor'=4] {'dp'}, dimensions={2}, use_global_device_ids=true | all-gather | bytes 3456 | tf_op jit(solution)/shard_map/all_gather | solution.py:96
  59.8 36.1 %all-gather.13.cloned.1.call-done = bf16[1024,2048]{1,0:T(8,128)(2,1)} async-done(((bf16[256,2048]{1,0:T(8,128)(2,1)}), bf16[1024,2048]{1,0:T(8,128)(2,1)}) %all-gather.13.cloned.1.call-update) | async-done | bytes 4194320 | tf_op jit(solution)/shard_map/all_gather | solution.py:107
  96.0 5.2 convolution_add_fusion.1
  101.3 25.5 %all-gather.17.cloned.1.call-done = bf16[2048,512]{1,0:T(8,128)(2,1)} async-done(((bf16[256,512]{1,0:T(8,128)(2,1)}), bf16[2048,512]{1,0:T(8,128)(2,1)}) %all-gather.17.cloned.1.call-update) | async-done | bytes 2097168 | tf_op jit(solution)/shard_map/all_gather | solution.py:94
  133.6 23.2 %all-gather.19.cloned.1.call-done = bf16[2048,512]{1,0:T(8,128)(2,1)} async-done(((bf16[256,512]{1,0:T(8,128)(2,1)}), bf16[2048,512]{1,0:T(8,128)(2,1)}) %all-gather.19.cloned.1.call-update) | async-done | bytes 2097168 | tf_op jit(solution)/shard_map/all_gather | solution.py:95
  156.8 6.2 add_convert_fusion.4
  163.1 35.0 %while.28 = (s32[]{:T(128)}, bf16[2,512,8,64]{1,3,2,0:T(8,128)(2,1)S(1)}, f32[2,8,512,1]{2,1,3,0:T(8,128)}, s32[2]{0:T(128)S(1)}, bf16[1024,8,64]{0,2,1:T(8,128)...) while((s32[]{:T(128)}, ...), condition=%wide.region_5.6_spmd.clone, body=%wide.region_2.5_spmd.clone.sunk | while | flops 1125381632 | bytes 55712444 | solution.py:138
  174.9 5.9 fusion.136
  192.2 5.9 fusion.136
  198.1 43.5 %all-gather.27.cloned.1.call-done = bf16[1024,2048]{1,0:T(8,128)(2,1)} async-done(((bf16[256,2048]{1,0:T(8,128)(2,1)}), bf16[1024,2048]{1,0:T(8,128)(2,1)}) %all-gather.27.cloned.1.call-update) | async-done | bytes 4194320 | tf_op jit(solution)/shard_map/all_gather | solution.py:151
  241.6 6.2 convolution_convert_fusion.6
  247.8 170.4 %while.29 = (s32[]{:T(128)}, f32[1024,8,64]{0,2,1:T(8,128)}, f32[1024,8,64]{0,2,1:T(8,128)}, f32[2,512,8,64]{1,0,3,2:T(2,128)}, s32[2]{0:T(128)S(1)}, /*index=5*...) while((s32[]{:T(128)}, f32[1024,8,64]{0,2,1:T(8,128)}, ...), condition=%wide.region_9.10_spmd.clone, body=%wide.region_7.9_spmd.clone.sunk | while | flops 2726032896 | bytes 212949424 | solution.py:202
  249.2 9.6 %fusion.146 = f32[8,512,1024]{2,1,0:T(8,128)} fusion(bf16[1024,8,64]{0,2,1:T(8,128)(2,1)} %get-tuple-element.543, bf16[1024,8,64]{0,2,1:T(8,128)(2,1)} %get-tuple-element.542, s32[]{:T(128)S(6)} %select_n.49), kind=kOutput, calls=%fused_computation.35.clone.1 | convolution fusion | flops 536870912 | bytes 18350084 | tf_op jit(solution)/shard_map/while/body/eval_jaxpr/qhe,khe->hqk/dot_general | solution.py:182
  264.0 16.4 %multiply_reduce_fusion.2 = (f32[8,512]{1,0:T(8,128)}, f32[8,512,1024]{2,1,0:T(8,128)}) fusion(f32[8,512,1024]{2,1,0:T(8,128)} %fusion.146, f32[8,512]{1,0:T(8,128)} %dynamic-slice_bitcast_fusion.2, bf16[1024,8,64]{0,2,1:T(8,128)(2,1)S(1)} %get-tuple-element.540, bf16[1024,8,64]{0,2,1:T(8,128)(2,1)} %get-tuple-element.539, s32[]{:T(128)S(6)} %select_n.49, ...), kind=kOutput, calls=%fused_computation.24.clone.1 | convolution fusion | flops 557838336 | bytes 35684356 | tf_op jit(solution)/shard_map/while/body/eval_jaxpr/qhe,khe->hqk/dot_general | solution.py:121
  280.4 9.5 %multiply_convert_fusion.5 = bf16[8,512,1024]{2,1,0:T(8,128)(2,1)} fusion(f32[8,512,1024]{2,1,0:T(8,128)} %get-tuple-element.464, f32[8,512,1024]{2,1,0:T(8,128)S(1)} %bitcast.120, f32[8,512]{1,0:T(8,128)} %get-tuple-element.465), kind=kLoop, calls=%fused_computation.23.clone.1 | loop fusion | flops 12582912 | bytes 41959424 | tf_op jit(solution)/shard_map/while/body/eval_jaxpr/convert_element_type | solution.py:186
  289.9 6.2 fusion.148
  298.2 19.7 %dynamic_update_slice.22 = f32[2,512,8,64]{1,0,3,2:T(2,128)} dynamic-update-slice(f32[2,512,8,64]{1,0,3,2:T(2,128)} %get-tuple-element.521, f32[1,512,8,64]{1,0,3,2:T(1,128)} %copy.84, s32[]{:T(128)} %get-tuple-element.518, s32[]{:T(128)} %constant.52.clone.1..sunk.1, s32[]{:T(128)} %constant.52.clone.1..sunk.1, s32[]{:T(128)} %constant.52.clone.1..sunk.1) | dynamic-update-slice | bytes 2097156 | tf_op jit(solution)/shard_map/while/body/jit(dynamic_update_index_in_dim)/dynamic_update_slice | solution.py:202
  317.9 5.4 bitcast_add_fusion.4
  323.3 9.6 %bitcast_add_fusion.5 = f32[1024,8,64]{0,2,1:T(8,128)} fusion(f32[1024,8,64]{0,2,1:T(8,128)} %get-tuple-element.520, f32[8,512,1024]{2,1,0:T(8,128)} %get-tuple-element.464, pred[]{:T(512)S(6)} %compare.9, bf16[1024,8,64]{0,2,1:T(8,128)(2,1)} %get-tuple-element.542, s32[]{:T(128)S(6)} %select_n.49), kind=kOutput, calls=%fused_computation.28.clone.1 | convolution fusion | flops 542113792 | bytes 21495812 | tf_op jit(solution)/shard_map/while/body/eval_jaxpr/hqk,qhe->khe/dot_general | solution.py:196
  334.2 9.7 %fusion.146 = f32[8,512,1024]{2,1,0:T(8,128)} fusion(bf16[1024,8,64]{0,2,1:T(8,128)(2,1)} %get-tuple-element.543, bf16[1024,8,64]{0,2,1:T(8,128)(2,1)} %get-tuple-element.542, s32[]{:T(128)S(6)} %select_n.49), kind=kOutput, calls=%fused_computation.35.clone.1 | convolution fusion | flops 536870912 | bytes 18350084 | tf_op jit(solution)/shard_map/while/body/eval_jaxpr/qhe,khe->hqk/dot_general | solution.py:182
  349.0 16.3 %multiply_reduce_fusion.2 = (f32[8,512]{1,0:T(8,128)}, f32[8,512,1024]{2,1,0:T(8,128)}) fusion(f32[8,512,1024]{2,1,0:T(8,128)} %fusion.146, f32[8,512]{1,0:T(8,128)} %dynamic-slice_bitcast_fusion.2, bf16[1024,8,64]{0,2,1:T(8,128)(2,1)S(1)} %get-tuple-element.540, bf16[1024,8,64]{0,2,1:T(8,128)(2,1)} %get-tuple-element.539, s32[]{:T(128)S(6)} %select_n.49, ...), kind=kOutput, calls=%fused_computation.24.clone.1 | convolution fusion | flops 557838336 | bytes 35684356 | tf_op jit(solution)/shard_map/while/body/eval_jaxpr/qhe,khe->hqk/dot_general | solution.py:121
  365.4 9.3 %multiply_convert_fusion.5 = bf16[8,512,1024]{2,1,0:T(8,128)(2,1)} fusion(f32[8,512,1024]{2,1,0:T(8,128)} %get-tuple-element.464, f32[8,512,1024]{2,1,0:T(8,128)S(1)} %bitcast.120, f32[8,512]{1,0:T(8,128)} %get-tuple-element.465), kind=kLoop, calls=%fused_computation.23.clone.1 | loop fusion | flops 12582912 | bytes 41959424 | tf_op jit(solution)/shard_map/while/body/eval_jaxpr/convert_element_type | solution.py:186
  374.7 6.3 fusion.148
  383.1 19.7 %dynamic_update_slice.22 = f32[2,512,8,64]{1,0,3,2:T(2,128)} dynamic-update-slice(f32[2,512,8,64]{1,0,3,2:T(2,128)} %get-tuple-element.521, f32[1,512,8,64]{1,0,3,2:T(1,128)} %copy.84, s32[]{:T(128)} %get-tuple-element.518, s32[]{:T(128)} %constant.52.clone.1..sunk.1, s32[]{:T(128)} %constant.52.clone.1..sunk.1, s32[]{:T(128)} %constant.52.clone.1..sunk.1) | dynamic-update-slice | bytes 2097156 | tf_op jit(solution)/shard_map/while/body/jit(dynamic_update_index_in_dim)/dynamic_update_slice | solution.py:202
  402.7 5.3 bitcast_add_fusion.4
  408.1 10.2 %bitcast_add_fusion.5 = f32[1024,8,64]{0,2,1:T(8,128)} fusion(f32[1024,8,64]{0,2,1:T(8,128)} %get-tuple-element.520, f32[8,512,1024]{2,1,0:T(8,128)} %get-tuple-element.464, pred[]{:T(512)S(6)} %compare.9, bf16[1024,8,64]{0,2,1:T(8,128)(2,1)} %get-tuple-element.542, s32[]{:T(128)S(6)} %select_n.49), kind=kOutput, calls=%fused_computation.28.clone.1 | convolution fusion | flops 542113792 | bytes 21495812 | tf_op jit(solution)/shard_map/while/body/eval_jaxpr/hqk,qhe->khe/dot_general | solution.py:196
  431.4 5.9 convolution_convert_fusion.4
  439.8 6.0 convolution_convert_fusion.3
  445.9 13.2 %all_gather.58 = bf16[32,64]{0,1:T(8,128)(2,1)S(1)} all-gather(bf16[32,8]{0,1:T(8,128)(2,1)S(1)} %copy-done.35), channel_id=1, replica_groups=mesh['dp'=8,'tensor'=4] {'dp'}, dimensions={1}, use_global_device_ids=true | all-gather | bytes 4608 | tf_op jit(solution)/shard_map/all_gather | solution.py:100
  465.4 7.8 fusion.70
  473.1 5.6 fusion.69
  478.8 14.8 %fusion.68 = f32[1024,2048]{1,0:T(8,128)} fusion(bf16[1024,2048]{1,0:T(8,128)(2,1)} %all-gather.13.cloned.1.call-done, bf16[2048,2048]{1,0:T(8,128)(2,1)} %all-gather.23.cloned.1.call-done), kind=kOutput, calls=%fused_computation.129 | convolution fusion | flops 8589934592 | bytes 20971520 | tf_op jit(solution)/shard_map/dot_general | solution.py:52
  493.6 18.7 %fusion.62 = (bf16[2048]{0:T(1024)(128)(2,1)S(1)}, bf16[1024,2048]{1,0:T(8,128)(2,1)S(1)}) fusion(f32[1024,2048]{1,0:T(8,128)} %fusion.68, f32[2048]{0:T(1024)S(1)} %reshape.308, bf16[1024,2048]{1,0:T(8,128)(2,1)} %all-gather.27.cloned.1.call-done, bf16[2048,2048]{1,0:T(8,128)(2,1)} %all-gather.25.cloned.1.call-done), kind=kOutput, calls=%fused_computation.124 | convolution fusion | flops 8636069888 | bytes 25178112 | tf_op jit(solution)/shard_map/dot_general | solution.py:46
  514.2 13.9 %fusion.71 = f32[1024,2048]{1,0:T(8,128)} fusion(bf16[1024,2048]{1,0:T(8,128)(2,1)S(1)} %get-tuple-element.310, bf16[2048,2048]{1,0:T(8,128)(2,1)} %all-gather.23.cloned.1.call-done), kind=kOutput, calls=%fused_computation.132 | convolution fusion | flops 8589934592 | bytes 20971520 | tf_op jit(solution)/shard_map/dot_general | solution.py:46
  528.2 11.6 %add_convert_fusion = bf16[1024,2048]{1,0:T(8,128)(2,1)} fusion(f32[1024,2048]{1,0:T(8,128)} %fusion.71, f32[1024,2048]{1,0:T(8,128)S(1)} %copy-done.6, f32[1024,2048]{1,0:T(8,128)} %fusion.70, bf16[1024,512]{0,1:T(8,128)(2,1)S(1)} %bitcast.122, bf16[2048,512]{1,0:T(8,128)(2,1)} %all-gather.19.cloned.1.call-done), kind=kOutput, calls=%fused_computation.55 | convolution fusion | flops 2155872256 | bytes 32505856 | tf_op jit(solution)/shard_map/dot_general | solution.py:46
  539.8 16.2 %fusion.61 = f32[1024,2048]{1,0:T(8,128)S(1)} fusion(bf16[2048,2048]{1,0:T(8,128)(2,1)} %all-gather.25.cloned.1.call-done, f32[1024,2048]{1,0:T(8,128)} %fusion.68, f32[2048]{0:T(1024)S(1)} %reshape.308), kind=kOutput, calls=%fused_computation.123 | convolution fusion | flops 8610906112 | bytes 25174016 | tf_op jit(solution)/shard_map/dot_general | solution.py:52
  560.5 14.1 %convolution_convert_fusion.1 = bf16[2048,2048]{1,0:T(8,128)(2,1)} fusion(bf16[1024,2048]{1,0:T(8,128)(2,1)} %all-gather.13.cloned.1.call-done, bf16[1024,2048]{1,0:T(8,128)(2,1)} %copy-done.42), kind=kOutput, calls=%fused_computation.59 | convolution fusion | flops 8594128896 | bytes 16777216 | tf_op jit(solution)/shard_map/dot_general | solution.py:40
  574.6 16.1 %convolution_convert_fusion = bf16[2048,2048]{1,0:T(8,128)(2,1)} fusion(bf16[1024,2048]{1,0:T(8,128)(2,1)} %all-gather.27.cloned.1.call-done, f32[1024,2048]{1,0:T(8,128)} %fusion.68, f32[2048]{0:T(1024)S(1)} %reshape.308), kind=kOutput, calls=%fused_computation.58 | convolution fusion | flops 8615100416 | bytes 20979712 | tf_op jit(solution)/shard_map/dot_general | solution.py:40
  593.3 10.4 %all-gather.2 = bf16[8,1,256]{2,1,0:T(2,128)(2,1)S(1)} all-gather(bf16[1,1,256]{2,1,0:T(2,128)(2,1)S(1)} %reshape.313), channel_id=1, replica_groups=mesh['dp'=8,'tensor'=4] {'dp'}, dimensions={0}, use_global_device_ids=true | all-gather | bytes 4608 | tf_op jit(solution)/shard_map/all_gather | solution.py:98
  603.8 8.8 all-gather.3
  623.1 10.6 %reduce-scatter.13.cloned.1.call-done = bf16[256,2048]{1,0:T(8,128)(2,1)} async-done(((bf16[1024,2048]{1,0:T(8,128)(2,1)}), bf16[256,2048]{1,0:T(8,128)(2,1)}) %reduce-scatter.13.cloned.1.call-update) | async-done | bytes 1048592 | tf_op jit(solution)/shard_map/reduce_scatter | solution.py:228
  639.3 15.9 %all-reduce.11 = (bf16[2048]{0:T(1024)(128)(2,1)S(1)}, bf16[2048]{0:T(1024)(128)(2,1)S(1)}) all-reduce(bf16[2048]{0:T(1024)(128)(2,1)S(1)} %get-tuple-element.262, bf16[2048]{0:T(1024)(128)(2,1)S(1)} %reduce_sum.155), channel_id=1, replica_groups=mesh['dp'=8,'tensor'=4] {'tensor'}, use_global_device_ids=true, to_apply=%region_14.15 | all-reduce | flops 4096 | bytes 16384 | tf_op jit(solution)/shard_map/psum | solution.py:237
  655.2 26.0 %all-reduce.12 = (bf16[2048]{0:T(1024)(128)(2,1)S(1)}, bf16[2048]{0:T(1024)(128)(2,1)S(1)}, bf16[3,8,64]{2,1,0:T(8,128)(2,1)S(1)}, bf16[2048]{0:T(1024)(128)(2,1)S(1)}, bf16[32,64]{1,0:T(8,128)(2,1)S(1)}) all-reduce(bf16[2048]{0:T(1024)(128)(2,1)S(1)} %get-tuple-element.302, ...), channel_id=4, replica_groups=mesh['dp'=8,'tensor'=4] {'dp'}, use_global_device_ids=true, to_apply=%region_15.16.clone | all-reduce | flops 9728 | bytes 38912
  683.9 5.6 reduce-scatter.11.cloned.1.call-done
  693.7 87.5 %reduce-scatter.23.cloned.1.call-done = bf16[256,2048]{1,0:T(8,128)(2,1)} async-done(((bf16[2048,2048]{1,0:T(8,128)(2,1)}), bf16[256,2048]{1,0:T(8,128)(2,1)}) %reduce-scatter.23.cloned.1.call-update) | async-done | bytes 1048592 | tf_op jit(solution)/shard_map/reduce_scatter | solution.py:277
  784.1 87.4 %reduce-scatter.25.cloned.1.call-done = bf16[2048,256]{1,0:T(8,128)(2,1)} async-done(((bf16[2048,2048]{1,0:T(8,128)(2,1)}), bf16[2048,256]{1,0:T(8,128)(2,1)}) %reduce-scatter.25.cloned.1.call-update) | async-done | bytes 1048592 | tf_op jit(solution)/shard_map/reduce_scatter | solution.py:283
  (249 shorter events, 113.6 us)
Async XLA Ops:
  7.2 34.8 %copy-start.8 = (bf16[256,2048]{1,0:T(8,128)(2,1)S(1)}, bf16[256,2048]{1,0:T(8,128)(2,1)}, u32[]{:S(2)}) copy-start(bf16[256,2048]{1,0:T(8,128)(2,1)} %param.20) | copy-start | bytes 3145732
  7.2 52.7 %all-gather.15.cloned.1.call-start = ((), (), s32[]{:S(2)}) async-start(), calls=%async_computation.9 | async-start | bytes 2359296 | tf_op jit(solution)/shard_map/all_gather | solution.py:93
  7.9 88.1 %all-gather.13.cloned.1.call-start = ((), (), s32[]{:S(2)}) async-start(), calls=%async_computation.8 | async-start | bytes 5242880 | tf_op jit(solution)/shard_map/all_gather | solution.py:107
  22.1 13.4 %copy-start.20 = (f32[8,1,256]{2,1,0:T(1,128)}, f32[8,1,256]{2,1,0:T(1,128)S(1)}, u32[]{:S(2)}) copy-start(f32[8,1,256]{2,1,0:T(1,128)S(1)} %convert_element_type.290) | copy-start | bytes 24580
  38.8 88.0 %all-gather.17.cloned.1.call-start = ((), (), s32[]{:S(2)}) async-start(), calls=%async_computation.10 | async-start | bytes 2359296 | tf_op jit(solution)/shard_map/all_gather | solution.py:94
  39.5 117.3 %all-gather.19.cloned.1.call-start = ((), (), s32[]{:S(2)}) async-start(), calls=%async_computation.11 | async-start | bytes 2359296 | tf_op jit(solution)/shard_map/all_gather | solution.py:95
  40.1 158.0 %all-gather.21.cloned.1.call-start = ((), (), s32[]{:S(2)}) async-start(), calls=%async_computation.12 | async-start | bytes 2359296 | tf_op jit(solution)/shard_map/all_gather | solution.py:97
  40.7 200.9 %all-gather.27.cloned.1.call-start = ((), (), s32[]{:S(2)}) async-start(), calls=%async_computation.16 | async-start | bytes 5242880 | tf_op jit(solution)/shard_map/all_gather | solution.py:151
  43.2 435.5 %all-gather.23.cloned.1.call-start = ((), (), s32[]{:S(2)}) async-start(), calls=%async_computation.13 | async-start | bytes 9437184 | tf_op jit(solution)/shard_map/all_gather | solution.py:99
  44.0 449.6 %all-gather.25.cloned.1.call-start = ((), (), s32[]{:S(2)}) async-start(), calls=%async_computation.14 | async-start | bytes 9437184 | tf_op jit(solution)/shard_map/all_gather | solution.py:101
  44.7 571.0 %reduce-scatter.15.cloned.1.call-start = ((), (), s32[]{:S(2)}) async-start(), calls=%async_computation.18 | async-start | bytes 2359296 | tf_op jit(solution)/shard_map/reduce_scatter | solution.py:259
  59.7 72.4 %copy-start.16 = (f32[1024,16]{0,1:T(8,128)}, f32[1024,16]{0,1:T(8,128)S(1)}, u32[]{:S(2)}) copy-start(f32[1024,16]{0,1:T(8,128)S(1)} %get-tuple-element.338) | copy-start | bytes 196612
  59.7 72.4 %copy-start.18 = (f32[1024,16]{0,1:T(8,128)}, f32[1024,16]{0,1:T(8,128)S(1)}, u32[]{:S(2)}) copy-start(f32[1024,16]{0,1:T(8,128)S(1)} %get-tuple-element.339) | copy-start | bytes 196612
  133.6 29.5 %copy-start.10 = (bf16[2,512,8,64]{1,3,2,0:T(8,128)(2,1)S(1)}, bf16[2,512,8,64]{1,3,2,0:T(8,128)(2,1)}, u32[]{:S(2)}) copy-start(bf16[2,512,8,64]{1,3,2,0:T(8,128)(2,1)} %custom-call.2) | copy-start | bytes 3145732
  198.0 49.8 %copy-start.11 = (bf16[2,512,8,64]{1,3,2,0:T(8,128)(2,1)}, bf16[2,512,8,64]{1,3,2,0:T(8,128)(2,1)S(1)}, u32[]{:S(2)}) copy-start(bf16[2,512,8,64]{1,3,2,0:T(8,128)(2,1)S(1)} %get-tuple-element.126) | copy-start | bytes 3145732
  264.0 16.4 %slice-start = ((s8[16777216]{0:T(1024)(128)(4,1)}), s8[4194304]{0:T(1024)(128)(4,1)S(1)}, s32[]{:S(2)}) async-start(s8[16777216]{0:T(1024)(128)(4,1)} %bitcast.119), calls=%async_computation.24 | async-start | bytes 8388608 | tf_op jit(solution)/shard_map/while
  264.0 16.4 %slice-start.1 = ((s8[16777216]{0:T(1024)(128)(4,1)}), s8[4194304]{0:T(1024)(128)(4,1)S(1)}, s32[]{:S(2)}) async-start(s8[16777216]{0:T(1024)(128)(4,1)} %bitcast.119), calls=%async_computation.25 | async-start | bytes 8388608 | tf_op jit(solution)/shard_map/while
  264.0 16.4 %slice-start.2 = ((s8[16777216]{0:T(1024)(128)(4,1)}), s8[4194304]{0:T(1024)(128)(4,1)S(1)}, s32[]{:S(2)}) async-start(s8[16777216]{0:T(1024)(128)(4,1)} %bitcast.119), calls=%async_computation.26 | async-start | bytes 8388608 | tf_op jit(solution)/shard_map/while
  264.0 16.4 %slice-start.3 = ((s8[16777216]{0:T(1024)(128)(4,1)}), s8[4194304]{0:T(1024)(128)(4,1)S(1)}, s32[]{:S(2)}) async-start(s8[16777216]{0:T(1024)(128)(4,1)} %bitcast.119), calls=%async_computation.27 | async-start | bytes 8388608 | tf_op jit(solution)/shard_map/while
  296.1 21.7 %copy-start = (f32[1024,8,64]{0,2,1:T(8,128)S(1)}, f32[1024,8,64]{0,2,1:T(8,128)}, u32[]{:S(2)}) copy-start(f32[1024,8,64]{0,2,1:T(8,128)} %get-tuple-element.519) | copy-start | bytes 6291460 | tf_op jit(solution)/shard_map/while
  349.0 16.4 %slice-start = ((s8[16777216]{0:T(1024)(128)(4,1)}), s8[4194304]{0:T(1024)(128)(4,1)S(1)}, s32[]{:S(2)}) async-start(s8[16777216]{0:T(1024)(128)(4,1)} %bitcast.119), calls=%async_computation.24 | async-start | bytes 8388608 | tf_op jit(solution)/shard_map/while
  349.0 16.4 %slice-start.1 = ((s8[16777216]{0:T(1024)(128)(4,1)}), s8[4194304]{0:T(1024)(128)(4,1)S(1)}, s32[]{:S(2)}) async-start(s8[16777216]{0:T(1024)(128)(4,1)} %bitcast.119), calls=%async_computation.25 | async-start | bytes 8388608 | tf_op jit(solution)/shard_map/while
  349.0 16.4 %slice-start.2 = ((s8[16777216]{0:T(1024)(128)(4,1)}), s8[4194304]{0:T(1024)(128)(4,1)S(1)}, s32[]{:S(2)}) async-start(s8[16777216]{0:T(1024)(128)(4,1)} %bitcast.119), calls=%async_computation.26 | async-start | bytes 8388608 | tf_op jit(solution)/shard_map/while
  349.0 16.4 %slice-start.3 = ((s8[16777216]{0:T(1024)(128)(4,1)}), s8[4194304]{0:T(1024)(128)(4,1)S(1)}, s32[]{:S(2)}) async-start(s8[16777216]{0:T(1024)(128)(4,1)} %bitcast.119), calls=%async_computation.27 | async-start | bytes 8388608 | tf_op jit(solution)/shard_map/while
  381.0 21.7 %copy-start = (f32[1024,8,64]{0,2,1:T(8,128)S(1)}, f32[1024,8,64]{0,2,1:T(8,128)}, u32[]{:S(2)}) copy-start(f32[1024,8,64]{0,2,1:T(8,128)} %get-tuple-element.519) | copy-start | bytes 6291460 | tf_op jit(solution)/shard_map/while
  431.4 186.2 %reduce-scatter.17.cloned.1.call-start = ((), (), s32[]{:S(2)}) async-start(), calls=%async_computation.19 | async-start | bytes 2359296 | tf_op jit(solution)/shard_map/reduce_scatter | solution.py:262
  437.4 182.1 %reduce-scatter.19.cloned.1.call-start = ((), (), s32[]{:S(2)}) async-start(), calls=%async_computation.20 | async-start | bytes 2359296 | tf_op jit(solution)/shard_map/reduce_scatter | solution.py:265
  439.8 19.5 %copy-start.12 = (bf16[2,512,8,64]{1,3,2,0:T(8,128)(2,1)S(1)}, bf16[2,512,8,64]{1,3,2,0:T(8,128)(2,1)}, u32[]{:S(2)}) copy-start(bf16[2,512,8,64]{1,3,2,0:T(8,128)(2,1)} %copy-done.11) | copy-start | bytes 3145732
  445.8 175.4 %reduce-scatter.21.cloned.1.call-start = ((), (), s32[]{:S(2)}) async-start(), calls=%async_computation.21 | async-start | bytes 2359296 | tf_op jit(solution)/shard_map/reduce_scatter | solution.py:271
  465.3 168.4 %reduce-scatter.13.cloned.1.call-start = ((), (), s32[]{:S(2)}) async-start(), calls=%async_computation.17 | async-start | bytes 5242880 | tf_op jit(solution)/shard_map/reduce_scatter | solution.py:228
  514.2 13.9 %copy-start.6 = (f32[1024,2048]{1,0:T(8,128)S(1)}, f32[1024,2048]{1,0:T(8,128)}, u32[]{:S(2)}) copy-start(f32[1024,2048]{1,0:T(8,128)} %fusion.69) | copy-start | bytes 25165828
  539.8 149.8 %reduce-scatter.11.cloned.1.call-start = ((), (), s32[]{:S(2)}) async-start(), calls=%async_computation.15 | async-start | bytes 5242880 | tf_op jit(solution)/shard_map/reduce_scatter | solution.py:144
  539.8 16.2 %copy-start.38 = (bf16[512,2048]{1,0:T(8,128)(2,1)S(1)}, bf16[512,2048]{1,0:T(8,128)(2,1)}, u32[]{:S(2)}) copy-start(bf16[512,2048]{1,0:T(8,128)(2,1)} %all-gather.21.cloned.1.call-done) | copy-start | bytes 6291460
  560.4 220.9 %reduce-scatter.23.cloned.1.call-start = ((), (), s32[]{:S(2)}) async-start(), calls=%async_computation.22 | async-start | bytes 9437184 | tf_op jit(solution)/shard_map/reduce_scatter | solution.py:277
  574.6 296.9 %reduce-scatter.25.cloned.1.call-start = ((), (), s32[]{:S(2)}) async-start(), calls=%async_computation.23 | async-start | bytes 9437184 | tf_op jit(solution)/shard_map/reduce_scatter | solution.py:283
  590.8 13.0 %copy-start.40 = (bf16[256]{0:T(256)(128)(2,1)S(1)}, bf16[256]{0:T(256)(128)(2,1)}, u32[]{:S(2)}) copy-start(bf16[256]{0:T(256)(128)(2,1)} %param.33) | copy-start | bytes 1540
  590.8 24.8 %copy-start.30 = (bf16[8,64]{1,0:T(8,128)(2,1)S(1)}, bf16[8,64]{1,0:T(8,128)(2,1)}, u32[]{:S(2)}) copy-start(bf16[8,64]{1,0:T(8,128)(2,1)} %get-tuple-element.311) | copy-start | bytes 3076
  590.8 24.8 %copy-start.31 = (bf16[8,64]{1,0:T(8,128)(2,1)S(1)}, bf16[8,64]{1,0:T(8,128)(2,1)}, u32[]{:S(2)}) copy-start(bf16[8,64]{1,0:T(8,128)(2,1)} %get-tuple-element.340) | copy-start | bytes 3076
  590.8 24.8 %copy-start.32 = (bf16[8,64]{1,0:T(8,128)(2,1)S(1)}, bf16[8,64]{1,0:T(8,128)(2,1)}, u32[]{:S(2)}) copy-start(bf16[8,64]{1,0:T(8,128)(2,1)} %get-tuple-element.315) | copy-start | bytes 3076
  612.6 22.6 %copy-start.3 = (bf16[256,2048]{1,0:T(8,128)(2,1)S(1)}, bf16[256,2048]{1,0:T(8,128)(2,1)}, u32[]{:S(2)}) copy-start(bf16[256,2048]{1,0:T(8,128)(2,1)} %param.19) | copy-start | bytes 3145732
  612.6 22.6 %copy-start.21 = (f32[8,1,256]{2,1,0:T(1,128)S(1)}, f32[8,1,256]{2,1,0:T(1,128)}, u32[]{:S(2)}) copy-start(f32[8,1,256]{2,1,0:T(1,128)} %copy-done.20) | copy-start | bytes 24580
  612.6 22.6 %copy-start.23 = (f32[256]{0:T(256)S(1)}, f32[256]{0:T(256)}, u32[]{:S(2)}) copy-start(f32[256]{0:T(256)} %copy-done.22) | copy-start | bytes 3076
  615.6 21.4 %copy-start.29 = (f32[256]{0:T(256)S(1)}, f32[256]{0:T(256)}, u32[]{:S(2)}) copy-start(f32[256]{0:T(256)} %copy-done.28) | copy-start | bytes 3076
  615.6 21.4 %copy-start.25 = (f32[256]{0:T(256)S(1)}, f32[256]{0:T(256)}, u32[]{:S(2)}) copy-start(f32[256]{0:T(256)} %copy-done.24) | copy-start | bytes 3076
  615.7 73.9 %copy-start.9 = (bf16[256,2048]{1,0:T(8,128)(2,1)S(1)}, bf16[256,2048]{1,0:T(8,128)(2,1)}, u32[]{:S(2)}) copy-start(bf16[256,2048]{1,0:T(8,128)(2,1)} %param.20) | copy-start | bytes 3145732
  615.7 73.9 %copy-start.27 = (f32[256]{0:T(256)S(1)}, f32[256]{0:T(256)}, u32[]{:S(2)}) copy-start(f32[256]{0:T(256)} %copy-done.26) | copy-start | bytes 3076
  633.7 55.9 %copy-start.4 = (bf16[256,2048]{1,0:T(8,128)(2,1)S(1)}, bf16[256,2048]{1,0:T(8,128)(2,1)}, u32[]{:S(2)}) copy-start(bf16[256,2048]{1,0:T(8,128)(2,1)} %reduce-scatter.13.cloned.1.call-done) | copy-start | bytes 3145732
  682.0 192.2 %copy-start.34 = (f32[256]{0:T(256)}, f32[256]{0:T(256)S(1)}, u32[]{:S(2)}) copy-start(f32[256]{0:T(256)S(1)} %dynamic-slice_convert_fusion.2) | copy-start | bytes 3076
  (22 other events, 88.2 us)
Sparse Core Ops, SparseCore 0:
  9.6 31.9 all-gather.14
  44.0 51.9 all-gather.12
  97.6 29.1 all-gather.16
  128.2 28.5 all-gather.18
  158.2 29.9 all-gather.20
  190.0 51.5 all-gather.26
  243.2 82.0 all-gather.22
  326.8 80.9 all-gather.24
  431.5 36.3 reduce-scatter.14
  470.6 35.0 reduce-scatter.16
  508.5 34.3 reduce-scatter.18
  545.0 34.8 reduce-scatter.20
  582.9 50.7 reduce-scatter.12
  636.5 53.0 reduce-scatter.10
  691.7 89.5 reduce-scatter.22
  783.4 88.0 reduce-scatter.24
where the time goes:
time: 893 us; the launch traced here: 881 us
  waiting for transfers between devices  324 us (36%)
  matrix products  281 us (31%)
  blocking collectives  111 us (12%)
  other arithmetic  74.4 us (8%)
  local copies, waits for them, and re-layouts  67.2 us (8%)
  between operations  16.7 us (2%)
    reduce_scatter x1, waiting for transfers between devices, on_device(): lax.psum_scatter(up_grad.astype(jnp.bfloat16), 'dp', scatter_dimension=0,...  87.5 us
    reduce_scatter x1, waiting for transfers between devices, on_device(): lax.psum_scatter(down_grad.astype(jnp.bfloat16), 'dp', scatter_dimension=...  87.4 us
    dot_general x6, matrix products, times_trans(): lax.dot_general(left, right, (((1,), (1,)), ((), ())), preferred_element_...  63.8 us
    dot_general x6, matrix products, product(): return jnp.dot(left, right, preferred_element_type=jnp.float32)  52.1 us
    dot_general x6, matrix products, inner_rows(): lax.dot_general(left, right, (((0,), (0,)), ((), ())), preferred_element_...  49.7 us
    all_gather x1, waiting for transfers between devices, on_device(): lax.all_gather(grad_local.astype(jnp.bfloat16), 'tensor', axis=0, tiled=T...  43.5 us
    dynamic_update_slice x4, local copies, waits for them, and re-layouts, on_device(): lax.scan(backward_block, (zeros_heads, zeros_heads), jnp.arange(blocks))  43.5 us
    dot_general x4, matrix products, block_scores(): jnp.einsum('qhe,khe->hqk', q_block, k_rot, preferred_element_type=jnp.flo...  41 us
  transfers between devices with their start and end apart: 16, of which 8 were waited for; matrix products, arithmetic and copies ran while one was open for 47% of the time, Pallas kernels for 0%

commit v1 on v0

v1 whole, which is shorter than its diff:
```python
import functools

import jax
import jax.numpy as jnp
from jax import lax
from jax.experimental import pallas as pl
from jax.experimental.pallas import tpu as pltpu
from jax.sharding import PartitionSpec as P

HEAD = 64
ROT = 32
LANES = 128
QBLOCK = 256
MLP_PARTS = (1, 1)
ATTN_RS = "line"
MLP_RS = ("sc", "line")

norm_eps = 1e-05
masked_score = -1000000000.0
F32 = jnp.float32
BF16 = jnp.bfloat16


def layer_norm(rows, gain, shift):
    center = rows - jnp.mean(rows, axis=-1, keepdims=True)
    spread = jnp.mean(center * center, axis=-1, keepdims=True)
    return center * lax.rsqrt(spread + norm_eps) * gain + shift


def product(left, right):
    return jnp.dot(left, right, preferred_element_type=F32)


def times_trans(left, right):
    return lax.dot_general(left, right, (((1,), (1,)), ((), ())), preferred_element_type=F32)


def inner_rows(left, right):
    return lax.dot_general(left, right, (((0,), (0,)), ((), ())), preferred_element_type=F32)


def rotary_lanes(count):
    half = ROT // 2
    lane = jnp.arange(LANES) % HEAD
    freq = 1.0 / 10000.0 ** ((lane % half).astype(F32) * (2.0 / ROT))
    angle = jnp.arange(count, dtype=F32)[:, None] * freq[None, :]
    cosine, sine = jnp.cos(angle), jnp.sin(angle)
    keep = jnp.where(lane < ROT, cosine, 1.0)
    from_left = jnp.where((lane >= half) & (lane < ROT), sine, 0.0)
    from_right = jnp.where(lane < half, -sine, 0.0)
    return keep, from_left, from_right


def turn(field, keep, from_left, from_right):
    half = ROT // 2
    left = pltpu.roll(field, half, 1)
    right = pltpu.roll(field, LANES - half, 1)
    return field * keep + left * from_left + right * from_right


def lane_iota(rows):
    return lax.broadcasted_iota(jnp.int32, (rows, LANES), 1)


def attn_fwd_kernel(len_ref, qkv_ref, keep_ref, left_ref, right_ref, q_ref, k_ref, v_ref, mix_ref, lse_ref):
    seq = qkv_ref.shape[0]
    scale = HEAD ** (-0.5)
    slot_len = len_ref[0]
    keep, left, right = keep_ref[...], left_ref[...], right_ref[...]
    q_low = turn(qkv_ref[:, :LANES], keep, left, right).astype(BF16) * jnp.asarray(scale, BF16)
    k_low = turn(qkv_ref[:, LANES : 2 * LANES], keep, left, right).astype(BF16)
    v_low = qkv_ref[:, 2 * LANES :].astype(BF16)
    q_ref[...] = q_low
    k_ref[...] = k_low
    v_ref[...] = v_low
    lane = lane_iota(seq)
    key_row = lax.broadcasted_iota(jnp.int32, (seq, LANES), 0)
    key_bias = jnp.where(key_row < slot_len, 0.0, masked_score).astype(BF16)
    one = jnp.ones((seq, LANES), BF16)
    none = jnp.zeros((seq, LANES), BF16)
    q_heads, k_heads, v_heads = [], [], []
    for head in range(2):
        inside = (lane // HEAD) == head
        flag = lane == (1 - head) * HEAD
        q_heads.append(jnp.where(inside, q_low, jnp.where(flag, one, none)))
        k_heads.append(jnp.where(flag, key_bias, k_low))
        v_heads.append(jnp.where(flag, one, v_low))
    rows = lax.broadcasted_iota(jnp.int32, (QBLOCK, QBLOCK), 0)
    cols = lax.broadcasted_iota(jnp.int32, (QBLOCK, QBLOCK), 1)
    causal = cols <= rows
    lane_q = lane_iota(QBLOCK)
    for block in range(seq // QBLOCK):
        start = block * QBLOCK
        mixed = []
        lses = []
        for head in range(2):
            q_block = q_heads[head][start : start + QBLOCK]
            diag = times_trans(q_block, k_heads[head][start : start + QBLOCK])
            diag = jnp.where(causal, diag, masked_score)
            top = jnp.max(diag, axis=1, keepdims=True)
            if block:
                past = times_trans(q_block, k_heads[head][:start])
                top = jnp.maximum(top, jnp.max(past, axis=1, keepdims=True))
            total = product(jnp.exp(diag - top).astype(BF16), v_heads[head][start : start + QBLOCK])
            if block:
                total += product(jnp.exp(past - top).astype(BF16), v_heads[head][:start])
            flag = (1 - head) * HEAD
            norm = total[:, flag : flag + 1]
            mixed.append(total * (1.0 / norm))
            lses.append(top + jnp.log(norm))
        mix_ref[start : start + QBLOCK, :] = jnp.where(lane_q < HEAD, mixed[0], mixed[1]).astype(BF16)
        lse_ref[start : start + QBLOCK, :] = jnp.where(lane_q < HEAD, lses[0], lses[1])


def attn_bwd_kernel(
    len_ref, q_ref, k_ref, v_ref, grad_ref, lse_ref, keep_ref, left_ref, right_ref, out_ref, dk_ref, dv_ref
):
    seq = q_ref.shape[0]
    scale = HEAD ** (-0.5)
    slot_len = len_ref[0]
    lane = lane_iota(seq)
    key_row = lax.broadcasted_iota(jnp.int32, (seq, LANES), 0)
    key_bias = jnp.where(key_row < slot_len, 0.0, masked_score).astype(BF16)
    none = jnp.zeros((seq, LANES), BF16)
    one = jnp.ones((seq, LANES), BF16)
    k_low = k_ref[...]
    v_low = v_ref[...]
    lane_q = lane_iota(QBLOCK)
    rows = lax.broadcasted_iota(jnp.int32, (QBLOCK, QBLOCK), 0)
    cols = lax.broadcasted_iota(jnp.int32, (QBLOCK, QBLOCK), 1)
    causal = cols <= rows
    k_heads, q_flags, q_clean, g_clean = [], [], [], []
    for head in range(2):
        inside = (lane // HEAD) == head
        flag = lane == (1 - head) * HEAD
        k_heads.append(jnp.where(flag, key_bias, k_low))
        clean = jnp.where(inside, q_ref[...], none)
        q_clean.append(clean)
        q_flags.append(jnp.where(flag, one, clean))
        g_clean.append(jnp.where(inside, grad_ref[...], none))
    blocks = seq // QBLOCK
    for block in range(blocks):
        start = block * QBLOCK
        stop = start + QBLOCK
        parts = []
        for head in range(2):
            lse = lse_ref[start:stop, head * HEAD : head * HEAD + 1]
            q_block = q_clean[head][start:stop]
            g_block = g_clean[head][start:stop]
            spans = [(start, stop)] + ([(0, start)] if block else [])
            kept = []
            row_dot = 0.0
            for low, high in spans:
                logits = times_trans(q_flags[head][start:stop], k_heads[head][low:high])
                if low == start:
                    logits = jnp.where(causal, logits, masked_score)
                probs = jnp.exp(logits - lse)
                prob_grad = times_trans(g_block, v_low[low:high])
                row_dot = row_dot + jnp.sum(probs * prob_grad, axis=1, keepdims=True)
                kept.append((low, high, probs, prob_grad))
            query = 0.0
            for low, high, probs, prob_grad in kept:
                score_grad = (probs * (prob_grad - row_dot)).astype(BF16)
                query = query + product(score_grad, k_low[low:high])
                key_part = inner_rows(score_grad, q_block)
                value_part = inner_rows(probs.astype(BF16), g_block)
                if low == start and head == 0:
                    dk_ref[low:high, :] = key_part
                    dv_ref[low:high, :] = value_part
                else:
                    dk_ref[low:high, :] += key_part
                    dv_ref[low:high, :] += value_part
            parts.append(query)
        query = jnp.where(lane_q < HEAD, parts[0], parts[1]) * scale
        out_ref[start:stop, :LANES] = turn(
            query, keep_ref[start:stop, :], -left_ref[start:stop, :], -right_ref[start:stop, :]
        ).astype(BF16)
    out_ref[:, LANES : 2 * LANES] = turn(
        dk_ref[...], keep_ref[...], -left_ref[...], -right_ref[...]
    ).astype(BF16)
    out_ref[:, 2 * LANES :] = dv_ref[...].astype(BF16)


def attention_forward(lengths, qkv, tables):
    seq, width = qkv.shape
    pairs = width // (3 * LANES)
    wide = pl.BlockSpec((seq, 3 * LANES), lambda p: (0, p))
    col = pl.BlockSpec((seq, LANES), lambda p: (0, p))
    whole = pl.BlockSpec((seq, LANES), lambda p: (0, 0))
    low = jax.ShapeDtypeStruct((seq, pairs * LANES), BF16)
    return pl.pallas_call(
        attn_fwd_kernel,
        grid=(pairs,),
        in_specs=[pl.BlockSpec(memory_space=pltpu.SMEM), wide, whole, whole, whole],
        out_specs=[col] * 5,
        out_shape=[low, low, low, low, jax.ShapeDtypeStruct((seq, pairs * LANES), F32)],
        compiler_params=pltpu.CompilerParams(
            dimension_semantics=("arbitrary",), vmem_limit_bytes=48 * 1024 * 1024
        ),
        cost_estimate=pl.CostEstimate(
            flops=pairs * 12 * seq * seq * LANES, bytes_accessed=pairs * seq * LANES * 24, transcendentals=0
        ),
        name="attn_fwd",
    )(lengths, qkv, *tables)


def attention_backward(lengths, q_low, k_low, v_low, mixed_grad, lse, tables):
    seq = q_low.shape[0]
    pairs = q_low.shape[1] // LANES
    wide = pl.BlockSpec((seq, 3 * LANES), lambda p: (0, p))
    col = pl.BlockSpec((seq, LANES), lambda p: (0, p))
    whole = pl.BlockSpec((seq, LANES), lambda p: (0, 0))
    return pl.pallas_call(
        attn_bwd_kernel,
        grid=(pairs,),
        in_specs=[pl.BlockSpec(memory_space=pltpu.SMEM)] + [col] * 5 + [whole] * 3,
        out_specs=wide,
        out_shape=jax.ShapeDtypeStruct((seq, pairs * 3 * LANES), BF16),
        scratch_shapes=[pltpu.VMEM((seq, LANES), F32), pltpu.VMEM((seq, LANES), F32)],
        compiler_params=pltpu.CompilerParams(
            dimension_semantics=("arbitrary",), vmem_limit_bytes=48 * 1024 * 1024
        ),
        cost_estimate=pl.CostEstimate(
            flops=pairs * 30 * seq * seq * LANES, bytes_accessed=pairs * seq * LANES * 24, transcendentals=0
        ),
        name="attn_bwd",
    )(lengths, q_low, k_low, v_low, mixed_grad, lse, *tables)


def swap_pairs(count, flip):
    return [(i, i ^ flip) for i in range(count)]


def line_scatter(grad, places):
    size = lax.axis_size("dp")
    stations = size // 2
    me = lax.axis_index("dp")
    core, place = me % 2, me // 2
    rows = grad.shape[0] // size
    stack = grad.reshape(stations, 2, rows, grad.shape[1])
    mine = lax.dynamic_index_in_dim(stack, core, 1, keepdims=False)
    other = lax.dynamic_index_in_dim(stack, 1 - core, 1, keepdims=False)
    got = lax.ppermute(other, "dp", swap_pairs(size, 1))
    pair = (mine.astype(F32) + got.astype(F32)).astype(BF16)

    def at(target):
        return lax.dynamic_index_in_dim(pair, jnp.clip(target, 0, stations - 1), 0, keepdims=False)

    up = down = None
    for step in range(1, stations):
        send_up = at(place + stations - step)
        send_down = at(place - stations + step)
        if step > 1:
            send_up = (send_up.astype(F32) + up.astype(F32)).astype(BF16)
            send_down = (send_down.astype(F32) + down.astype(F32)).astype(BF16)
        up_pairs = [(2 * z + c, 2 * z + 2 + c) for z in range(step) for c in range(2)]
        down_pairs = [(size - 1 - a, size - 1 - b) for a, b in up_pairs]
        up = lax.ppermute(send_up, "dp", up_pairs)
        down = lax.ppermute(send_down, "dp", down_pairs)
    return at(place).astype(F32) + up.astype(F32) + down.astype(F32)


def scatter(grad, how):
    if how == "line":
        return line_scatter(grad, None)
    return lax.psum_scatter(grad, "dp", scatter_dimension=0, tiled=True).astype(F32)


def gather_rows(parts, seq_rows):
    tensor = lax.axis_index("tensor")
    tok_rows, width = parts[0].shape
    whole = jnp.zeros((seq_rows, width), parts[0].dtype)
    for flip, part in enumerate(parts):
        whole = lax.dynamic_update_slice_in_dim(whole, part, (tensor ^ flip) * tok_rows, 0)
    return whole


def tensor_scatter(partial, tok_rows):
    count = lax.axis_size("tensor")
    tensor = lax.axis_index("tensor")

    def block(flip):
        return lax.dynamic_slice_in_dim(partial, (tensor ^ flip) * tok_rows, tok_rows, 0)

    total = block(0)
    low = partial.astype(BF16)
    for flip in range(1, count):
        sent = lax.dynamic_slice_in_dim(low, (tensor ^ flip) * tok_rows, tok_rows, 0)
        total = total + lax.ppermute(sent, "tensor", swap_pairs(count, flip)).astype(F32)
    return total


def on_device(
    tokens,
    cotangent,
    lengths,
    norm_gain,
    norm_bias,
    query_weight,
    key_weight,
    value_weight,
    qkv_bias,
    proj_weight,
    proj_bias,
    up_weight,
    up_bias,
    down_weight,
    down_bias,
):
    tensor_count = lax.axis_size("tensor")
    dp_count = lax.axis_size("dp")
    tensor = lax.axis_index("tensor")
    tok_rows, width = tokens.shape
    seq_rows = tok_rows * tensor_count
    heads_width = query_weight.shape[1]
    ff = up_weight.shape[1]
    pairs = heads_width // LANES
    slot_len = lengths[0]

    attn_in = jnp.concatenate(
        [
            item[:, p * LANES : (p + 1) * LANES]
            for p in range(pairs)
            for item in (query_weight, key_weight, value_weight)
        ],
        axis=1,
    )
    attn_pack = jnp.concatenate([attn_in, proj_weight.T], axis=1)
    attn_full = lax.all_gather(attn_pack, "dp", axis=0, tiled=True)
    down_t = down_weight.T
    weight_sum = sum(MLP_PARTS)
    edges = [0]
    for part in MLP_PARTS:
        edges.append(edges[-1] + ff * part // weight_sum)
    mlp_full = []
    for low, high in zip(edges[:-1], edges[1:]):
        pack = jnp.concatenate([up_weight[:, low:high], down_t[:, low:high]], axis=1)
        mlp_full.append(lax.all_gather(pack, "dp", axis=0, tiled=True))

    small = jnp.concatenate(
        [norm_gain, norm_bias, proj_bias, down_bias, qkv_bias.reshape(-1), up_bias.reshape(-1)]
    )
    small_all = lax.all_gather(small, "dp", axis=0, tiled=False)
    shard = norm_gain.shape[0]
    n_gain = small_all[:, :shard].reshape(-1).astype(F32)
    n_shift = small_all[:, shard : 2 * shard].reshape(-1).astype(F32)
    b_out = (
        small_all[:, 2 * shard : 3 * shard].astype(F32) + small_all[:, 3 * shard : 4 * shard].astype(F32)
    ).reshape(-1)
    heads_here = qkv_bias.shape[1]
    head_size = qkv_bias.size
    b_heads = (
        small_all[:, 4 * shard : 4 * shard + head_size]
        .reshape((dp_count,) + qkv_bias.shape)
        .transpose(1, 2, 0, 3)
        .reshape(3, pairs, LANES)
    )
    b_qkv = b_heads.transpose(1, 0, 2).reshape(-1).astype(F32)
    b_up = (
        small_all[:, 4 * shard + head_size :]
        .reshape((dp_count,) + up_bias.shape)
        .transpose(1, 0, 2)
        .reshape(-1)
        .astype(F32)
    )

    tok_parts = [tokens] + [
        lax.ppermute(tokens, "tensor", swap_pairs(tensor_count, flip)) for flip in range(1, tensor_count)
    ]
    grad_parts = [cotangent] + [
        lax.ppermute(cotangent, "tensor", swap_pairs(tensor_count, flip)) for flip in range(1, tensor_count)
    ]
    normed_parts = [layer_norm(part.astype(F32), n_gain, n_shift).astype(BF16) for part in tok_parts]
    normed = gather_rows(normed_parts, seq_rows)

    def masked(part, flip):
        pos = (tensor ^ flip) * tok_rows + jnp.arange(tok_rows)
        return jnp.where((pos < slot_len)[:, None], part, jnp.zeros_like(part))

    grad_all = gather_rows([masked(part, flip) for flip, part in enumerate(grad_parts)], seq_rows)

    tables = rotary_lanes(seq_rows)
    in_cols = 3 * heads_width
    w_qkv = attn_full[:, :in_cols]
    w_proj_t = attn_full[:, in_cols:]
    qkv = product(normed, w_qkv) + b_qkv
    q_low, k_low, v_low, mixed, lse = attention_forward(lengths, qkv, tables)
    mixed_grad = product(grad_all, w_proj_t).astype(BF16)
    proj_grad_t = inner_rows(grad_all, mixed).astype(BF16)
    qkv_grad = attention_backward(lengths, q_low, k_low, v_low, mixed_grad, lse, tables)
    in_grad = inner_rows(normed, qkv_grad).astype(BF16)
    attn_shard = scatter(jnp.concatenate([in_grad, proj_grad_t], axis=1), ATTN_RS)
    branch = times_trans(mixed, w_proj_t)
    normed_grad = times_trans(qkv_grad, w_qkv)
    head_bias_grad = jnp.sum(qkv_grad, axis=0, dtype=F32)

    mlp_shards = []
    up_bias_grads = []
    for index, (low, high) in enumerate(zip(edges[:-1], edges[1:])):
        units = high - low
        w_up = mlp_full[index][:, :units]
        w_down_t = mlp_full[index][:, units:]
        up_pre = product(normed, w_up) + b_up[low:high]
        act, gelu_back = jax.vjp(lambda value: jax.nn.gelu(value, approximate=True), up_pre)
        act = act.astype(BF16)
        up_pre_grad = gelu_back(product(grad_all, w_down_t))[0].astype(BF16)
        down_grad_t = inner_rows(grad_all, act).astype(BF16)
        up_grad = inner_rows(normed, up_pre_grad).astype(BF16)
        mlp_shards.append(scatter(jnp.concatenate([up_grad, down_grad_t], axis=1), MLP_RS[index]))
        up_bias_grads.append(jnp.sum(up_pre_grad, axis=0, dtype=F32))
        normed_grad = normed_grad + times_trans(up_pre_grad, w_up)
        branch = branch + times_trans(act, w_down_t)

    own = tokens.astype(F32)
    output = (own + tensor_scatter(branch, tok_rows) + b_out).astype(BF16)
    own_normed_grad = tensor_scatter(normed_grad, tok_rows)
    _, norm_back = jax.vjp(layer_norm, own, n_gain, n_shift)
    input_part, gain_part, shift_part = norm_back(own_normed_grad)
    input_grad = masked(cotangent, 0).astype(F32) + input_part
    gain_sum, shift_sum = lax.psum((gain_part, shift_part), "tensor")

    head_part = (
        head_bias_grad.reshape(pairs, 3, LANES)
        .transpose(1, 0, 2)
        .reshape(3, heads_here, dp_count, HEAD // dp_count)
        .transpose(2, 0, 1, 3)
        .reshape(dp_count, -1)
    )
    up_part = (
        jnp.concatenate(up_bias_grads)
        .reshape(up_bias.shape[0], dp_count, -1)
        .transpose(1, 0, 2)
        .reshape(dp_count, -1)
    )
    out_bias_part = jnp.sum(grad_all, axis=0, dtype=F32).reshape(dp_count, shard)
    small_grad = jnp.concatenate(
        [gain_sum.reshape(dp_count, shard), shift_sum.reshape(dp_count, shard), out_bias_part, head_part, up_part],
        axis=1,
    ).astype(BF16)
    small_out = lax.psum_scatter(small_grad, "dp", scatter_dimension=0, tiled=True)[0].astype(F32)
    gain_grad = small_out[:shard]
    shift_grad = small_out[shard : 2 * shard]
    out_bias = small_out[2 * shard : 3 * shard]
    head_out = small_out[3 * shard : 3 * shard + head_size].reshape(qkv_bias.shape)
    up_bias_out = small_out[3 * shard + head_size :].reshape(up_bias.shape)

    def part_of(which):
        return jnp.concatenate(
            [attn_shard[:, (3 * p + which) * LANES : (3 * p + which + 1) * LANES] for p in range(pairs)], axis=1
        )

    up_out = jnp.concatenate([item[:, : item.shape[1] // 2] for item in mlp_shards], axis=1)
    down_out = jnp.concatenate([item[:, item.shape[1] // 2 :].T for item in mlp_shards], axis=0)
    return (
        output,
        input_grad,
        gain_grad,
        shift_grad,
        part_of(0),
        part_of(1),
        part_of(2),
        head_out,
        attn_shard[:, in_cols:].T,
        out_bias,
        up_out,
        up_bias_out,
        down_out,
        out_bias,
    )


def solution(mesh):
    rows = P(("dp", "tensor"), None)
    both = P("dp", "tensor")
    turned = P("tensor", "dp")
    heads = P(None, "tensor", "dp")
    vec = P("dp")
    return jax.shard_map(
        on_device,
        mesh=mesh,
        in_specs=(rows, rows, vec, vec, vec, both, both, both, heads, turned, vec, both, turned, turned, vec),
        out_specs=(rows, rows, vec, vec, both, both, both, heads, turned, vec, both, turned, turned, vec),
        check_vma=False,
    )
```

time: 893 us -> 708 us (0.79)
  the two profiles are of different devices: /device:TPU:0 before, /device:TPU:17 now
where the time goes in v1:
time: 708 us; the launch traced here: 703 us
  matrix products  168 us (24%)
  local copies, waits for them, and re-layouts  115 us (16%)
  waiting for transfers between devices  112 us (16%)
  blocking collectives  108 us (15%)
  other arithmetic  104 us (15%)
  Pallas kernels  43.5 us (6%)
  starting transfers between devices  35.9 us (5%)
  between operations  16.7 us (2%)
    unnamed x2, blocking collectives  95.3 us
    ppermute x6, waiting for transfers between devices, line_scatter(): down = lax.ppermute(send_down, 'dp', down_pairs)  74.4 us
    dot_general x6, matrix products, times_trans(): lax.dot_general(left, right, (((1,), (1,)), ((), ())), preferred_element_...  62 us
    dot_general x6, matrix products, product(): return jnp.dot(left, right, preferred_element_type=F32)  56.4 us
    dot_general x6, matrix products, inner_rows(): lax.dot_general(left, right, (((0,), (0,)), ((), ())), preferred_element_...  50 us
    dynamic_slice x2, local copies, waits for them, and re-layouts, line_scatter(): mine = lax.dynamic_index_in_dim(stack, core, 1, keepdims=False)  29.1 us
    all_gather x2, waiting for transfers between devices, on_device(): mlp_full.append(lax.all_gather(pack, 'dp', axis=0, tiled=True))  28 us
    pallas_call x1, Pallas kernels, attention_backward(): pl.pallas_call(attn_bwd_kernel, grid=(pairs,), in_specs=[pl.BlockSpec(mem...  26.6 us
  transfers between devices with their start and end apart: 30, of which 7 were waited for; matrix products, arithmetic and copies ran while one was open for 48% of the time, Pallas kernels for 6%

profile of v1, /device:TPU:17, one launch (start us, length us, event | category | flops | bytes accessed | tf_op | source)
XLA Modules:
  0.0 702.7 jit_solution(2693501522823968031)
XLA Ops:
  25.5 35.4 %all-reduce = bf16[11776]{0:T(1024)(128)(2,1)S(1)} all-reduce(bf16[11776]{0:T(1024)(128)(2,1)S(1)} %dynamic-update-slice), channel_id=2, replica_groups=mesh['dp'=8,'tensor'=4] {'dp'}, use_global_device_ids=true, to_apply=%add | all-reduce | flops 11776 | bytes 47104
  99.7 9.8 %collective-permute-done.8 = bf16[256,2048]{1,0:T(8,128)(2,1)S(1)} collective-permute-done((bf16[256,2048]{1,0:T(8,128)(2,1)}, bf16[256,2048]{1,0:T(8,128)(2,1)S(1)}, u32[]{:S(2)}, u32[]{:S(2)}) %collective-permute-start.8) | collective-permute-done | bytes 1048608 | tf_op jit(solution)/shard_map/ppermute | solution.py:371
  114.3 11.7 %fusion.6.qkv_ref = f32[1024,1536]{1,0:T(8,128)} fusion(bf16[1024,2048]{1,0:T(8,128)(2,1)} %fusion.91, bf16[2048,2048]{0,1:T(8,128)(2,1)} %all-gather.5.cloned.1.call-done, f32[1536]{0:T(1024)S(1)} %reshape.277), kind=kOutput, calls=%fused_computation.18 | convolution fusion | flops 6444023808 | bytes 16783360 | tf_op jit(solution)/shard_map/dot_general | solution.py:31
  126.1 16.8 %attn_fwd.1 = (bf16[1024,512]{1,0:T(8,128)(2,1)S(1)}, bf16[1024,512]{1,0:T(8,128)(2,1)S(1)}, bf16[1024,512]{1,0:T(8,128)(2,1)S(1)}, bf16[1024,512]{1,0:T(8,128)(2,1)S(1)}, f32[1024,512]{1,0:T(8,128)}) custom-call(s32[1]{0:T(128)} %copy.196.len_ref, f32[1024,1536]{1,0:T(8,128)} %fusion.6.qkv_ref, f32[1024,128]{1,0:T(8,128)S(1)} %get-tuple-element.149.keep_ref, ...), custom_call_target="tpu_custom_call" | custom-call | flops 6442450944 | bytes 12582912 | tf_op jit(solution)/shard_map/attn_fwd/pallas_call | solution.py:191
  145.8 6.2 fusion.86.grad_ref
  152.0 28.0 %all-gather.7.cloned.1.call-done = bf16[2048,2048]{0,1:T(8,128)(2,1)} async-done(((bf16[256,2048]{0,1:T(8,128)(2,1)}), bf16[2048,2048]{0,1:T(8,128)(2,1)}) %all-gather.7.cloned.1.call-update) | async-done | bytes 8388624 | tf_op jit(solution)/shard_map/all_gather | solution.py:338
  180.1 7.7 %fusion.36 = f32[1024,1024]{1,0:T(8,128)S(1)} fusion(bf16[1024,2048]{1,0:T(8,128)(2,1)} %fusion.91, bf16[2048,2048]{0,1:T(8,128)(2,1)} %all-gather.7.cloned.1.call-done), kind=kOutput, calls=%fused_computation.54 | convolution fusion | flops 4294967296 | bytes 12582912 | tf_op jit(solution)/shard_map/dot_general | solution.py:31
  187.8 11.8 %fusion.118 = (bf16[1024]{0:T(1024)(128)(2,1)}, bf16[1024,1024]{1,0:T(8,128)(2,1)S(1)}) fusion(f32[1024,1024]{1,0:T(8,128)S(1)} %fusion.36, f32[1024]{0:T(1024)S(1)} %slice.207, bf16[1024,2048]{1,0:T(8,128)(2,1)} %select_dynamic-update-slice_fusion, bf16[2048,2048]{0,1:T(8,128)(2,1)S(1)} %copy-done.43), kind=kOutput, calls=%fused_computation.228 | convolution fusion | flops 4318034944 | bytes 14686208 | tf_op jit(solution)/shard_map/dot_general | solution.py:31
  199.6 8.4 %convolution_convert_fusion.4 = bf16[2048,1024]{0,1:T(8,128)(2,1)} fusion(bf16[1024,2048]{1,0:T(8,128)(2,1)} %fusion.91, bf16[1024,1024]{1,0:T(8,128)(2,1)S(1)} %get-tuple-element.157), kind=kOutput, calls=%fused_computation.40 | convolution fusion | flops 4297064448 | bytes 10485760 | tf_op jit(solution)/shard_map/dot_general | solution.py:39
  208.0 6.8 fusion.34
  214.8 8.9 %convolution_convert_fusion.3 = bf16[2048,1024]{0,1:T(8,128)(2,1)} fusion(bf16[1024,2048]{1,0:T(8,128)(2,1)} %select_dynamic-update-slice_fusion, f32[1024,1024]{1,0:T(8,128)S(1)} %fusion.36, f32[1024]{0:T(1024)S(1)} %slice.207), kind=kOutput, calls=%fused_computation.39 | convolution fusion | flops 4307550208 | bytes 12587008 | tf_op jit(solution)/shard_map/dot_general | solution.py:39
  223.8 26.6 %attn_bwd.1 = bf16[1024,1536]{1,0:T(8,128)(2,1)} custom-call(s32[1]{0:T(128)} %copy.196.len_ref, bf16[1024,512]{1,0:T(8,128)(2,1)S(1)} %copy-done.2, bf16[1024,512]{1,0:T(8,128)(2,1)S(1)} %copy-done.4, bf16[1024,512]{1,0:T(8,128)(2,1)S(1)} %copy-done.6, bf16[1024,512]{1,0:T(8,128)(2,1)S(1)} %copy-done, f32[1024,512]{1,0:T(8,128)} %get-tuple-element.23.lse_ref, ...), custom_call_target="tpu_custom_call" | custom-call | flops 16106127360 | bytes 12582912 | tf_op jit(solution)/shard_map/attn_bwd/pallas_call | solution.py:213
  250.4 10.4 %fusion.2 = f32[1024,2048]{1,0:T(8,128)} fusion(bf16[1024,1536]{1,0:T(8,128)(2,1)} %attn_bwd.1, bf16[2048,2048]{0,1:T(8,128)(2,1)S(1)} %bitcast.125), kind=kOutput, calls=%fused_computation.14 | convolution fusion | flops 6442450944 | bytes 17825792 | tf_op jit(solution)/shard_map/dot_general | solution.py:35
  260.8 10.9 %convolution_convert_fusion = bf16[2048,1536]{0,1:T(8,128)(2,1)} fusion(bf16[1024,2048]{1,0:T(8,128)(2,1)} %fusion.91, bf16[1024,1536]{1,0:T(8,128)(2,1)S(1)} %copy-done.16), kind=kOutput, calls=%fused_computation.9 | convolution fusion | flops 6445596672 | bytes 13631488 | tf_op jit(solution)/shard_map/dot_general | solution.py:39
  271.7 7.9 %fusion.28 = f32[1024,1024]{1,0:T(8,128)S(1)} fusion(bf16[1024,2048]{1,0:T(8,128)(2,1)} %fusion.91, bf16[2048,2048]{0,1:T(8,128)(2,1)} %all-gather.9.cloned.1.call-done), kind=kOutput, calls=%fused_computation.46 | convolution fusion | flops 4294967296 | bytes 12582912 | tf_op jit(solution)/shard_map/dot_general | solution.py:31
  279.6 11.0 %fusion.117 = (bf16[1024]{0:T(1024)(128)(2,1)S(1)}, bf16[1024,1024]{1,0:T(8,128)(2,1)S(1)}) fusion(f32[1024,1024]{1,0:T(8,128)S(1)} %fusion.28, f32[1024]{0:T(1024)S(1)} %slice.213, bf16[1024,2048]{1,0:T(8,128)(2,1)} %select_dynamic-update-slice_fusion, bf16[2048,2048]{0,1:T(8,128)(2,1)S(1)} %copy-done.44), kind=kOutput, calls=%fused_computation.227 | convolution fusion | flops 4318034944 | bytes 14686208 | tf_op jit(solution)/shard_map/dot_general | solution.py:31
  290.6 11.1 %fusion.115 = (bf16[1024,2048]{1,0:T(8,128)(2,1)S(1)}, f32[1024,2048]{1,0:T(8,128)}) fusion(bf16[1024,1024]{1,0:T(8,128)(2,1)S(1)} %get-tuple-element.155, bf16[2048,2048]{0,1:T(8,128)(2,1)S(1)} %copy-done.44, f32[1024,2048]{1,0:T(8,128)} %fusion.2, f32[1024,2048]{1,0:T(8,128)} %fusion.34), kind=kOutput, calls=%fused_computation.225 | convolution fusion | flops 4301258752 | bytes 35651584 | tf_op jit(solution)/shard_map/dot_general | solution.py:35
  306.1 4.6 convolution_convert_fusion.5
  310.7 7.7 %pad_maximum_fusion = bf16[2048,2048]{0,1:T(8,128)(2,1)} fusion(bf16[2048,512]{0,1:T(8,128)(2,1)S(1)} %convolution_convert_fusion.5, bf16[2048,1536]{0,1:T(8,128)(2,1)} %convolution_convert_fusion), kind=kLoop, calls=%fused_computation | loop fusion | flops 16777216 | bytes 16777216 | tf_op jit(solution)/shard_map/concatenate | solution.py:392
  318.4 14.4 %reshape.273 = bf16[4,2,256,2048]{2,1,0,3:T(2,128)(2,1)} reshape(bf16[2048,2048]{0,1:T(8,128)(2,1)} %pad_maximum_fusion) | data formatting | bytes 16777216 | tf_op jit(solution)/shard_map/reshape | solution.py:240
  332.8 20.6 %constant_dynamic-slice_fusion.3 = (bf16[4,1,256,2048]{2,1,0,3:T(2,128)(2,1)}, bf16[4,1,256,2048]{2,1,0,3:T(2,128)(2,1)S(1)}) fusion(bf16[4,2,256,2048]{2,1,0,3:T(2,128)(2,1)} %reshape.273, s32[]{:T(128)S(6)} %select_n.144, s32[]{:T(128)S(6)} %select_n.145), kind=kLoop, calls=%fused_computation.170 | loop fusion | bytes 16777224 | tf_op jit(solution)/shard_map/jit(dynamic_index_in_dim)/dynamic_slice | solution.py:241
  353.4 3.4 copy.170
  358.1 8.4 %pad_maximum_fusion.1 = bf16[2048,2048]{0,1:T(8,128)(2,1)} fusion(bf16[2048,1024]{0,1:T(8,128)(2,1)} %convolution_convert_fusion.3, bf16[2048,1024]{0,1:T(8,128)(2,1)} %convolution_convert_fusion.4), kind=kLoop, calls=%fused_computation.1 | loop fusion | flops 16777216 | bytes 16777216 | tf_op jit(solution)/shard_map/concatenate | solution.py:409
  368.2 8.5 %convolution_convert_fusion.2 = bf16[2048,1024]{0,1:T(8,128)(2,1)} fusion(bf16[1024,2048]{1,0:T(8,128)(2,1)} %fusion.91, bf16[1024,1024]{1,0:T(8,128)(2,1)S(1)} %copy-done.46), kind=kOutput, calls=%fused_computation.38 | convolution fusion | flops 4297064448 | bytes 10485760 | tf_op jit(solution)/shard_map/dot_general | solution.py:39
  376.7 8.8 %convolution_convert_fusion.1 = bf16[2048,1024]{0,1:T(8,128)(2,1)} fusion(bf16[1024,2048]{1,0:T(8,128)(2,1)} %select_dynamic-update-slice_fusion, f32[1024,1024]{1,0:T(8,128)S(1)} %copy-done.49, f32[1024]{0:T(1024)S(1)} %slice.213), kind=kOutput, calls=%fused_computation.37 | convolution fusion | flops 4307550208 | bytes 12587008 | tf_op jit(solution)/shard_map/dot_general | solution.py:39
  385.5 8.5 %pad_maximum_fusion.2 = bf16[2048,2048]{0,1:T(8,128)(2,1)} fusion(bf16[2048,1024]{0,1:T(8,128)(2,1)} %convolution_convert_fusion.1, bf16[2048,1024]{0,1:T(8,128)(2,1)} %convolution_convert_fusion.2), kind=kLoop, calls=%fused_computation.2 | loop fusion | flops 16777216 | bytes 16777216 | tf_op jit(solution)/shard_map/concatenate | solution.py:409
  394.0 12.3 %copy.138 = bf16[2048,2048]{1,0:T(8,128)(2,1)} copy(bf16[2048,2048]{0,1:T(8,128)(2,1)} %pad_maximum_fusion.2) | data formatting | bytes 16777216 | tf_op jit(solution)/shard_map/concatenate | solution.py:409
  406.3 8.6 %constant_dynamic-slice_fusion.1 = (bf16[4,1,256,2048]{3,2,1,0:T(8,128)(2,1)}, bf16[4,1,256,2048]{3,2,1,0:T(8,128)(2,1)}) fusion(bf16[4,2,256,2048]{3,2,1,0:T(8,128)(2,1)} %bitcast.114, s32[]{:T(128)S(6)} %select_n.144, s32[]{:T(128)S(6)} %select_n.145), kind=kLoop, calls=%fused_computation.168 | loop fusion | bytes 16777224 | tf_op jit(solution)/shard_map/jit(dynamic_index_in_dim)/dynamic_slice | solution.py:241
  414.9 6.4 copy.140
  421.4 11.8 %fusion.25 = f32[1024,2048]{1,0:T(8,128)} fusion(bf16[2048,2048]{0,1:T(8,128)(2,1)} %all-gather.9.cloned.1.call-done, f32[1024,1024]{1,0:T(8,128)} %copy-done.48, f32[1024]{0:T(1024)S(1)} %slice.213), kind=kOutput, calls=%fused_computation.43 | convolution fusion | flops 4305453056 | bytes 16781312 | tf_op jit(solution)/shard_map/dot_general | solution.py:35
  433.6 11.9 %fusion.32 = f32[1024,2048]{1,0:T(8,128)} fusion(bf16[2048,2048]{0,1:T(8,128)(2,1)} %all-gather.7.cloned.1.call-done, f32[1024,1024]{1,0:T(8,128)} %copy-done.47, f32[1024]{0:T(1024)S(1)} %copy-done.32), kind=kOutput, calls=%fused_computation.50 | convolution fusion | flops 4305453056 | bytes 16781312 | tf_op jit(solution)/shard_map/dot_general | solution.py:35
  445.5 10.0 %fusion.116 = (bf16[1024,2048]{1,0:T(8,128)(2,1)S(1)}, f32[1024,2048]{1,0:T(8,128)}) fusion(f32[1024,2048]{1,0:T(8,128)S(1)} %copy-done.13, f32[1024,2048]{1,0:T(8,128)} %fusion.32, bf16[1024,512]{1,0:T(8,128)(2,1)S(1)} %get-tuple-element.19, bf16[2048,2048]{0,1:T(8,128)(2,1)} %all-gather.5.cloned.1.call-done), kind=kOutput, calls=%fused_computation.226 | convolution fusion | flops 2153775104 | bytes 32505856 | tf_op jit(solution)/shard_map/dot_general | solution.py:35
  459.6 6.4 copy.161
  466.7 6.3 fusion.1
  475.4 3.6 fusion.105
  480.3 3.1 fusion
  490.3 12.4 %all-reduce.2 = (bf16[2048]{0:T(1024)(128)(2,1)S(1)}, bf16[2048]{0:T(1024)(128)(2,1)S(1)}) all-reduce(f32[2048]{0:T(1024)S(1)} %get-tuple-element.80, f32[2048]{0:T(1024)S(1)} %get-tuple-element.82), channel_id=1, replica_groups=mesh['dp'=8,'tensor'=4] {'tensor'}, use_global_device_ids=true, to_apply=%region_11.12 | all-reduce | flops 4096 | bytes 24576 | tf_op jit(solution)/shard_map/psum | solution.py:420
  502.9 59.9 %all-reduce.1 = bf16[8,1216]{1,0:T(8,128)(2,1)S(1)} all-reduce(bf16[8,1216]{1,0:T(8,128)(2,1)S(1)} %concatenate.56), channel_id=3, replica_groups=mesh['dp'=8,'tensor'=4] {'dp'}, use_global_device_ids=true, to_apply=%region_18.19.clone | all-reduce | flops 9728 | bytes 38912
  568.1 4.0 fusion.81
  572.2 4.0 collective-permute-start.17
  580.3 11.5 %collective-permute-done.23 = bf16[256,2048]{0,1:T(8,128)(2,1)} collective-permute-done((bf16[256,2048]{0,1:T(8,128)(2,1)}, bf16[256,2048]{0,1:T(8,128)(2,1)}, u32[]{:S(2)}, u32[]{:S(2)}) %collective-permute-start.23) | collective-permute-done | bytes 1048608 | tf_op jit(solution)/shard_map/ppermute | solution.py:259
  593.9 3.7 fusion.76
  597.6 15.4 %collective-permute-done.17 = bf16[256,2048]{0,1:T(8,128)(2,1)} collective-permute-done((bf16[256,2048]{0,1:T(8,128)(2,1)}, bf16[256,2048]{0,1:T(8,128)(2,1)}, u32[]{:S(2)}, u32[]{:S(2)}) %collective-permute-start.17) | collective-permute-done | bytes 1048608 | tf_op jit(solution)/shard_map/ppermute | solution.py:259
  618.4 4.6 add_add_fusion.3
  623.1 3.4 collective-permute-start.22
  626.5 13.7 %collective-permute-done.24 = bf16[256,2048]{0,1:T(8,128)(2,1)S(1)} collective-permute-done((bf16[256,2048]{0,1:T(8,128)(2,1)S(1)}, bf16[256,2048]{0,1:T(8,128)(2,1)S(1)}, u32[]{:S(2)}, u32[]{:S(2)}) %collective-permute-start.24) | collective-permute-done | bytes 1048608 | tf_op jit(solution)/shard_map/ppermute | solution.py:259
  644.8 17.8 %collective-permute-done.18 = bf16[256,2048]{0,1:T(8,128)(2,1)S(1)} collective-permute-done((bf16[256,2048]{0,1:T(8,128)(2,1)S(1)}, bf16[256,2048]{0,1:T(8,128)(2,1)S(1)}, u32[]{:S(2)}, u32[]{:S(2)}) %collective-permute-start.18) | collective-permute-done | bytes 1048608 | tf_op jit(solution)/shard_map/ppermute | solution.py:259
  668.6 16.0 %collective-permute-done.25 = bf16[256,2048]{0,1:T(8,128)(2,1)} collective-permute-done((bf16[256,2048]{0,1:T(8,128)(2,1)}, bf16[256,2048]{0,1:T(8,128)(2,1)}, u32[]{:S(2)}, u32[]{:S(2)}) %collective-permute-start.25) | collective-permute-done | bytes 1048608 | tf_op jit(solution)/shard_map/ppermute | solution.py:259
  (307 shorter events, 124.8 us)
Async XLA Ops:
  7.2 107.2 %all-gather.5.cloned.1.call-start = ((), (), s32[]{:S(2)}) async-start(), calls=%async_computation.1 | async-start | bytes 9437184 | tf_op jit(solution)/shard_map/all_gather | solution.py:329
  12.8 167.3 %all-gather.7.cloned.1.call-start = ((), (), s32[]{:S(2)}) async-start(), calls=%async_computation.2 | async-start | bytes 9437184 | tf_op jit(solution)/shard_map/all_gather | solution.py:338
  16.8 254.8 %all-gather.9.cloned.1.call-start = ((), (), s32[]{:S(2)}) async-start(), calls=%async_computation.3 | async-start | bytes 9437184 | tf_op jit(solution)/shard_map/all_gather | solution.py:338
  16.9 58.2 %collective-permute-start = (bf16[256,2048]{1,0:T(8,128)(2,1)S(1)}, bf16[256,2048]{1,0:T(8,128)(2,1)}, u32[]{:S(2)}, u32[]{:S(2)}) collective-permute-start(bf16[256,2048]{1,0:T(8,128)(2,1)S(1)} %copy-done.7), channel_id=1, source_target_pairs={{0,1},{1,0},{2,3},{3,2},{4,5},{5,4},{6,7},{7,6},{8,9},{9,8},{10,11... | collective-permute-start | bytes 3145736 | tf_op jit(solution)/shard_map/ppermute | solution.py:368
  18.1 60.7 %collective-permute-start.1 = (bf16[256,2048]{1,0:T(8,128)(2,1)S(1)}, bf16[256,2048]{1,0:T(8,128)(2,1)}, u32[]{:S(2)}, u32[]{:S(2)}) collective-permute-start(bf16[256,2048]{1,0:T(8,128)(2,1)S(1)} %copy-done.7), channel_id=1, source_target_pairs={{0,2},{1,3},{2,0},{3,1},{4,6},{5,7},{6,4},{7,5},{8,10},{9,11},{10,... | collective-permute-start | bytes 3145736 | tf_op jit(solution)/shard_map/ppermute | solution.py:368
  19.4 62.5 %collective-permute-start.2 = (bf16[256,2048]{1,0:T(8,128)(2,1)S(1)}, bf16[256,2048]{1,0:T(8,128)(2,1)}, u32[]{:S(2)}, u32[]{:S(2)}) collective-permute-start(bf16[256,2048]{1,0:T(8,128)(2,1)S(1)} %copy-done.7), channel_id=1, source_target_pairs={{0,3},{1,2},{2,1},{3,0},{4,7},{5,6},{6,5},{7,4},{8,11},{9,10},{10,... | collective-permute-start | bytes 3145736 | tf_op jit(solution)/shard_map/ppermute | solution.py:368
  19.6 67.1 %collective-permute-start.6 = (bf16[256,2048]{1,0:T(8,128)(2,1)}, bf16[256,2048]{1,0:T(8,128)(2,1)}, u32[]{:S(2)}, u32[]{:S(2)}) collective-permute-start(bf16[256,2048]{1,0:T(8,128)(2,1)} %param.16), channel_id=1, source_target_pairs={{0,1},{1,0},{2,3},{3,2},{4,5},{5,4},{6,7},{7,6},{8,9},{9,8},{10,11... | collective-permute-start | bytes 3145736 | tf_op jit(solution)/shard_map/ppermute | solution.py:371
  20.8 71.0 %collective-permute-start.7 = (bf16[256,2048]{1,0:T(8,128)(2,1)}, bf16[256,2048]{1,0:T(8,128)(2,1)}, u32[]{:S(2)}, u32[]{:S(2)}) collective-permute-start(bf16[256,2048]{1,0:T(8,128)(2,1)} %param.16), channel_id=1, source_target_pairs={{0,2},{1,3},{2,0},{3,1},{4,6},{5,7},{6,4},{7,5},{8,10},{9,11},{10,... | collective-permute-start | bytes 3145736 | tf_op jit(solution)/shard_map/ppermute | solution.py:371
  23.3 665.0 %reduce-scatter.2.cloned.1.call-start = ((), (), s32[]{:S(2)}) async-start(), calls=%async_computation.4 | async-start | bytes 9437184 | tf_op jit(solution)/shard_map/reduce_scatter | solution.py:266
  61.2 12.5 %copy-start.22 = (f32[256]{0:T(256)}, f32[256]{0:T(256)S(1)}, u32[]{:S(2)}) copy-start(f32[256]{0:T(256)S(1)} %broadcast_multiply_fusion.3) | copy-start | bytes 3076
  61.6 12.0 %copy-start.25 = (f32[256]{0:T(256)}, f32[256]{0:T(256)S(1)}, u32[]{:S(2)}) copy-start(f32[256]{0:T(256)S(1)} %fusion.98) | copy-start | bytes 3076
  67.9 29.1 %copy-start.19 = (f32[1,2,8,128]{3,1,2,0:T(2,128)}, f32[1,2,8,128]{3,1,2,0:T(2,128)S(1)}, u32[]{:S(2)}) copy-start(f32[1,2,8,128]{3,1,2,0:T(2,128)S(1)} %copy.162) | copy-start | bytes 24580
  68.5 146.3 %copy-start.31 = (f32[1024]{0:T(1024)}, f32[1024]{0:T(1024)S(1)}, u32[]{:S(2)}) copy-start(f32[1024]{0:T(1024)S(1)} %slice.207) | copy-start | bytes 12292
  75.1 34.4 %collective-permute-start.8 = (bf16[256,2048]{1,0:T(8,128)(2,1)}, bf16[256,2048]{1,0:T(8,128)(2,1)S(1)}, u32[]{:S(2)}, u32[]{:S(2)}) collective-permute-start(bf16[256,2048]{1,0:T(8,128)(2,1)} %param.16), channel_id=1, source_target_pairs={{0,3},{1,2},{2,1},{3,0},{4,7},{5,6},{6,5},{7,4},{8,11},{9,10},{10,... | collective-permute-start | bytes 3145736 | tf_op jit(solution)/shard_map/ppermute | solution.py:371
  187.8 27.0 %copy-start.47 = (f32[1024,1024]{1,0:T(8,128)}, f32[1024,1024]{1,0:T(8,128)S(1)}, u32[]{:S(2)}) copy-start(f32[1024,1024]{1,0:T(8,128)S(1)} %fusion.36) | copy-start | bytes 12582916
  214.8 35.6 %slice-start = ((s8[8388608]{0:T(1024)(128)(4,1)}), s8[4194304]{0:T(1024)(128)(4,1)S(1)}, s32[]{:S(2)}) async-start(s8[8388608]{0:T(1024)(128)(4,1)} %bitcast.124), calls=%async_computation.5 | async-start | bytes 8388608
  223.7 26.6 %slice-start.1 = ((s8[8388608]{0:T(1024)(128)(4,1)}), s8[4194304]{0:T(1024)(128)(4,1)S(1)}, s32[]{:S(2)}) async-start(s8[8388608]{0:T(1024)(128)(4,1)} %bitcast.124), calls=%async_computation.6 | async-start | bytes 8388608
  279.6 11.0 %copy-start.48 = (f32[1024,1024]{1,0:T(8,128)}, f32[1024,1024]{1,0:T(8,128)S(1)}, u32[]{:S(2)}) copy-start(f32[1024,1024]{1,0:T(8,128)S(1)} %fusion.28) | copy-start | bytes 12582916
  290.6 11.1 %copy-start.45 = (bf16[1024,1024]{1,0:T(8,128)(2,1)}, bf16[1024,1024]{1,0:T(8,128)(2,1)S(1)}, u32[]{:S(2)}) copy-start(bf16[1024,1024]{1,0:T(8,128)(2,1)S(1)} %get-tuple-element.155) | copy-start | bytes 6291460
  303.5 170.7 %collective-permute-start.11 = (bf16[256,2048]{1,0:T(8,128)(2,1)}, bf16[256,2048]{1,0:T(8,128)(2,1)}, u32[]{:S(2)}, u32[]{:S(2)}) collective-permute-start(bf16[256,2048]{1,0:T(8,128)(2,1)} %get-tuple-element.100), channel_id=1, source_target_pairs={{0,3},{1,2},{2,1},{3,0},{4,7},{5,6},{6,5},{7,4},{8,11},{9,10},{10,... | collective-permute-start | bytes 3145736 | tf_op jit(solution)/shard_map/ppermute | solution.py:289
  304.3 170.3 %collective-permute-start.10 = (bf16[256,2048]{1,0:T(8,128)(2,1)}, bf16[256,2048]{1,0:T(8,128)(2,1)}, u32[]{:S(2)}, u32[]{:S(2)}) collective-permute-start(bf16[256,2048]{1,0:T(8,128)(2,1)} %get-tuple-element.101), channel_id=1, source_target_pairs={{0,2},{1,3},{2,0},{3,1},{4,6},{5,7},{6,4},{7,5},{8,10},{9,11},{10,... | collective-permute-start | bytes 3145736 | tf_op jit(solution)/shard_map/ppermute | solution.py:289
  304.6 170.7 %collective-permute-start.9 = (bf16[256,2048]{1,0:T(8,128)(2,1)}, bf16[256,2048]{1,0:T(8,128)(2,1)}, u32[]{:S(2)}, u32[]{:S(2)}) collective-permute-start(bf16[256,2048]{1,0:T(8,128)(2,1)} %get-tuple-element.99), channel_id=1, source_target_pairs={{0,1},{1,0},{2,3},{3,2},{4,5},{5,4},{6,7},{7,6},{8,9},{9,8},{10,11... | collective-permute-start | bytes 3145736 | tf_op jit(solution)/shard_map/ppermute | solution.py:289
  356.8 109.3 %collective-permute-start.12 = (bf16[4,256,2048]{1,2,0:T(8,128)(2,1)}, bf16[4,256,2048]{1,2,0:T(8,128)(2,1)}, u32[]{:S(2)}, u32[]{:S(2)}) collective-permute-start(bf16[4,256,2048]{1,2,0:T(8,128)(2,1)} %bitcast.108), channel_id=1, source_target_pairs={{0,4},{4,0},{8,12},{12,8},{16,20},{20,16},{24,28},{28,24},{1,5},{5... | collective-permute-start | bytes 12582920 | tf_op jit(solution)/shard_map/ppermute | solution.py:243
  421.3 12.1 %copy-start.35 = (bf16[1024]{0:T(1024)(128)(2,1)S(1)}, bf16[1024]{0:T(1024)(128)(2,1)}, u32[]{:S(2)}) copy-start(bf16[1024]{0:T(1024)(128)(2,1)} %get-tuple-element.156) | copy-start | bytes 6148
  421.3 12.3 %copy-start.32 = (f32[1024]{0:T(1024)S(1)}, f32[1024]{0:T(1024)}, u32[]{:S(2)}) copy-start(f32[1024]{0:T(1024)} %copy-done.31) | copy-start | bytes 12292
  421.3 58.9 %collective-permute-start.19 = (bf16[4,256,2048]{1,2,0:T(8,128)(2,1)}, bf16[4,256,2048]{1,2,0:T(8,128)(2,1)}, u32[]{:S(2)}, u32[]{:S(2)}) collective-permute-start(bf16[4,256,2048]{1,2,0:T(8,128)(2,1)} %bitcast.115), channel_id=1, source_target_pairs={{0,4},{4,0},{8,12},{12,8},{16,20},{20,16},{24,28},{28,24},{1,5},{5... | collective-permute-start | bytes 12582920 | tf_op jit(solution)/shard_map/ppermute | solution.py:243
  433.6 11.9 %copy-start.13 = (f32[1024,2048]{1,0:T(8,128)S(1)}, f32[1024,2048]{1,0:T(8,128)}, u32[]{:S(2)}) copy-start(f32[1024,2048]{1,0:T(8,128)} %fusion.25) | copy-start | bytes 25165828
  466.0 150.4 %collective-permute-start.5 = (bf16[256,2048]{1,0:T(8,128)(2,1)}, bf16[256,2048]{1,0:T(8,128)(2,1)}, u32[]{:S(2)}, u32[]{:S(2)}) collective-permute-start(bf16[256,2048]{1,0:T(8,128)(2,1)} %get-tuple-element.103), channel_id=1, source_target_pairs={{0,3},{1,2},{2,1},{3,0},{4,7},{5,6},{6,5},{7,4},{8,11},{9,10},{10,... | collective-permute-start | bytes 3145736 | tf_op jit(solution)/shard_map/ppermute | solution.py:289
  473.0 13.9 %copy-start.10 = (bf16[4,256,2048]{1,2,0:T(8,128)(2,1)}, bf16[4,256,2048]{1,2,0:T(8,128)(2,1)S(1)}, u32[]{:S(2)}) copy-start(bf16[4,256,2048]{1,2,0:T(8,128)(2,1)S(1)} %fusion.1) | copy-start | bytes 12582916
  474.2 144.2 %collective-permute-start.4 = (bf16[256,2048]{1,0:T(8,128)(2,1)}, bf16[256,2048]{1,0:T(8,128)(2,1)}, u32[]{:S(2)}, u32[]{:S(2)}) collective-permute-start(bf16[256,2048]{1,0:T(8,128)(2,1)} %get-tuple-element.104), channel_id=1, source_target_pairs={{0,2},{1,3},{2,0},{3,1},{4,6},{5,7},{6,4},{7,5},{8,10},{9,11},{10,... | collective-permute-start | bytes 3145736 | tf_op jit(solution)/shard_map/ppermute | solution.py:289
  474.6 12.2 %collective-permute-start.13 = (bf16[256,2048]{0,1:T(8,128)(2,1)S(1)}, bf16[256,2048]{0,1:T(8,128)(2,1)S(1)}, u32[]{:S(2)}, u32[]{:S(2)}) collective-permute-start(bf16[256,2048]{0,1:T(8,128)(2,1)S(1)} %get-tuple-element.97), channel_id=1, source_target_pairs={{0,8},{4,12},{1,9},{5,13},{2,10},{6,14},{3,11},{7,15}} | collective-permute-start | bytes 3145736 | tf_op jit(solution)/shard_map/ppermute | solution.py:258
  478.9 87.9 %collective-permute-start.16 = (bf16[256,2048]{0,1:T(8,128)(2,1)}, bf16[256,2048]{0,1:T(8,128)(2,1)}, u32[]{:S(2)}, u32[]{:S(2)}) collective-permute-start(bf16[256,2048]{0,1:T(8,128)(2,1)} %get-tuple-element.98), channel_id=1, source_target_pairs={{28,20},{24,16},{29,21},{25,17},{30,22},{26,18},{31,23},{27,19}} | collective-permute-start | bytes 3145736 | tf_op jit(solution)/shard_map/ppermute | solution.py:259
  485.0 17.8 %copy-start.27 = (bf16[8,256]{1,0:T(8,128)(2,1)S(1)}, bf16[8,256]{1,0:T(8,128)(2,1)}, u32[]{:S(2)}) copy-start(bf16[8,256]{1,0:T(8,128)(2,1)} %reshape.268) | copy-start | bytes 12292
  485.0 77.7 %collective-permute-start.20 = (bf16[256,2048]{0,1:T(8,128)(2,1)}, bf16[256,2048]{0,1:T(8,128)(2,1)}, u32[]{:S(2)}, u32[]{:S(2)}) collective-permute-start(bf16[256,2048]{0,1:T(8,128)(2,1)} %get-tuple-element.93), channel_id=1, source_target_pairs={{0,8},{4,12},{1,9},{5,13},{2,10},{6,14},{3,11},{7,15}} | collective-permute-start | bytes 3145736 | tf_op jit(solution)/shard_map/ppermute | solution.py:258
  488.1 80.0 %collective-permute-start.14 = (bf16[256,2048]{0,1:T(8,128)(2,1)}, bf16[256,2048]{0,1:T(8,128)(2,1)}, u32[]{:S(2)}, u32[]{:S(2)}) collective-permute-start(bf16[256,2048]{0,1:T(8,128)(2,1)} %fusion.80), channel_id=1, source_target_pairs={{0,8},{4,12},{8,16},{12,20},{1,9},{5,13},{9,17},{13,21},{2,10},{6,... | collective-permute-start | bytes 3145736 | tf_op jit(solution)/shard_map/ppermute | solution.py:258
  562.7 29.1 %collective-permute-start.23 = (bf16[256,2048]{0,1:T(8,128)(2,1)}, bf16[256,2048]{0,1:T(8,128)(2,1)}, u32[]{:S(2)}, u32[]{:S(2)}) collective-permute-start(bf16[256,2048]{0,1:T(8,128)(2,1)} %get-tuple-element.94), channel_id=1, source_target_pairs={{28,20},{24,16},{29,21},{25,17},{30,22},{26,18},{31,23},{27,19}} | collective-permute-start | bytes 3145736 | tf_op jit(solution)/shard_map/ppermute | solution.py:259
  566.8 25.0 %collective-permute-start.21 = (bf16[256,2048]{0,1:T(8,128)(2,1)}, bf16[256,2048]{0,1:T(8,128)(2,1)}, u32[]{:S(2)}, u32[]{:S(2)}) collective-permute-start(bf16[256,2048]{0,1:T(8,128)(2,1)} %fusion.75), channel_id=1, source_target_pairs={{0,8},{4,12},{8,16},{12,20},{1,9},{5,13},{9,17},{13,21},{2,10},{6,... | collective-permute-start | bytes 3145736 | tf_op jit(solution)/shard_map/ppermute | solution.py:258
  572.2 40.8 %collective-permute-start.17 = (bf16[256,2048]{0,1:T(8,128)(2,1)}, bf16[256,2048]{0,1:T(8,128)(2,1)}, u32[]{:S(2)}, u32[]{:S(2)}) collective-permute-start(bf16[256,2048]{0,1:T(8,128)(2,1)} %get-tuple-element.96), channel_id=1, source_target_pairs={{28,20},{24,16},{20,12},{16,8},{29,21},{25,17},{21,13},{17,9},{30,... | collective-permute-start | bytes 3145736 | tf_op jit(solution)/shard_map/ppermute | solution.py:259
  579.7 35.1 %copy-start.11 = (bf16[4,256,2048]{1,2,0:T(8,128)(2,1)S(1)}, bf16[4,256,2048]{1,2,0:T(8,128)(2,1)}, u32[]{:S(2)}) copy-start(bf16[4,256,2048]{1,2,0:T(8,128)(2,1)} %copy-done.10) | copy-start | bytes 12582916
  580.3 115.0 %copy-start.33 = (f32[1,256]{1,0:T(1,128)}, f32[1,256]{1,0:T(1,128)S(1)}, u32[]{:S(2)}) copy-start(f32[1,256]{1,0:T(1,128)S(1)} %get-tuple-element.142) | copy-start | bytes 3076
  591.8 26.6 %collective-permute-start.3 = (bf16[256,2048]{1,0:T(8,128)(2,1)}, bf16[256,2048]{1,0:T(8,128)(2,1)S(1)}, u32[]{:S(2)}, u32[]{:S(2)}) collective-permute-start(bf16[256,2048]{1,0:T(8,128)(2,1)} %get-tuple-element.102), channel_id=1, source_target_pairs={{0,1},{1,0},{2,3},{3,2},{4,5},{5,4},{6,7},{7,6},{8,9},{9,8},{10,11... | collective-permute-start | bytes 3145736 | tf_op jit(solution)/shard_map/ppermute | solution.py:289
  591.8 26.6 %copy-start.24 = (f32[1,2,8,128]{3,1,2,0:T(2,128)S(1)}, f32[1,2,8,128]{3,1,2,0:T(2,128)}, u32[]{:S(2)}) copy-start(f32[1,2,8,128]{3,1,2,0:T(2,128)} %copy.164) | copy-start | bytes 24580
  591.8 26.6 %copy-start.38 = (pred[256]{0:T(512)(128)(4,1)S(1)}, pred[256]{0:T(512)(128)(4,1)}, u32[]{:S(2)}) copy-start(pred[256]{0:T(512)(128)(4,1)} %copy-done.37) | copy-start | bytes 772
  591.8 53.0 %collective-permute-start.15 = (bf16[256,2048]{0,1:T(8,128)(2,1)}, bf16[256,2048]{0,1:T(8,128)(2,1)S(1)}, u32[]{:S(2)}, u32[]{:S(2)}) collective-permute-start(bf16[256,2048]{0,1:T(8,128)(2,1)} %get-tuple-element.95), channel_id=1, source_target_pairs={{0,8},{4,12},{8,16},{12,20},{16,24},{20,28},{1,9},{5,13},{9,17},{1... | collective-permute-start | bytes 3145736 | tf_op jit(solution)/shard_map/ppermute | solution.py:258
  613.0 27.2 %collective-permute-start.24 = (bf16[256,2048]{0,1:T(8,128)(2,1)S(1)}, bf16[256,2048]{0,1:T(8,128)(2,1)S(1)}, u32[]{:S(2)}, u32[]{:S(2)}) collective-permute-start(bf16[256,2048]{0,1:T(8,128)(2,1)S(1)} %get-tuple-element.92), channel_id=1, source_target_pairs={{28,20},{24,16},{20,12},{16,8},{29,21},{25,17},{21,13},{17,9},{30,... | collective-permute-start | bytes 3145736 | tf_op jit(solution)/shard_map/ppermute | solution.py:259
  616.5 46.2 %collective-permute-start.18 = (bf16[256,2048]{0,1:T(8,128)(2,1)S(1)}, bf16[256,2048]{0,1:T(8,128)(2,1)S(1)}, u32[]{:S(2)}, u32[]{:S(2)}) collective-permute-start(bf16[256,2048]{0,1:T(8,128)(2,1)S(1)} %fusion.79), channel_id=1, source_target_pairs={{28,20},{24,16},{20,12},{16,8},{12,4},{8,0},{29,21},{25,17},{21,13... | collective-permute-start | bytes 3145736 | tf_op jit(solution)/shard_map/ppermute | solution.py:259
  623.1 45.5 %collective-permute-start.22 = (bf16[256,2048]{0,1:T(8,128)(2,1)}, bf16[256,2048]{0,1:T(8,128)(2,1)}, u32[]{:S(2)}, u32[]{:S(2)}) collective-permute-start(bf16[256,2048]{0,1:T(8,128)(2,1)} %get-tuple-element.91), channel_id=1, source_target_pairs={{0,8},{4,12},{8,16},{12,20},{16,24},{20,28},{1,9},{5,13},{9,17},{1... | collective-permute-start | bytes 3145736 | tf_op jit(solution)/shard_map/ppermute | solution.py:258
  642.6 42.0 %collective-permute-start.25 = (bf16[256,2048]{0,1:T(8,128)(2,1)}, bf16[256,2048]{0,1:T(8,128)(2,1)}, u32[]{:S(2)}, u32[]{:S(2)}) collective-permute-start(bf16[256,2048]{0,1:T(8,128)(2,1)} %fusion.74), channel_id=1, source_target_pairs={{28,20},{24,16},{20,12},{16,8},{12,4},{8,0},{29,21},{25,17},{21,13... | collective-permute-start | bytes 3145736 | tf_op jit(solution)/shard_map/ppermute | solution.py:259
  (34 other events, 190.6 us)
Sparse Core Ops, SparseCore 0:
  12.9 84.2 all-gather.4
  98.7 81.2 all-gather.6
  182.2 80.6 all-gather.8
  366.7 85.8 reduce-scatter.1

commit v2 on v1

--- a/solution.py
+++ b/solution.py
@@ -11,9 +11,7 @@
 ROT = 32
 LANES = 128
 QBLOCK = 256
-MLP_PARTS = (1, 1)
-ATTN_RS = "line"
-MLP_RS = ("sc", "line")
+MLP_PARTS = (9, 7)
 
 norm_eps = 1e-05
 masked_score = -1000000000.0
@@ -231,63 +229,341 @@
     return [(i, i ^ flip) for i in range(count)]
 
 
-def line_scatter(grad, places):
+def bits_below(count):
+    return [1 << b for b in range(count.bit_length() - 1)]
+
+
+def norm_rows(rows):
+    center = rows - jnp.mean(rows, axis=-1, keepdims=True)
+    spread = jnp.mean(center * center, axis=-1, keepdims=True)
+    return center * lax.rsqrt(spread + norm_eps)
+
+
+def joined(pieces, low, high):
+    return jnp.concatenate([piece[low:high, :].astype(F32) for piece in pieces], axis=1)
+
+
+def norm_kernel(at_ref, *refs):
+    *pieces, gain_ref, shift_ref = refs[:-2]
+    out_ref = refs[-1]
+    rows = out_ref.shape[0]
+    for low in range(0, rows, 32):
+        part = norm_rows(joined(pieces, low, low + 32))
+        out_ref[low : low + 32, :] = (part * gain_ref[...] + shift_ref[...]).astype(BF16)
+
+
+def mask_kernel(at_ref, len_ref, *refs):
+    pieces = refs[:-2]
+    out_ref = refs[-1]
+    rows, width = out_ref.shape
+    pos = at_ref[0] * rows + lax.broadcasted_iota(jnp.int32, (rows, width), 0)
+    whole = jnp.concatenate([piece[...] for piece in pieces], axis=1)
+    out_ref[...] = jnp.where(pos < len_ref[0], whole, jnp.zeros_like(whole))
+
+
+def place_rows(kernel, name, seq_rows, pieces, extra, scalars, buffer):
+    tok_rows = pieces[0].shape[0]
+    width = sum(piece.shape[1] for piece in pieces)
+    count = len(scalars)
+    whole = lambda item: pl.BlockSpec(item.shape, lambda i, *s: (0, 0))
+    last = [] if buffer is None else [buffer]
+    operands = list(pieces) + list(extra) + (last or [extra[0] if extra else pieces[0]])
+    specs = [whole(item) for item in list(pieces) + list(extra)] + [pl.BlockSpec(memory_space=pl.ANY)]
+    return pl.pallas_call(
+        kernel,
+        grid_spec=pltpu.PrefetchScalarGridSpec(
+            num_scalar_prefetch=count,
+            grid=(1,),
+            in_specs=specs,
+            out_specs=pl.BlockSpec((tok_rows, width), lambda i, at, *s: (at[0], 0)),
+        ),
+        out_shape=jax.ShapeDtypeStruct((seq_rows, width), BF16),
+        input_output_aliases={count + len(operands) - 1: 0} if last else {},
+        name=name,
+    )(*scalars, *operands)
+
+
+def sums_kernel(counts, at_ref, *refs):
+    parts, (grad_ref, out_ref, gain_acc, shift_acc) = list(refs[:-4]), refs[-4:]
+    rows = parts[0].shape[0]
+    gain_acc[...] = jnp.zeros_like(gain_acc)
+    shift_acc[...] = jnp.zeros_like(shift_acc)
+    step = gain_acc.shape[0]
+    for flip, count in enumerate(counts):
+        pieces = [parts.pop(0) for _ in range(count)]
+        base = pl.multiple_of((at_ref[0] ^ flip) * rows, rows)
+        for low in range(0, rows, step):
+            grad = grad_ref[pl.ds(base + low, step), :].astype(F32)
+            gain_acc[...] += grad * norm_rows(joined(pieces, low, low + step))
+            shift_acc[...] += grad
+    out_ref[0:1, :] = jnp.sum(gain_acc[...], axis=0, keepdims=True)
+    out_ref[1:2, :] = jnp.sum(shift_acc[...], axis=0, keepdims=True)
+
+
+def norm_sums(tensor, parts, grad):
+    width = grad.shape[1]
+    pieces = [piece for part in parts for piece in part]
+    vmem = pl.BlockSpec(memory_space=pltpu.VMEM)
+    return pl.pallas_call(
+        functools.partial(sums_kernel, [len(part) for part in parts]),
+        in_specs=[pl.BlockSpec(memory_space=pltpu.SMEM)] + [vmem] * (len(pieces) + 1),
+        out_specs=vmem,
+        out_shape=jax.ShapeDtypeStruct((2, width), F32),
+        scratch_shapes=[pltpu.VMEM((32, width), F32), pltpu.VMEM((32, width), F32)],
+        compiler_params=pltpu.CompilerParams(vmem_limit_bytes=32 * 1024 * 1024),
+        cost_estimate=pl.CostEstimate(flops=16 * grad.size, bytes_accessed=4 * grad.size, transcendentals=0),
+        name="norm_sums",
+    )(tensor, *pieces, grad)
+
+
+def weight_kernel(at_ref, left_a, right_a, left_b, right_b, out_ref):
+    width = right_a.shape[1]
+    out_ref[:, :width] = inner_rows(left_a[...], right_a[...]).astype(BF16)
+    out_ref[:, width:] = inner_rows(left_b[...], right_b[...]).astype(BF16)
+
+
+def weight_grads(left_a, right_a, left_b, right_b, first, stride, blocks, rows):
+    seq = left_a.shape[0]
+    width = right_a.shape[1] + right_b.shape[1]
+    block = pl.BlockSpec((seq, rows), lambda i, at: (0, stride * i + at[0]))
+    whole = lambda item: pl.BlockSpec(item.shape, lambda i, at: (0, 0))
+    return pl.pallas_call(
+        weight_kernel,
+        grid_spec=pltpu.PrefetchScalarGridSpec(
+            num_scalar_prefetch=1,
+            grid=(blocks,),
+            in_specs=[block, whole(right_a), block, whole(right_b)],
+            out_specs=pl.BlockSpec((rows, width), lambda i, at: (i, 0)),
+        ),
+        out_shape=jax.ShapeDtypeStruct((blocks * rows, width), BF16),
+        compiler_params=pltpu.CompilerParams(vmem_limit_bytes=32 * 1024 * 1024),
+        cost_estimate=pl.CostEstimate(
+            flops=2 * seq * blocks * rows * width,
+            bytes_accessed=2 * seq * (width + 2 * blocks * rows) + 2 * blocks * rows * width,
+            transcendentals=0,
+        ),
+        name="weight_grads",
+    )(first, left_a, right_a, left_b, right_b)
+
+
+def tie(*values):
+    return lax.optimization_barrier(values)
+
+
+class LineScatter:
+    def __init__(self, left_a, right_a, left_b, right_b):
+        self.size = lax.axis_size("dp")
+        self.stations = self.size // 2
+        me = lax.axis_index("dp")
+        self.core, self.place = me % 2, me // 2
+        self.rows = left_a.shape[1] // self.size
+        self.other = weight_grads(
+            left_a, right_a, left_b, right_b, (1 - self.core)[None], 2, self.stations, self.rows
+        )
+        self.step = 0
+
+    def finish_pair(self, left_a, right_a, left_b, right_b):
+        self.mine = weight_grads(
+            left_a, right_a, left_b, right_b, self.core[None], 2, self.stations, self.rows
+        )
+        self.held = (lax.ppermute(self.other, "dp", swap_pairs(self.size, 1)),)
+
+    def at(self, target):
+        target = jnp.clip(target, 0, self.stations - 1)
+        pick = lambda item: lax.dynamic_slice_in_dim(item, target * self.rows, self.rows, 0).astype(F32)
+        return pick(self.mine) + pick(self.got)
+
+    def next_sends(self):
+        if self.step == 0:
+            (self.got,) = self.held
+            self.held = (None, None)
+        self.step += 1
+        if self.step >= self.stations:
+            up, down = self.held
+            self.total = self.at(self.place) + up.astype(F32) + down.astype(F32)
+            return ()
+        up, down = self.held if len(self.held) == 2 else self.held * 2
+        above = self.place + self.stations - self.step
+        below = self.place - self.stations + self.step
+        add = lambda sent, item: (sent if item is None else sent + item.astype(F32)).astype(BF16)
+        if 2 * self.step < self.stations - 1:
+            near = 2 * self.place < self.stations
+            sent = self.at(jnp.where(near, above, below))
+            return (add(sent, up),)
+        return add(self.at(above), up), add(self.at(below), down)
+
+    def send(self, sends):
+        to_up = [(2 * z + c, 2 * z + 2 + c) for z in range(self.step) for c in range(2)]
+        to_down = [(self.size - 1 - a, self.size - 1 - b) for a, b in to_up]
+        if len(sends) == 1:
+            self.held = (lax.ppermute(sends[0], "dp", to_up + to_down),)
+        else:
+            self.held = tuple(lax.ppermute(item, "dp", way) for item, way in zip(sends, (to_up, to_down)))
+
+    def done(self):
+        return self.step >= self.stations
+
+
+def weave_kernel(at_ref, mine_ref, got_ref, out_ref):
+    same = pl.program_id(0) % 2 == at_ref[1]
+
+    @pl.when(same)
+    def _():
+        out_ref[...] = mine_ref[...]
+
+    @pl.when(jnp.logical_not(same))
+    def _():
+        out_ref[...] = got_ref[...]
+
+
+class LineGather:
+    def __init__(self, pack):
+        self.size = lax.axis_size("dp")
+        self.stations = self.size // 2
+        me = lax.axis_index("dp")
+        self.core, self.place = me % 2, me // 2
+        self.pack = pack
+        self.step = 1
+        self.came = []
+        self.send((pack, pack))
+
+    def send(self, sends):
+        if self.step == self.stations:
+            self.held = (lax.ppermute(sends[0], "dp", swap_pairs(self.size, 1)),)
+            return
+        to_up = [(2 * z + c, 2 * z + 2 + c) for z in range(self.step - 1, self.stations - 1) for c in range(2)]
+        to_down = [(self.size - 1 - a, self.size - 1 - b) for a, b in to_up]
+        if len(sends) == 1:
+            self.held = (lax.ppermute(sends[0], "dp", to_up + to_down),)
+        else:
+            self.held = tuple(lax.ppermute(item, "dp", way) for item, way in zip(sends, (to_up, to_down)))
+
+    def next_sends(self):
+        self.step += 1
+        if self.step == self.stations + 1:
+            self.full = self.weave(self.stack, self.held[0])
+            return ()
+        up, down = self.held if len(self.held) == 2 else self.held * 2
+        self.came.append((up, down))
+        if self.step == self.stations:
+            parts = [self.pack]
+            for far in range(1, self.stations):
+                ahead = self.place + far < self.stations
+                parts.append(jnp.where(ahead, self.came[far - 1][1], self.came[self.stations - far - 1][0]))
+            self.stack = jnp.concatenate(parts)
+            return (self.stack,)
+        if 2 * self.step > self.stations + 1:
+            return (jnp.where(2 * self.place >= self.stations, up, down),)
+        return up, down
+
+    def weave(self, mine, got):
+        rows, width = self.pack.shape
+        stations = self.stations
+        half = pl.BlockSpec((rows, width), lambda i, at: ((i // 2 + stations - at[0]) % stations, 0))
+        return pl.pallas_call(
+            weave_kernel,
+            grid_spec=pltpu.PrefetchScalarGridSpec(
+                num_scalar_prefetch=1,
+                grid=(self.size,),
+                in_specs=[half, half],
+                out_specs=pl.BlockSpec((rows, width), lambda i, at: (i, 0)),
+            ),
+            out_shape=jax.ShapeDtypeStruct((self.size * rows, width), BF16),
+            cost_estimate=pl.CostEstimate(
+                flops=0, bytes_accessed=6 * self.size * rows * width, transcendentals=0
+            ),
+            name="weave",
+        )(jnp.stack([self.place, self.core]).astype(jnp.int32), mine, got)
+
+    def done(self):
+        return self.step > self.stations
+
+
+def advance(lines, *values):
+    lines = [line for line in lines if not line.done()]
+    flat = tie(*[item for line in lines for item in line.held], *values)
+    for line in lines:
+        line.held, flat = flat[: len(line.held)], flat[len(line.held) :]
+    sends = [line.next_sends() for line in lines]
+    flat = tie(*[item for sent in sends for item in sent], *flat)
+    for line, sent in zip(lines, sends):
+        if sent:
+            line.send(flat[: len(sent)])
+            flat = flat[len(sent) :]
+    return flat
+
+
+def natural_grads(left_a, right_a, left_b, right_b):
     size = lax.axis_size("dp")
-    stations = size // 2
-    me = lax.axis_index("dp")
-    core, place = me % 2, me // 2
-    rows = grad.shape[0] // size
-    stack = grad.reshape(stations, 2, rows, grad.shape[1])
-    mine = lax.dynamic_index_in_dim(stack, core, 1, keepdims=False)
-    other = lax.dynamic_index_in_dim(stack, 1 - core, 1, keepdims=False)
-    got = lax.ppermute(other, "dp", swap_pairs(size, 1))
-    pair = (mine.astype(F32) + got.astype(F32)).astype(BF16)
-
-    def at(target):
-        return lax.dynamic_index_in_dim(pair, jnp.clip(target, 0, stations - 1), 0, keepdims=False)
-
-    up = down = None
-    for step in range(1, stations):
-        send_up = at(place + stations - step)
-        send_down = at(place - stations + step)
-        if step > 1:
-            send_up = (send_up.astype(F32) + up.astype(F32)).astype(BF16)
-            send_down = (send_down.astype(F32) + down.astype(F32)).astype(BF16)
-        up_pairs = [(2 * z + c, 2 * z + 2 + c) for z in range(step) for c in range(2)]
-        down_pairs = [(size - 1 - a, size - 1 - b) for a, b in up_pairs]
-        up = lax.ppermute(send_up, "dp", up_pairs)
-        down = lax.ppermute(send_down, "dp", down_pairs)
-    return at(place).astype(F32) + up.astype(F32) + down.astype(F32)
-
-
-def scatter(grad, how):
-    if how == "line":
-        return line_scatter(grad, None)
-    return lax.psum_scatter(grad, "dp", scatter_dimension=0, tiled=True).astype(F32)
-
-
-def gather_rows(parts, seq_rows):
-    tensor = lax.axis_index("tensor")
-    tok_rows, width = parts[0].shape
-    whole = jnp.zeros((seq_rows, width), parts[0].dtype)
-    for flip, part in enumerate(parts):
-        whole = lax.dynamic_update_slice_in_dim(whole, part, (tensor ^ flip) * tok_rows, 0)
-    return whole
-
-
-def tensor_scatter(partial, tok_rows):
-    count = lax.axis_size("tensor")
-    tensor = lax.axis_index("tensor")
-
-    def block(flip):
-        return lax.dynamic_slice_in_dim(partial, (tensor ^ flip) * tok_rows, tok_rows, 0)
-
-    total = block(0)
-    low = partial.astype(BF16)
-    for flip in range(1, count):
-        sent = lax.dynamic_slice_in_dim(low, (tensor ^ flip) * tok_rows, tok_rows, 0)
-        total = total + lax.ppermute(sent, "tensor", swap_pairs(count, flip)).astype(F32)
-    return total
+    zero = jnp.zeros((1,), jnp.int32)
+    return weight_grads(left_a, right_a, left_b, right_b, zero, 1, size, left_a.shape[1] // size)
+
+
+class TensorScatter:
+    def __init__(self, partial, tok_rows):
+        self.count = lax.axis_size("tensor")
+        tensor = lax.axis_index("tensor")
+        half = partial.shape[1] // 2
+
+        def block(flip, side):
+            start = ((tensor ^ flip) * tok_rows, side * half)
+            return lax.dynamic_slice(partial, start, (tok_rows, half))
+
+        self.block, self.tok_rows = block, tok_rows
+        self.rest = []
+        if self.count > 4:
+            self.rest = [
+                lax.ppermute(block(flip, side), "tensor", swap_pairs(self.count, flip))
+                for side in (0, 1)
+                for flip in range(1, self.count)
+            ]
+            return
+        self.first = []
+        for side, flip in ((0, 1), (1, 2)):
+            sent = jnp.concatenate([block(flip, side), block(3, side)])
+            self.first.append(lax.ppermute(sent, "tensor", swap_pairs(self.count, flip)))
+
+    def second(self, *values):
+        if self.count > 4:
+            return values
+        self.total = []
+        flat = tie(*self.first, *values)
+        self.first, values = flat[:2], flat[2:]
+        for side, flip in ((0, 1), (1, 2)):
+            got = self.first[side].astype(F32)
+            far = (self.block(3 - flip, side).astype(F32) + got[self.tok_rows :]).astype(BF16)
+            near = self.block(0, side).astype(F32) + got[: self.tok_rows]
+            self.total.append((near, lax.ppermute(far, "tensor", swap_pairs(self.count, 3 - flip))))
+        return values
+
+    def result(self, *values):
+        if self.count > 4:
+            flat = tie(*self.rest, *values)
+            many = self.count - 1
+            total = [
+                sum((item.astype(F32) for item in flat[side * many : (side + 1) * many]), self.block(0, side).astype(F32))
+                for side in (0, 1)
+            ]
+            return (jnp.concatenate(total, axis=1),) + flat[2 * many :]
+        flat = tie(*[item for _, item in self.total], *values)
+        total = [near + item.astype(F32) for (near, _), item in zip(self.total, flat)]
+        return (jnp.concatenate(total, axis=1),) + flat[2:]
+
+
+def all_sum(value, axis):
+    count = lax.axis_size(axis)
+    for bit in bits_below(count):
+        value = value + lax.ppermute(value, axis, swap_pairs(count, bit))
+    return value
+
+
+def gelu_pair(value):
+    slope = (2.0 / jnp.pi) ** 0.5
+    square = value * value
+    flat = jnp.tanh(slope * value * (1.0 + 0.044715 * square))
+    act = 0.5 * value * (1.0 + flat)
+    back = 0.5 * (1.0 + flat) + 0.5 * value * (1.0 - flat * flat) * slope * (1.0 + 3 * 0.044715 * square)
+    return act.astype(BF16), back.astype(BF16)
 
 
 def on_device(
@@ -310,6 +586,7 @@
     tensor_count = lax.axis_size("tensor")
     dp_count = lax.axis_size("dp")
     tensor = lax.axis_index("tensor")
+    place = lax.axis_index("dp")
     tok_rows, width = tokens.shape
     seq_rows = tok_rows * tensor_count
     heads_width = query_weight.shape[1]
@@ -317,33 +594,12 @@
     pairs = heads_width // LANES
     slot_len = lengths[0]
 
-    attn_in = jnp.concatenate(
-        [
-            item[:, p * LANES : (p + 1) * LANES]
-            for p in range(pairs)
-            for item in (query_weight, key_weight, value_weight)
-        ],
-        axis=1,
-    )
-    attn_pack = jnp.concatenate([attn_in, proj_weight.T], axis=1)
-    attn_full = lax.all_gather(attn_pack, "dp", axis=0, tiled=True)
-    down_t = down_weight.T
-    weight_sum = sum(MLP_PARTS)
-    edges = [0]
-    for part in MLP_PARTS:
-        edges.append(edges[-1] + ff * part // weight_sum)
-    mlp_full = []
-    for low, high in zip(edges[:-1], edges[1:]):
-        pack = jnp.concatenate([up_weight[:, low:high], down_t[:, low:high]], axis=1)
-        mlp_full.append(lax.all_gather(pack, "dp", axis=0, tiled=True))
-
     small = jnp.concatenate(
         [norm_gain, norm_bias, proj_bias, down_bias, qkv_bias.reshape(-1), up_bias.reshape(-1)]
     )
-    small_all = lax.all_gather(small, "dp", axis=0, tiled=False)
+    mine_row = (jnp.arange(dp_count) == place)[:, None]
+    small_all = all_sum(jnp.where(mine_row, small[None, :], jnp.zeros((), BF16)), "dp")
     shard = norm_gain.shape[0]
-    n_gain = small_all[:, :shard].reshape(-1).astype(F32)
-    n_shift = small_all[:, shard : 2 * shard].reshape(-1).astype(F32)
     b_out = (
         small_all[:, 2 * shard : 3 * shard].astype(F32) + small_all[:, 3 * shard : 4 * shard].astype(F32)
     ).reshape(-1)
@@ -364,20 +620,65 @@
         .astype(F32)
     )
 
-    tok_parts = [tokens] + [
-        lax.ppermute(tokens, "tensor", swap_pairs(tensor_count, flip)) for flip in range(1, tensor_count)
+    down_t = down_weight.T
+    weight_sum = sum(MLP_PARTS)
+    edges = [0]
+    for part in MLP_PARTS:
+        edges.append(edges[-1] + ff * part // weight_sum)
+
+    def mlp_pack(index):
+        low, high = edges[index], edges[index + 1]
+        return jnp.concatenate([up_weight[:, low:high], down_t[:, low:high]], axis=1)
+
+    attn_in = [
+        item[:, p * LANES : (p + 1) * LANES]
+        for p in range(pairs)
+        for item in (query_weight, key_weight, value_weight)
     ]
-    grad_parts = [cotangent] + [
-        lax.ppermute(cotangent, "tensor", swap_pairs(tensor_count, flip)) for flip in range(1, tensor_count)
-    ]
-    normed_parts = [layer_norm(part.astype(F32), n_gain, n_shift).astype(BF16) for part in tok_parts]
-    normed = gather_rows(normed_parts, seq_rows)
-
-    def masked(part, flip):
-        pos = (tensor ^ flip) * tok_rows + jnp.arange(tok_rows)
-        return jnp.where((pos < slot_len)[:, None], part, jnp.zeros_like(part))
-
-    grad_all = gather_rows([masked(part, flip) for flip, part in enumerate(grad_parts)], seq_rows)
+    attn_pack = jnp.concatenate(attn_in + [proj_weight.T], axis=1)
+    attn_full = lax.all_gather(attn_pack, "dp", axis=0, tiled=True)
+    near_pack, far_pack = mlp_pack(0), mlp_pack(1)
+
+    half = width // 2
+
+    def direct(rows, flip):
+        return lax.ppermute(rows, "tensor", swap_pairs(tensor_count, flip))
+
+    def third(first, second):
+        return [direct(first[:, :half], 2), direct(second[:, half:], 1)]
+
+    tok_one, tok_two, small_all = tie(direct(tokens, 1), direct(tokens, 2), small_all)
+    tok_one, near_pack = tie(tok_one, near_pack)
+    near_full = lax.all_gather(near_pack, "dp", axis=0, tiled=True)
+    tok_three = third(tok_one, tok_two)
+    cot_held, tok_one, tok_two = tie(cotangent, tok_one, tok_two)
+    cot_one, cot_two = direct(cot_held, 1), direct(cot_held, 2)
+    more = range(4, tensor_count)
+    tok_more = [[direct(tokens, flip)] for flip in more]
+
+    n_gain = small_all[:, :shard].reshape(-1).astype(F32)
+    n_shift = small_all[:, shard : 2 * shard].reshape(-1).astype(F32)
+
+    def where_of(flip):
+        return (tensor ^ flip).astype(jnp.int32)[None]
+
+    gain_row, shift_row = n_gain[None, :], n_shift[None, :]
+    tok_parts = [[tokens], [tok_one], [tok_two], tok_three] + tok_more
+    normed = None
+    for flip in range(tensor_count):
+        if flip == 3:
+            normed, cot_one, cot_two = tie(normed, cot_one, cot_two)
+            cot_three = third(cot_one, cot_two)
+        normed = place_rows(
+            norm_kernel, "norm_rows", seq_rows, tok_parts[flip], [gain_row, shift_row], [where_of(flip)], normed
+        )
+    cot_parts = [[cotangent], [cot_one], [cot_two], cot_three] + [[direct(cot_held, flip)] for flip in more]
+    grad_all = None
+    for flip in range(tensor_count):
+        grad_all = place_rows(
+            mask_kernel, "mask_rows", seq_rows, cot_parts[flip], [], [where_of(flip), lengths], grad_all
+        )
+    normed, grad_all, far_pack = tie(normed, grad_all, far_pack)
 
     tables = rotary_lanes(seq_rows)
     in_cols = 3 * heads_width
@@ -386,63 +687,90 @@
     qkv = product(normed, w_qkv) + b_qkv
     q_low, k_low, v_low, mixed, lse = attention_forward(lengths, qkv, tables)
     mixed_grad = product(grad_all, w_proj_t).astype(BF16)
-    proj_grad_t = inner_rows(grad_all, mixed).astype(BF16)
     qkv_grad = attention_backward(lengths, q_low, k_low, v_low, mixed_grad, lse, tables)
-    in_grad = inner_rows(normed, qkv_grad).astype(BF16)
-    attn_shard = scatter(jnp.concatenate([in_grad, proj_grad_t], axis=1), ATTN_RS)
-    branch = times_trans(mixed, w_proj_t)
-    normed_grad = times_trans(qkv_grad, w_qkv)
     head_bias_grad = jnp.sum(qkv_grad, axis=0, dtype=F32)
-
-    mlp_shards = []
-    up_bias_grads = []
-    for index, (low, high) in enumerate(zip(edges[:-1], edges[1:])):
-        units = high - low
-        w_up = mlp_full[index][:, :units]
-        w_down_t = mlp_full[index][:, units:]
-        up_pre = product(normed, w_up) + b_up[low:high]
-        act, gelu_back = jax.vjp(lambda value: jax.nn.gelu(value, approximate=True), up_pre)
-        act = act.astype(BF16)
-        up_pre_grad = gelu_back(product(grad_all, w_down_t))[0].astype(BF16)
-        down_grad_t = inner_rows(grad_all, act).astype(BF16)
-        up_grad = inner_rows(normed, up_pre_grad).astype(BF16)
-        mlp_shards.append(scatter(jnp.concatenate([up_grad, down_grad_t], axis=1), MLP_RS[index]))
-        up_bias_grads.append(jnp.sum(up_pre_grad, axis=0, dtype=F32))
-        normed_grad = normed_grad + times_trans(up_pre_grad, w_up)
-        branch = branch + times_trans(act, w_down_t)
-
+    attn_line = LineScatter(normed, qkv_grad, grad_all, mixed)
+    qkv_grad, mixed, attn_line.other = tie(qkv_grad, mixed, attn_line.other)
+    attn_line.finish_pair(normed, qkv_grad, grad_all, mixed)
+    far_pack, attn_line.mine = tie(far_pack, attn_line.mine)
+    gather = LineGather(far_pack)
+    near_full, normed, attn_line.mine = tie(near_full, normed, attn_line.mine)
+
+    def forward(full, low, high):
+        w_up, w_down_t = full[:, : high - low], full[:, high - low :]
+        act, back = tie(*gelu_pair(product(normed, w_up) + b_up[low:high]))
+        return w_up, w_down_t, act, back
+
+    def plus(total, left, right):
+        return (total.astype(F32) + times_trans(left, right)).astype(BF16)
+
+    near_up, near_down_t, near_act, back = forward(near_full, edges[0], edges[1])
+    near_grad = (product(grad_all, near_down_t) * back.astype(F32)).astype(BF16)
+    near_act, near_grad, grad_all = advance([attn_line, gather], near_act, near_grad, grad_all)
+    line = LineScatter(normed, near_grad, grad_all, near_act)
+    near_act, near_grad, line.other = tie(near_act, near_grad, line.other)
+    line.finish_pair(normed, near_grad, grad_all, near_act)
+    near_act, line.mine, mixed, qkv_grad = advance(
+        [attn_line, gather], near_act, line.mine, mixed, qkv_grad
+    )
+    branch = times_trans(mixed, w_proj_t).astype(BF16)
+    normed_grad = times_trans(qkv_grad, w_qkv).astype(BF16)
+    branch, normed_grad, near_act = advance([gather, line], branch, normed_grad, near_act)
+    branch = plus(branch, near_act, near_down_t)
+    lines = [attn_line, line]
+    branch, normed, grad_all, near_grad = advance([gather, attn_line], branch, normed, grad_all, near_grad)
+    while not gather.done():
+        normed, grad_all = advance([gather], normed, grad_all)
+    w_up, w_down_t, act, back = forward(gather.full, edges[1], edges[2])
+    up_pre_grad = (product(grad_all, w_down_t) * back.astype(F32)).astype(BF16)
+    far_grad = natural_grads(normed, up_pre_grad, grad_all, act)
+    far_grad, act, up_pre_grad, near_grad = advance(lines, far_grad, act, up_pre_grad, near_grad)
+    far_shard = lax.psum_scatter(far_grad, "dp", scatter_dimension=0, tiled=True)
+    branch_low = plus(branch, act, w_down_t)
+
+    output_sum = TensorScatter(branch_low, tok_rows)
+    near_grad, branch_low = tie(near_grad, branch_low)
+    normed_grad_low = plus(plus(normed_grad, near_grad, near_up), up_pre_grad, w_up)
+    (normed_grad_low,) = output_sum.second(normed_grad_low)
+    up_bias_grads = [jnp.sum(item, axis=0, dtype=F32) for item in (near_grad, up_pre_grad)]
+    grad_sum = TensorScatter(normed_grad_low, tok_rows)
+    gain_shift = norm_sums(tensor.astype(jnp.int32)[None], tok_parts, normed_grad_low)
+    (gain_shift,) = advance(lines, gain_shift)
+    (gain_shift,) = grad_sum.second(gain_shift)
     own = tokens.astype(F32)
-    output = (own + tensor_scatter(branch, tok_rows) + b_out).astype(BF16)
-    own_normed_grad = tensor_scatter(normed_grad, tok_rows)
-    _, norm_back = jax.vjp(layer_norm, own, n_gain, n_shift)
-    input_part, gain_part, shift_part = norm_back(own_normed_grad)
-    input_grad = masked(cotangent, 0).astype(F32) + input_part
-    gain_sum, shift_sum = lax.psum((gain_part, shift_part), "tensor")
-
-    head_part = (
-        head_bias_grad.reshape(pairs, 3, LANES)
+    (output_rows,) = output_sum.result()
+    output = (own + output_rows + b_out).astype(BF16)
+    own_pos = tensor * tok_rows + jnp.arange(tok_rows)
+    own_grad = jnp.where((own_pos < slot_len)[:, None], cotangent.astype(F32), 0.0)
+
+    shared = jnp.concatenate([gain_shift.reshape(-1), jnp.sum(own_grad, axis=0)])
+    kept = jnp.concatenate([head_bias_grad] + up_bias_grads)
+    summed = all_sum(jnp.concatenate([shared, kept]).reshape(-1, LANES), "dp")
+    many = shared.shape[0] // LANES
+    shared = summed[:many]
+    while not all(item.done() for item in lines):
+        (shared,) = advance(lines, shared)
+    shared = all_sum(shared, "tensor")
+    attn_shard = attn_line.total
+    mlp_shards = [line.total, far_shard.astype(F32)]
+    own_normed_grad, shared = grad_sum.result(shared)
+    _, norm_back = jax.vjp(lambda rows: layer_norm(rows, n_gain, n_shift), own)
+    input_grad = own_grad + norm_back(own_normed_grad)[0]
+    shared = shared.reshape(3, dp_count, shard)
+    gain_grad, shift_grad, out_bias = lax.dynamic_index_in_dim(shared, place, 1, keepdims=False)
+    kept = summed[many:].reshape(-1)
+    head_out = lax.dynamic_index_in_dim(
+        kept[: head_bias_grad.shape[0]]
+        .reshape(pairs, 3, LANES)
         .transpose(1, 0, 2)
-        .reshape(3, heads_here, dp_count, HEAD // dp_count)
-        .transpose(2, 0, 1, 3)
-        .reshape(dp_count, -1)
+        .reshape(3, heads_here, dp_count, HEAD // dp_count),
+        place,
+        2,
+        keepdims=False,
     )
-    up_part = (
-        jnp.concatenate(up_bias_grads)
-        .reshape(up_bias.shape[0], dp_count, -1)
-        .transpose(1, 0, 2)
-        .reshape(dp_count, -1)
+    up_bias_out = lax.dynamic_index_in_dim(
+        kept[head_bias_grad.shape[0] :].reshape(up_bias.shape[0], dp_count, -1), place, 1, keepdims=False
     )
-    out_bias_part = jnp.sum(grad_all, axis=0, dtype=F32).reshape(dp_count, shard)
-    small_grad = jnp.concatenate(
-        [gain_sum.reshape(dp_count, shard), shift_sum.reshape(dp_count, shard), out_bias_part, head_part, up_part],
-        axis=1,
-    ).astype(BF16)
-    small_out = lax.psum_scatter(small_grad, "dp", scatter_dimension=0, tiled=True)[0].astype(F32)
-    gain_grad = small_out[:shard]
-    shift_grad = small_out[shard : 2 * shard]
-    out_bias = small_out[2 * shard : 3 * shard]
-    head_out = small_out[3 * shard : 3 * shard + head_size].reshape(qkv_bias.shape)
-    up_bias_out = small_out[3 * shard + head_size :].reshape(up_bias.shape)
 
     def part_of(which):
         return jnp.concatenate(

time: 708 us -> 555 us (0.78)
  the two profiles are of different devices: /device:TPU:17 before, /device:TPU:0 now
where the time goes in v2:
time: 555 us; the launch traced here: 545 us
  Pallas kernels  118 us (21%)
  matrix products  102 us (18%)
  waiting for transfers between devices  100 us (18%)
  starting transfers between devices  78.2 us (14%)
  other arithmetic  71.4 us (13%)
  local copies, waits for them, and re-layouts  59.3 us (11%)
  between operations  16.3 us (3%)
    dot_general x6, matrix products, times_trans(): lax.dot_general(left, right, (((1,), (1,)), ((), ())), preferred_element_...  54.4 us
    ppermute x8, waiting for transfers between devices, all_sum(): value = value + lax.ppermute(value, axis, swap_pairs(count, bit))  48.5 us
    dot_general x6, matrix products, product(): return jnp.dot(left, right, preferred_element_type=F32)  47.8 us
    unnamed x180, local copies, waits for them, and re-layouts  39.5 us
    pallas_call x5, Pallas kernels, weight_grads(): pl.pallas_call(weight_kernel, grid_spec=pltpu.PrefetchScalarGridSpec(num_...  39 us
    ppermute x12, starting transfers between devices, send(): lax.ppermute(item, 'dp', way)  33.1 us
    pallas_call x1, Pallas kernels, attention_backward(): pl.pallas_call(attn_bwd_kernel, grid=(pairs,), in_specs=[pl.BlockSpec(mem...  26.6 us
    ppermute x12, waiting for transfers between devices, send(): lax.ppermute(item, 'dp', way)  25.6 us
  transfers between devices with their start and end apart: 45, of which 15 were waited for; matrix products, arithmetic and copies ran while one was open for 32% of the time, Pallas kernels for 20%

profile of v2, /device:TPU:0, one launch (start us, length us, event | category | flops | bytes accessed | tf_op | source)
XLA Modules:
  0.0 545.3 jit_solution(3393746366263476083)
XLA Ops:
  29.9 10.9 %collective-permute-done.4 = bf16[8,1472]{1,0:T(8,128)(2,1)S(1)} collective-permute-done((bf16[8,1472]{1,0:T(8,128)(2,1)S(1)}, bf16[8,1472]{1,0:T(8,128)(2,1)S(1)}, u32[]{:S(2)}, u32[]{:S(2)}) %collective-permute-start.4) | collective-permute-done | bytes 23584 | tf_op jit(solution)/shard_map/ppermute | solution.py:556
  51.5 3.0 norm_rows.4.refs_3_
  54.5 3.0 norm_rows.5.refs_3_
  57.5 3.0 norm_rows.6.refs_4_
  60.5 7.7 %collective-permute-done.8.refs_0_ = bf16[256,2048]{1,0:T(8,128)(2,1)} collective-permute-done((bf16[256,2048]{1,0:T(8,128)(2,1)}, bf16[256,2048]{1,0:T(8,128)(2,1)}, u32[]{:S(2)}, u32[]{:S(2)}) %collective-permute-start.8) | collective-permute-done | bytes 1048608 | tf_op jit(solution)/shard_map/ppermute | solution.py:645
  86.2 3.1 norm_rows.7.left_a
  92.5 8.2 %all-gather.5.cloned.1.call-done = bf16[2048,2048]{0,1:T(8,128)(2,1)} async-done(((bf16[256,2048]{0,1:T(8,128)(2,1)}), bf16[2048,2048]{0,1:T(8,128)(2,1)}) %all-gather.5.cloned.1.call-update) | async-done | bytes 8388624 | tf_op jit(solution)/shard_map/all_gather | solution.py:639
  100.7 11.9 %fusion.4.qkv_ref = f32[1024,1536]{1,0:T(8,128)} fusion(bf16[1024,2048]{1,0:T(8,128)(2,1)} %norm_rows.7.left_a, bf16[2048,2048]{0,1:T(8,128)(2,1)} %all-gather.5.cloned.1.call-done, f32[1536]{0:T(1024)S(1)} %reshape.185), kind=kOutput, calls=%fused_computation.15 | convolution fusion | flops 6444023808 | bytes 16783360 | tf_op jit(solution)/shard_map/dot_general | solution.py:29
  112.6 16.6 %attn_fwd.1 = (bf16[1024,512]{1,0:T(8,128)(2,1)S(1)}, bf16[1024,512]{1,0:T(8,128)(2,1)S(1)}, bf16[1024,512]{1,0:T(8,128)(2,1)S(1)}, bf16[1024,512]{1,0:T(8,128)(2,1)S(1)}, f32[1024,512]{1,0:T(8,128)}) custom-call(s32[1]{0:T(128)} %copy.135.len_ref, f32[1024,1536]{1,0:T(8,128)} %fusion.4.qkv_ref, f32[1024,128]{1,0:T(8,128)S(1)} %get-tuple-element.362.keep_ref, ...), custom_call_target="tpu_custom_call" | custom-call | flops 6442450944 | bytes 12582912 | tf_op jit(solution)/shard_map/attn_fwd/pallas_call | solution.py:189
  129.2 4.4 fusion.44.grad_ref
  133.6 26.6 %attn_bwd.1.right_a = bf16[1024,1536]{1,0:T(8,128)(2,1)} custom-call(s32[1]{0:T(128)} %copy.135.len_ref, bf16[1024,512]{1,0:T(8,128)(2,1)S(1)} %get-tuple-element.144.q_ref, bf16[1024,512]{1,0:T(8,128)(2,1)S(1)} %get-tuple-element.145.k_ref, bf16[1024,512]{1,0:T(8,128)(2,1)S(1)} %get-tuple-element.146.v_ref, bf16[1024,512]{1,0:T(8,128)(2,1)S(1)} %fusion.44.grad_ref, ...), custom_call_target="tpu_custom_call" | custom-call | flops 16106127360 | bytes 12582912 | tf_op jit(solution)/shard_map/attn_bwd/pallas_call | solution.py:211
  163.4 6.8 %weight_grads.5 = bf16[1024,2048]{1,0:T(8,128)(2,1)} custom-call(s32[1]{0:T(128)} %bitcast.9.at_ref, bf16[1024,2048]{1,0:T(8,128)(2,1)S(1)} %copy-done.5, bf16[1024,1536]{1,0:T(8,128)(2,1)S(1)} %copy-done.12, bf16[1024,2048]{1,0:T(8,128)(2,1)S(1)} %copy-done, bf16[1024,512]{1,0:T(8,128)(2,1)S(1)} %copy-done.25), custom_call_target="tpu_custom_call" | custom-call | flops 4294967296 | bytes 12582912 | tf_op jit(solution)/shard_map/weight_grads/pallas_call | solution.py:330
  176.5 5.8 %weight_grads.6 = bf16[1024,2048]{1,0:T(8,128)(2,1)S(1)} custom-call(s32[1]{0:T(128)} %bitcast.5.at_ref, bf16[1024,2048]{1,0:T(8,128)(2,1)S(1)} %copy-done.6, bf16[1024,1536]{1,0:T(8,128)(2,1)S(1)} %copy-done.13, bf16[1024,2048]{1,0:T(8,128)(2,1)S(1)} %copy-done.1, bf16[1024,512]{1,0:T(8,128)(2,1)S(1)} %copy-done.26), custom_call_target="tpu_custom_call" | custom-call | flops 4294967296 | bytes 12582912 | tf_op jit(solution)/shard_map/weight_grads/pallas_call | solution.py:330
  185.7 5.5 %collective-permute-start.12 = (bf16[256,1792]{1,0:T(8,128)(2,1)}, bf16[256,1792]{1,0:T(8,128)(2,1)}, u32[]{:S(2)}, u32[]{:S(2)}) collective-permute-start(bf16[256,1792]{1,0:T(8,128)(2,1)} %pad_maximum_fusion.8), channel_id=1, source_target_pairs={{0,8},{4,12},{8,16},{12,20},{16,24},{20,28},{1,9},{5,13},{9,17},{1... | collective-permute-start | bytes 2752520 | tf_op jit(solution)/shard_map/ppermute | solution.py:439
  193.3 11.5 %add_convert_fusion.4 = (bf16[1024,1152]{1,0:T(8,128)(2,1)S(1)}, bf16[1024,1152]{1,0:T(8,128)(2,1)S(1)}) fusion(f32[1152]{0:T(1024)S(1)} %slice.228, bf16[1024,2048]{1,0:T(8,128)(2,1)} %norm_rows.7.left_a, bf16[2048,2304]{1,0:T(8,128)(2,1)} %all-gather.3.cloned.1.call-done), kind=kOutput, calls=%fused_computation.11 | convolution fusion | flops 4855431168 | bytes 13636096 | tf_op jit(solution)/shard_map/dot_general | solution.py:29
  204.8 5.8 %fusion.13.right_a = bf16[1024,1152]{1,0:T(8,128)(2,1)S(1)} fusion(bf16[1024,1152]{1,0:T(8,128)(2,1)S(1)} %get-tuple-element.159, bf16[1024,2048]{1,0:T(8,128)(2,1)S(1)} %copy-done.2, bf16[2048,2304]{1,0:T(8,128)(2,1)S(1)} %copy-done.68), kind=kOutput, calls=%fused_computation.22 | convolution fusion | flops 4835377152 | bytes 13631488 | tf_op jit(solution)/shard_map/dot_general | solution.py:29
  210.7 3.7 add_convert_fusion.11
  214.4 7.9 %weight_grads.7 = bf16[1024,2304]{1,0:T(8,128)(2,1)} custom-call(s32[1]{0:T(128)} %bitcast.9.at_ref, bf16[1024,2048]{1,0:T(8,128)(2,1)S(1)} %copy-done.7, bf16[1024,1152]{1,0:T(8,128)(2,1)S(1)} %fusion.13.right_a, bf16[1024,2048]{1,0:T(8,128)(2,1)S(1)} %copy-done.2, bf16[1024,1152]{1,0:T(8,128)(2,1)S(1)} %get-tuple-element.196.right_b), custom_call_target="tpu_custom_call" | custom-call | flops 4831838208 | bytes 13631488 | tf_op jit(solution)/shard_map/weight_grads/pallas_call | solution.py:330
  222.6 4.0 collective-permute-start.14
  237.2 6.9 %weight_grads.8 = bf16[1024,2304]{1,0:T(8,128)(2,1)S(1)} custom-call(s32[1]{0:T(128)} %bitcast.5.at_ref, bf16[1024,2048]{1,0:T(8,128)(2,1)S(1)} %copy-done.8, bf16[1024,1152]{1,0:T(8,128)(2,1)S(1)} %copy-done.29, bf16[1024,2048]{1,0:T(8,128)(2,1)S(1)} %copy-done.3, bf16[1024,1152]{1,0:T(8,128)(2,1)S(1)} %copy-done.36), custom_call_target="tpu_custom_call" | custom-call | flops 4831838208 | bytes 13631488 | tf_op jit(solution)/shard_map/weight_grads/pallas_call | solution.py:330
  244.1 8.7 %collective-permute-done.16 = bf16[256,1792]{1,0:T(8,128)(2,1)} collective-permute-done((bf16[256,1792]{1,0:T(8,128)(2,1)}, bf16[256,1792]{1,0:T(8,128)(2,1)}, u32[]{:S(2)}, u32[]{:S(2)}) %collective-permute-start.16) | collective-permute-done | bytes 917536 | tf_op jit(solution)/shard_map/ppermute | solution.py:439
  252.8 4.4 fusion.33
  260.2 11.4 %fusion.16 = bf16[1024,2048]{1,0:T(8,128)(2,1)} fusion(bf16[1024,1536]{1,0:T(8,128)(2,1)S(1)} %copy-done.13, bf16[2048,2048]{0,1:T(8,128)(2,1)} %all-gather.5.cloned.1.call-done), kind=kOutput, calls=%fused_computation.23 | convolution fusion | flops 6444548096 | bytes 13631488 | tf_op jit(solution)/shard_map/dot_general | solution.py:33
  271.7 5.9 %convolution_convert_fusion = bf16[1024,2048]{1,0:T(8,128)(2,1)} fusion(bf16[1024,512]{1,0:T(8,128)(2,1)S(1)} %copy-done.27, bf16[2048,2048]{0,1:T(8,128)(2,1)} %all-gather.5.cloned.1.call-done), kind=kOutput, calls=%fused_computation.24 | convolution fusion | flops 2149580800 | bytes 7340032 | tf_op jit(solution)/shard_map/dot_general | solution.py:33
  277.6 4.8 collective-permute-done.17
  286.4 3.2 pad_maximum_fusion.mine_ref
  293.1 3.5 collective-permute-start.24
  296.5 10.1 %add_convert_fusion.3 = bf16[1024,2048]{1,0:T(8,128)(2,1)} fusion(bf16[1024,2048]{1,0:T(8,128)(2,1)} %convolution_convert_fusion, bf16[1024,1152]{1,0:T(8,128)(2,1)S(1)} %copy-done.37, bf16[2048,2304]{1,0:T(8,128)(2,1)} %all-gather.3.cloned.1.call-done), kind=kOutput, calls=%fused_computation.3 | convolution fusion | flops 4838129664 | bytes 15466496 | tf_op jit(solution)/shard_map/dot_general | solution.py:33
  306.7 9.5 %collective-permute-done.20 = bf16[256,2048]{1,0:T(8,128)(2,1)S(1)} collective-permute-done((bf16[256,2048]{1,0:T(8,128)(2,1)}, bf16[256,2048]{1,0:T(8,128)(2,1)S(1)}, u32[]{:S(2)}, u32[]{:S(2)}) %collective-permute-start.20) | collective-permute-done | bytes 1048608 | tf_op jit(solution)/shard_map/ppermute | solution.py:401
  316.1 4.1 add_convert_fusion.9
  320.3 5.6 %collective-permute-start.22 = (bf16[256,2048]{1,0:T(8,128)(2,1)}, bf16[256,2048]{1,0:T(8,128)(2,1)S(1)}, u32[]{:S(2)}, u32[]{:S(2)}) collective-permute-start(bf16[256,2048]{1,0:T(8,128)(2,1)} %get-tuple-element.204), channel_id=1, source_target_pairs={{0,8},{4,12},{8,16},{12,20},{16,24},{20,28},{1,9},{5,13},{9,17},{1... | collective-permute-start | bytes 3145736 | tf_op jit(solution)/shard_map/ppermute | solution.py:401
  327.2 10.2 %weave.1 = bf16[2048,1792]{1,0:T(8,128)(2,1)} custom-call(s32[2]{0:T(128)} %pad_add_fusion.at_ref, bf16[1024,1792]{1,0:T(8,128)(2,1)} %pad_maximum_fusion.mine_ref, bf16[1024,1792]{1,0:T(8,128)(2,1)} %collective-permute-done.19.got_ref), custom_call_target="tpu_custom_call" | custom-call | bytes 22020096 | tf_op jit(solution)/shard_map/weave/pallas_call | solution.py:463
  337.4 9.7 %add_convert_fusion.5 = (bf16[1024,896]{1,0:T(8,128)(2,1)S(1)}, bf16[1024,896]{1,0:T(8,128)(2,1)S(1)}) fusion(f32[896]{0:T(1024)S(1)} %slice.233, bf16[1024,2048]{1,0:T(8,128)(2,1)} %norm_rows.7.left_a, bf16[2048,1792]{1,0:T(8,128)(2,1)} %weave.1), kind=kOutput, calls=%fused_computation.28 | convolution fusion | flops 3776446464 | bytes 11537920 | tf_op jit(solution)/shard_map/dot_general | solution.py:29
  347.2 4.5 multiply_convert_fusion.1.right_a
  351.7 11.6 %weight_grads.9 = bf16[2048,1792]{1,0:T(8,128)(2,1)S(1)} custom-call(s32[1]{0:T(128)} %constant.140.clone.1.at_ref, bf16[1024,2048]{1,0:T(8,128)(2,1)S(1)} %copy-done.9, bf16[1024,896]{1,0:T(8,128)(2,1)S(1)} %multiply_convert_fusion.1.right_a, bf16[1024,2048]{1,0:T(8,128)(2,1)S(1)} %copy-done.4, bf16[1024,896]{1,0:T(8,128)(2,1)S(1)} %get-tuple-element.218.right_b), custom_call_target="tpu_custom_call" | custom-call | flops 7516192768 | bytes 19398656 | tf_op jit(solution)/shard_map/weight_grads/pallas_call | solution.py:330
  366.3 5.2 fusion.31
  377.8 7.9 %add_convert_fusion.2 = bf16[1024,2048]{1,0:T(8,128)(2,1)S(1)} fusion(bf16[1024,2048]{1,0:T(8,128)(2,1)} %add_convert_fusion.3, bf16[1024,896]{1,0:T(8,128)(2,1)S(1)} %copy-done.39, bf16[2048,1792]{1,0:T(8,128)(2,1)} %weave.1), kind=kOutput, calls=%fused_computation.2 | convolution fusion | flops 3764387840 | bytes 13893632 | tf_op jit(solution)/shard_map/dot_general | solution.py:33
  385.7 5.4 collective-permute-start.31
  399.1 10.3 %fusion.10 = f32[1024,2048]{1,0:T(8,128)} fusion(bf16[1024,1152]{1,0:T(8,128)(2,1)S(1)} %copy-done.30, bf16[2048,2304]{1,0:T(8,128)(2,1)} %all-gather.3.cloned.1.call-done), kind=kOutput, calls=%fused_computation.19 | convolution fusion | flops 4831838208 | bytes 15466496 | tf_op jit(solution)/shard_map/dot_general | solution.py:33
  409.4 8.8 %add_convert_fusion.refs_5_ = bf16[1024,2048]{1,0:T(8,128)(2,1)S(1)} fusion(f32[1024,2048]{1,0:T(8,128)} %fusion.10, bf16[1024,2048]{1,0:T(8,128)(2,1)} %fusion.16, bf16[1024,896]{1,0:T(8,128)(2,1)S(1)} %multiply_convert_fusion.1.right_a, bf16[2048,1792]{1,0:T(8,128)(2,1)} %weave.1), kind=kOutput, calls=%fused_computation | convolution fusion | flops 3770679296 | bytes 22282240 | tf_op jit(solution)/shard_map/dot_general | solution.py:33
  430.0 4.1 norm_sums.1
  434.1 7.4 %collective-permute-done.31 = bf16[256,2304]{1,0:T(8,128)(2,1)} collective-permute-done((bf16[256,2304]{1,0:T(8,128)(2,1)}, bf16[256,2304]{1,0:T(8,128)(2,1)}, u32[]{:S(2)}, u32[]{:S(2)}) %collective-permute-start.31) | collective-permute-done | bytes 1179680 | tf_op jit(solution)/shard_map/ppermute | solution.py:401
  443.3 4.8 add_convert_fusion.6
  453.6 5.1 collective-permute-start.35
  463.0 3.7 fusion.54
  468.2 30.6 %collective-permute-done.38 = f32[76,128]{1,0:T(8,128)S(1)} collective-permute-done((f32[76,128]{1,0:T(8,128)S(1)}, f32[76,128]{1,0:T(8,128)S(1)}, u32[]{:S(2)}, u32[]{:S(2)}) %collective-permute-start.38) | collective-permute-done | bytes 38944 | tf_op jit(solution)/shard_map/ppermute | solution.py:556
  498.8 4.1 collective-permute-start.39
  513.3 6.3 %collective-permute-done.40 = f32[48,128]{1,0:T(8,128)S(1)} collective-permute-done((f32[48,128]{1,0:T(8,128)S(1)}, f32[48,128]{1,0:T(8,128)S(1)}, u32[]{:S(2)}, u32[]{:S(2)}) %collective-permute-start.40) | collective-permute-done | bytes 24608 | tf_op jit(solution)/shard_map/ppermute | solution.py:556
  (365 shorter events, 161.7 us)
Async XLA Ops:
  7.2 93.5 %all-gather.5.cloned.1.call-start = ((), (), s32[]{:S(2)}) async-start(), calls=%async_computation.2 | async-start | bytes 9437184 | tf_op jit(solution)/shard_map/all_gather | solution.py:639
  12.8 180.5 %all-gather.3.cloned.1.call-start = ((), (), s32[]{:S(2)}) async-start(), calls=%async_computation.1 | async-start | bytes 10616832 | tf_op jit(solution)/shard_map/all_gather | solution.py:652
  13.4 4.6 collective-permute-start.2
  13.9 27.0 %collective-permute-start.1 = (bf16[256,2048]{1,0:T(8,128)(2,1)S(1)}, bf16[256,2048]{1,0:T(8,128)(2,1)S(1)}, u32[]{:S(2)}, u32[]{:S(2)}) collective-permute-start(bf16[256,2048]{1,0:T(8,128)(2,1)S(1)} %copy-done.10), channel_id=1, source_target_pairs={{0,2},{1,3},{2,0},{3,1},{4,6},{5,7},{6,4},{7,5},{8,10},{9,11},{10,... | collective-permute-start | bytes 3145736 | tf_op jit(solution)/shard_map/ppermute | solution.py:645
  16.5 25.2 %collective-permute-start = (bf16[256,2048]{1,0:T(8,128)(2,1)S(1)}, bf16[256,2048]{1,0:T(8,128)(2,1)S(1)}, u32[]{:S(2)}, u32[]{:S(2)}) collective-permute-start(bf16[256,2048]{1,0:T(8,128)(2,1)S(1)} %copy-done.10), channel_id=1, source_target_pairs={{0,1},{1,0},{2,3},{3,2},{4,5},{5,4},{6,7},{7,6},{8,9},{9,8},{10,11... | collective-permute-start | bytes 3145736 | tf_op jit(solution)/shard_map/ppermute | solution.py:645
  18.1 7.0 %collective-permute-start.3 = (bf16[8,1472]{1,0:T(8,128)(2,1)S(1)}, bf16[8,1472]{1,0:T(8,128)(2,1)S(1)}, u32[]{:S(2)}, u32[]{:S(2)}) collective-permute-start(bf16[8,1472]{1,0:T(8,128)(2,1)S(1)} %fusion.57), channel_id=1, source_target_pairs={{0,8},{4,12},{8,0},{12,4},{16,24},{20,28},{24,16},{28,20},{1,9},{5... | collective-permute-start | bytes 70664 | tf_op jit(solution)/shard_map/ppermute | solution.py:556
  25.2 15.7 %collective-permute-start.4 = (bf16[8,1472]{1,0:T(8,128)(2,1)S(1)}, bf16[8,1472]{1,0:T(8,128)(2,1)S(1)}, u32[]{:S(2)}, u32[]{:S(2)}) collective-permute-start(bf16[8,1472]{1,0:T(8,128)(2,1)S(1)} %fusion.82), channel_id=1, source_target_pairs={{0,16},{4,20},{8,24},{12,28},{16,0},{20,4},{24,8},{28,12},{1,17},{... | collective-permute-start | bytes 70664 | tf_op jit(solution)/shard_map/ppermute | solution.py:556
  40.9 129.7 %copy-start.59 = (bf16[8,1472]{1,0:T(8,128)(2,1)}, bf16[8,1472]{1,0:T(8,128)(2,1)S(1)}, u32[]{:S(2)}) copy-start(bf16[8,1472]{1,0:T(8,128)(2,1)S(1)} %add.390) | copy-start | bytes 70660
  41.7 489.8 %reduce-scatter.2.cloned.1.call-start = ((), (), s32[]{:S(2)}) async-start(), calls=%async_computation.3 | async-start | bytes 8257536 | tf_op jit(solution)/shard_map/reduce_scatter | solution.py:728
  41.8 26.4 %collective-permute-start.8 = (bf16[256,2048]{1,0:T(8,128)(2,1)}, bf16[256,2048]{1,0:T(8,128)(2,1)}, u32[]{:S(2)}, u32[]{:S(2)}) collective-permute-start(bf16[256,2048]{1,0:T(8,128)(2,1)} %refs_1_.1), channel_id=1, source_target_pairs={{0,2},{1,3},{2,0},{3,1},{4,6},{5,7},{6,4},{7,5},{8,10},{9,11},{10,... | collective-permute-start | bytes 3145736 | tf_op jit(solution)/shard_map/ppermute | solution.py:645
  42.5 26.3 %collective-permute-start.7 = (bf16[256,2048]{1,0:T(8,128)(2,1)}, bf16[256,2048]{1,0:T(8,128)(2,1)}, u32[]{:S(2)}, u32[]{:S(2)}) collective-permute-start(bf16[256,2048]{1,0:T(8,128)(2,1)} %refs_1_.1), channel_id=1, source_target_pairs={{0,1},{1,0},{2,3},{3,2},{4,5},{5,4},{6,7},{7,6},{8,9},{9,8},{10,11... | collective-permute-start | bytes 3145736 | tf_op jit(solution)/shard_map/ppermute | solution.py:645
  49.5 35.8 %collective-permute-start.6 = (bf16[256,1024]{1,0:T(8,128)(2,1)}, bf16[256,1024]{1,0:T(8,128)(2,1)S(1)}, u32[]{:S(2)}, u32[]{:S(2)}) collective-permute-start(bf16[256,1024]{1,0:T(8,128)(2,1)} %slice.203), channel_id=1, source_target_pairs={{0,1},{1,0},{2,3},{3,2},{4,5},{5,4},{6,7},{7,6},{8,9},{9,8},{10,11... | collective-permute-start | bytes 1572872 | tf_op jit(solution)/shard_map/ppermute | solution.py:645
  50.1 35.2 %collective-permute-start.5 = (bf16[256,1024]{1,0:T(8,128)(2,1)}, bf16[256,1024]{1,0:T(8,128)(2,1)S(1)}, u32[]{:S(2)}, u32[]{:S(2)}) collective-permute-start(bf16[256,1024]{1,0:T(8,128)(2,1)} %slice.202), channel_id=1, source_target_pairs={{0,2},{1,3},{2,0},{3,1},{4,6},{5,7},{6,4},{7,5},{8,10},{9,11},{10,... | collective-permute-start | bytes 1572872 | tf_op jit(solution)/shard_map/ppermute | solution.py:645
  72.5 16.8 %collective-permute-start.10 = (bf16[256,1024]{1,0:T(8,128)(2,1)}, bf16[256,1024]{1,0:T(8,128)(2,1)S(1)}, u32[]{:S(2)}, u32[]{:S(2)}) collective-permute-start(bf16[256,1024]{1,0:T(8,128)(2,1)} %slice.207), channel_id=1, source_target_pairs={{0,1},{1,0},{2,3},{3,2},{4,5},{5,4},{6,7},{7,6},{8,9},{9,8},{10,11... | collective-permute-start | bytes 1572872 | tf_op jit(solution)/shard_map/ppermute | solution.py:645
  73.9 15.4 %collective-permute-start.9 = (bf16[256,1024]{1,0:T(8,128)(2,1)}, bf16[256,1024]{1,0:T(8,128)(2,1)}, u32[]{:S(2)}, u32[]{:S(2)}) collective-permute-start(bf16[256,1024]{1,0:T(8,128)(2,1)} %slice.206), channel_id=1, source_target_pairs={{0,2},{1,3},{2,0},{3,1},{4,6},{5,7},{6,4},{7,5},{8,10},{9,11},{10,... | collective-permute-start | bytes 1572872 | tf_op jit(solution)/shard_map/ppermute | solution.py:645
  170.2 40.4 %collective-permute-start.11 = (bf16[1024,2048]{1,0:T(8,128)(2,1)}, bf16[1024,2048]{1,0:T(8,128)(2,1)}, u32[]{:S(2)}, u32[]{:S(2)}) collective-permute-start(bf16[1024,2048]{1,0:T(8,128)(2,1)} %weight_grads.5), channel_id=1, source_target_pairs={{0,4},{4,0},{8,12},{12,8},{16,20},{20,16},{24,28},{28,24},{1,5},{5... | collective-permute-start | bytes 12582920 | tf_op jit(solution)/shard_map/ppermute | solution.py:369
  184.4 26.2 %collective-permute-start.13 = (bf16[256,1792]{1,0:T(8,128)(2,1)}, bf16[256,1792]{1,0:T(8,128)(2,1)}, u32[]{:S(2)}, u32[]{:S(2)}) collective-permute-start(bf16[256,1792]{1,0:T(8,128)(2,1)} %pad_maximum_fusion.8), channel_id=1, source_target_pairs={{28,20},{24,16},{20,12},{16,8},{12,4},{8,0},{29,21},{25,17},{21,13... | collective-permute-start | bytes 2752520 | tf_op jit(solution)/shard_map/ppermute | solution.py:439
  185.7 25.0 %collective-permute-start.12 = (bf16[256,1792]{1,0:T(8,128)(2,1)}, bf16[256,1792]{1,0:T(8,128)(2,1)}, u32[]{:S(2)}, u32[]{:S(2)}) collective-permute-start(bf16[256,1792]{1,0:T(8,128)(2,1)} %pad_maximum_fusion.8), channel_id=1, source_target_pairs={{0,8},{4,12},{8,16},{12,20},{16,24},{20,28},{1,9},{5,13},{9,17},{1... | collective-permute-start | bytes 2752520 | tf_op jit(solution)/shard_map/ppermute | solution.py:439
  222.3 60.1 %collective-permute-start.18 = (bf16[1024,2304]{1,0:T(8,128)(2,1)}, bf16[1024,2304]{1,0:T(8,128)(2,1)}, u32[]{:S(2)}, u32[]{:S(2)}) collective-permute-start(bf16[1024,2304]{1,0:T(8,128)(2,1)} %weight_grads.7), channel_id=1, source_target_pairs={{0,4},{4,0},{8,12},{12,8},{16,20},{20,16},{24,28},{28,24},{1,5},{5... | collective-permute-start | bytes 14155784 | tf_op jit(solution)/shard_map/ppermute | solution.py:369
  222.6 30.2 %collective-permute-start.14 = (bf16[256,2048]{1,0:T(8,128)(2,1)}, bf16[256,2048]{1,0:T(8,128)(2,1)}, u32[]{:S(2)}, u32[]{:S(2)}) collective-permute-start(bf16[256,2048]{1,0:T(8,128)(2,1)} %add_convert_fusion.11), channel_id=1, source_target_pairs={{0,8},{4,12},{28,20},{24,16},{1,9},{5,13},{29,21},{25,17},{2,10},{... | collective-permute-start | bytes 3145736 | tf_op jit(solution)/shard_map/ppermute | solution.py:399
  226.6 17.5 %collective-permute-start.15 = (bf16[256,1792]{1,0:T(8,128)(2,1)}, bf16[256,1792]{1,0:T(8,128)(2,1)}, u32[]{:S(2)}, u32[]{:S(2)}) collective-permute-start(bf16[256,1792]{1,0:T(8,128)(2,1)} %collective-permute-done.12), channel_id=1, source_target_pairs={{8,16},{12,20},{16,24},{20,28},{9,17},{13,21},{17,25},{21,29},{10,... | collective-permute-start | bytes 2752520 | tf_op jit(solution)/shard_map/ppermute | solution.py:439
  228.1 24.7 %collective-permute-start.16 = (bf16[256,1792]{1,0:T(8,128)(2,1)}, bf16[256,1792]{1,0:T(8,128)(2,1)}, u32[]{:S(2)}, u32[]{:S(2)}) collective-permute-start(bf16[256,1792]{1,0:T(8,128)(2,1)} %collective-permute-done.13), channel_id=1, source_target_pairs={{20,12},{16,8},{12,4},{8,0},{21,13},{17,9},{13,5},{9,1},{22,14},{1... | collective-permute-start | bytes 2752520 | tf_op jit(solution)/shard_map/ppermute | solution.py:439
  244.1 38.4 %copy-start.18 = (bf16[1024,2304]{1,0:T(8,128)(2,1)}, bf16[1024,2304]{1,0:T(8,128)(2,1)S(1)}, u32[]{:S(2)}) copy-start(bf16[1024,2304]{1,0:T(8,128)(2,1)S(1)} %weight_grads.8) | copy-start | bytes 14155780
  258.8 23.6 %collective-permute-start.17 = (bf16[256,1792]{1,0:T(8,128)(2,1)S(1)}, bf16[256,1792]{1,0:T(8,128)(2,1)S(1)}, u32[]{:S(2)}, u32[]{:S(2)}) collective-permute-start(bf16[256,1792]{1,0:T(8,128)(2,1)S(1)} %get-tuple-element.181), channel_id=1, source_target_pairs={{16,24},{20,28},{12,4},{8,0},{17,25},{21,29},{13,5},{9,1},{18,26},... | collective-permute-start | bytes 2752520 | tf_op jit(solution)/shard_map/ppermute | solution.py:437
  289.6 26.6 %collective-permute-start.19 = (bf16[1024,1792]{1,0:T(8,128)(2,1)}, bf16[1024,1792]{1,0:T(8,128)(2,1)}, u32[]{:S(2)}, u32[]{:S(2)}) collective-permute-start(bf16[1024,1792]{1,0:T(8,128)(2,1)} %pad_maximum_fusion.mine_ref), channel_id=1, source_target_pairs={{0,4},{4,0},{8,12},{12,8},{16,20},{20,16},{24,28},{28,24},{1,5},{5... | collective-permute-start | bytes 11010056 | tf_op jit(solution)/shard_map/ppermute | solution.py:432
  290.3 25.8 %collective-permute-start.20 = (bf16[256,2048]{1,0:T(8,128)(2,1)}, bf16[256,2048]{1,0:T(8,128)(2,1)S(1)}, u32[]{:S(2)}, u32[]{:S(2)}) collective-permute-start(bf16[256,2048]{1,0:T(8,128)(2,1)} %get-tuple-element.193), channel_id=1, source_target_pairs={{0,8},{4,12},{8,16},{12,20},{1,9},{5,13},{9,17},{13,21},{2,10},{6,... | collective-permute-start | bytes 3145736 | tf_op jit(solution)/shard_map/ppermute | solution.py:401
  292.4 23.8 %collective-permute-start.21 = (bf16[256,2048]{1,0:T(8,128)(2,1)S(1)}, bf16[256,2048]{1,0:T(8,128)(2,1)S(1)}, u32[]{:S(2)}, u32[]{:S(2)}) collective-permute-start(bf16[256,2048]{1,0:T(8,128)(2,1)S(1)} %copy-done.56), channel_id=1, source_target_pairs={{28,20},{24,16},{20,12},{16,8},{29,21},{25,17},{21,13},{17,9},{30,... | collective-permute-start | bytes 3145736 | tf_op jit(solution)/shard_map/ppermute | solution.py:401
  293.1 73.2 %collective-permute-start.24 = (bf16[256,2304]{1,0:T(8,128)(2,1)}, bf16[256,2304]{1,0:T(8,128)(2,1)}, u32[]{:S(2)}, u32[]{:S(2)}) collective-permute-start(bf16[256,2304]{1,0:T(8,128)(2,1)} %add_convert_fusion.8), channel_id=1, source_target_pairs={{0,8},{4,12},{28,20},{24,16},{1,9},{5,13},{29,21},{25,17},{2,10},{... | collective-permute-start | bytes 3538952 | tf_op jit(solution)/shard_map/ppermute | solution.py:399
  320.3 46.0 %collective-permute-start.22 = (bf16[256,2048]{1,0:T(8,128)(2,1)}, bf16[256,2048]{1,0:T(8,128)(2,1)S(1)}, u32[]{:S(2)}, u32[]{:S(2)}) collective-permute-start(bf16[256,2048]{1,0:T(8,128)(2,1)} %get-tuple-element.204), channel_id=1, source_target_pairs={{0,8},{4,12},{8,16},{12,20},{16,24},{20,28},{1,9},{5,13},{9,17},{1... | collective-permute-start | bytes 3145736 | tf_op jit(solution)/shard_map/ppermute | solution.py:401
  325.9 40.4 %collective-permute-start.23 = (bf16[256,2048]{1,0:T(8,128)(2,1)}, bf16[256,2048]{1,0:T(8,128)(2,1)}, u32[]{:S(2)}, u32[]{:S(2)}) collective-permute-start(bf16[256,2048]{1,0:T(8,128)(2,1)} %get-tuple-element.205), channel_id=1, source_target_pairs={{28,20},{24,16},{20,12},{16,8},{12,4},{8,0},{29,21},{25,17},{21,13... | collective-permute-start | bytes 3145736 | tf_op jit(solution)/shard_map/ppermute | solution.py:401
  385.7 55.9 %collective-permute-start.31 = (bf16[256,2304]{1,0:T(8,128)(2,1)}, bf16[256,2304]{1,0:T(8,128)(2,1)}, u32[]{:S(2)}, u32[]{:S(2)}) collective-permute-start(bf16[256,2304]{1,0:T(8,128)(2,1)} %get-tuple-element.228), channel_id=1, source_target_pairs={{0,8},{4,12},{8,16},{12,20},{1,9},{5,13},{9,17},{13,21},{2,10},{6,... | collective-permute-start | bytes 3538952 | tf_op jit(solution)/shard_map/ppermute | solution.py:401
  391.1 52.2 %collective-permute-start.32 = (bf16[256,2304]{1,0:T(8,128)(2,1)}, bf16[256,2304]{1,0:T(8,128)(2,1)}, u32[]{:S(2)}, u32[]{:S(2)}) collective-permute-start(bf16[256,2304]{1,0:T(8,128)(2,1)} %get-tuple-element.229), channel_id=1, source_target_pairs={{28,20},{24,16},{20,12},{16,8},{29,21},{25,17},{21,13},{17,9},{30,... | collective-permute-start | bytes 3538952 | tf_op jit(solution)/shard_map/ppermute | solution.py:401
  393.1 29.0 %collective-permute-start.25 = (bf16[512,1024]{1,0:T(8,128)(2,1)S(1)}, bf16[512,1024]{1,0:T(8,128)(2,1)S(1)}, u32[]{:S(2)}, u32[]{:S(2)}) collective-permute-start(bf16[512,1024]{1,0:T(8,128)(2,1)S(1)} %pad_maximum_fusion.4), channel_id=1, source_target_pairs={{0,1},{1,0},{2,3},{3,2},{4,5},{5,4},{6,7},{7,6},{8,9},{9,8},{10,11... | collective-permute-start | bytes 3145736 | tf_op jit(solution)/shard_map/ppermute | solution.py:524
  395.1 27.1 %collective-permute-start.26 = (bf16[512,1024]{1,0:T(8,128)(2,1)S(1)}, bf16[512,1024]{1,0:T(8,128)(2,1)S(1)}, u32[]{:S(2)}, u32[]{:S(2)}) collective-permute-start(bf16[512,1024]{1,0:T(8,128)(2,1)S(1)} %pad_maximum_fusion.5), channel_id=1, source_target_pairs={{0,2},{1,3},{2,0},{3,1},{4,6},{5,7},{6,4},{7,5},{8,10},{9,11},{10,... | collective-permute-start | bytes 3145736 | tf_op jit(solution)/shard_map/ppermute | solution.py:524
  422.7 26.1 %collective-permute-start.29 = (bf16[512,1024]{1,0:T(8,128)(2,1)S(1)}, bf16[512,1024]{1,0:T(8,128)(2,1)S(1)}, u32[]{:S(2)}, u32[]{:S(2)}) collective-permute-start(bf16[512,1024]{1,0:T(8,128)(2,1)S(1)} %pad_maximum_fusion.6), channel_id=1, source_target_pairs={{0,1},{1,0},{2,3},{3,2},{4,5},{5,4},{6,7},{7,6},{8,9},{9,8},{10,11... | collective-permute-start | bytes 3145736 | tf_op jit(solution)/shard_map/ppermute | solution.py:524
  423.5 26.1 %collective-permute-start.30 = (bf16[512,1024]{1,0:T(8,128)(2,1)S(1)}, bf16[512,1024]{1,0:T(8,128)(2,1)S(1)}, u32[]{:S(2)}, u32[]{:S(2)}) collective-permute-start(bf16[512,1024]{1,0:T(8,128)(2,1)S(1)} %pad_maximum_fusion.7), channel_id=1, source_target_pairs={{0,2},{1,3},{2,0},{3,1},{4,6},{5,7},{6,4},{7,5},{8,10},{9,11},{10,... | collective-permute-start | bytes 3145736 | tf_op jit(solution)/shard_map/ppermute | solution.py:524
  428.3 32.0 %collective-permute-start.28 = (bf16[256,1024]{1,0:T(8,128)(2,1)}, bf16[256,1024]{1,0:T(8,128)(2,1)}, u32[]{:S(2)}, u32[]{:S(2)}) collective-permute-start(bf16[256,1024]{1,0:T(8,128)(2,1)} %get-tuple-element.312), channel_id=1, source_target_pairs={{0,1},{1,0},{2,3},{3,2},{4,5},{5,4},{6,7},{7,6},{8,9},{9,8},{10,11... | collective-permute-start | bytes 1572872 | tf_op jit(solution)/shard_map/ppermute | solution.py:536
  441.5 18.7 %collective-permute-start.27 = (bf16[256,1024]{1,0:T(8,128)(2,1)}, bf16[256,1024]{1,0:T(8,128)(2,1)}, u32[]{:S(2)}, u32[]{:S(2)}) collective-permute-start(bf16[256,1024]{1,0:T(8,128)(2,1)} %get-tuple-element.313), channel_id=1, source_target_pairs={{0,2},{1,3},{2,0},{3,1},{4,6},{5,7},{6,4},{7,5},{8,10},{9,11},{10,... | collective-permute-start | bytes 1572872 | tf_op jit(solution)/shard_map/ppermute | solution.py:536
  450.7 9.6 %collective-permute-start.37 = (f32[76,128]{1,0:T(8,128)S(1)}, f32[76,128]{1,0:T(8,128)S(1)}, u32[]{:S(2)}, u32[]{:S(2)}) collective-permute-start(f32[76,128]{1,0:T(8,128)S(1)} %bitcast.76), channel_id=1, source_target_pairs={{0,4},{4,0},{8,12},{12,8},{16,20},{20,16},{24,28},{28,24},{1,5},{5... | collective-permute-start | bytes 116744 | tf_op jit(solution)/shard_map/ppermute | solution.py:556
  453.6 56.3 %collective-permute-start.35 = (bf16[256,2304]{1,0:T(8,128)(2,1)}, bf16[256,2304]{1,0:T(8,128)(2,1)}, u32[]{:S(2)}, u32[]{:S(2)}) collective-permute-start(bf16[256,2304]{1,0:T(8,128)(2,1)} %get-tuple-element.236), channel_id=1, source_target_pairs={{0,8},{4,12},{8,16},{12,20},{16,24},{20,28},{1,9},{5,13},{9,17},{1... | collective-permute-start | bytes 3538952 | tf_op jit(solution)/shard_map/ppermute | solution.py:401
  458.7 51.2 %collective-permute-start.36 = (bf16[256,2304]{1,0:T(8,128)(2,1)}, bf16[256,2304]{1,0:T(8,128)(2,1)}, u32[]{:S(2)}, u32[]{:S(2)}) collective-permute-start(bf16[256,2304]{1,0:T(8,128)(2,1)} %get-tuple-element.237), channel_id=1, source_target_pairs={{28,20},{24,16},{20,12},{16,8},{12,4},{8,0},{29,21},{25,17},{21,13... | collective-permute-start | bytes 3538952 | tf_op jit(solution)/shard_map/ppermute | solution.py:401
  460.3 38.5 %collective-permute-start.38 = (f32[76,128]{1,0:T(8,128)S(1)}, f32[76,128]{1,0:T(8,128)S(1)}, u32[]{:S(2)}, u32[]{:S(2)}) collective-permute-start(f32[76,128]{1,0:T(8,128)S(1)} %bitcast_add_fusion), channel_id=1, source_target_pairs={{0,8},{4,12},{8,0},{12,4},{16,24},{20,28},{24,16},{28,20},{1,9},{5... | collective-permute-start | bytes 116744 | tf_op jit(solution)/shard_map/ppermute | solution.py:556
  468.2 34.6 %copy-start.41 = (f32[512,1024]{1,0:T(8,128)}, f32[512,1024]{1,0:T(8,128)S(1)}, u32[]{:S(2)}) copy-start(f32[512,1024]{1,0:T(8,128)S(1)} %convert_element_type.444) | copy-start | bytes 6291460
  498.8 9.5 %collective-permute-start.39 = (f32[76,128]{1,0:T(8,128)S(1)}, f32[76,128]{1,0:T(8,128)S(1)}, u32[]{:S(2)}, u32[]{:S(2)}) collective-permute-start(f32[76,128]{1,0:T(8,128)S(1)} %fusion.81), channel_id=1, source_target_pairs={{0,16},{4,20},{8,24},{12,28},{16,0},{20,4},{24,8},{28,12},{1,17},{... | collective-permute-start | bytes 116744 | tf_op jit(solution)/shard_map/ppermute | solution.py:556
  505.4 18.1 %collective-permute-start.34 = (bf16[256,1024]{1,0:T(8,128)(2,1)}, bf16[256,1024]{1,0:T(8,128)(2,1)}, u32[]{:S(2)}, u32[]{:S(2)}) collective-permute-start(bf16[256,1024]{1,0:T(8,128)(2,1)} %get-tuple-element.304), channel_id=1, source_target_pairs={{0,1},{1,0},{2,3},{3,2},{4,5},{5,4},{6,7},{7,6},{8,9},{9,8},{10,11... | collective-permute-start | bytes 1572872 | tf_op jit(solution)/shard_map/ppermute | solution.py:536
  506.9 16.7 %collective-permute-start.33 = (bf16[256,1024]{1,0:T(8,128)(2,1)}, bf16[256,1024]{1,0:T(8,128)(2,1)}, u32[]{:S(2)}, u32[]{:S(2)}) collective-permute-start(bf16[256,1024]{1,0:T(8,128)(2,1)} %get-tuple-element.305), channel_id=1, source_target_pairs={{0,2},{1,3},{2,0},{3,1},{4,6},{5,7},{6,4},{7,5},{8,10},{9,11},{10,... | collective-permute-start | bytes 1572872 | tf_op jit(solution)/shard_map/ppermute | solution.py:536
  509.9 9.7 %collective-permute-start.40 = (f32[48,128]{1,0:T(8,128)S(1)}, f32[48,128]{1,0:T(8,128)S(1)}, u32[]{:S(2)}, u32[]{:S(2)}) collective-permute-start(f32[48,128]{1,0:T(8,128)S(1)} %slice.283), channel_id=1, source_target_pairs={{0,1},{1,0},{2,3},{3,2},{4,5},{5,4},{6,7},{7,6},{8,9},{9,8},{10,11... | collective-permute-start | bytes 73736 | tf_op jit(solution)/shard_map/ppermute | solution.py:556
  519.7 3.8 collective-permute-start.41
  (69 other events, 410.3 us)
Sparse Core Ops, SparseCore 0:
  13.0 87.7 all-gather.4
  102.9 90.3 all-gather.2
  371.7 119.4 reduce-scatter.1

commit v3 on v2

--- a/solution.py
+++ b/solution.py
@@ -734,8 +734,8 @@
     (normed_grad_low,) = output_sum.second(normed_grad_low)
     up_bias_grads = [jnp.sum(item, axis=0, dtype=F32) for item in (near_grad, up_pre_grad)]
     grad_sum = TensorScatter(normed_grad_low, tok_rows)
+    (normed_grad_low,) = advance(lines, normed_grad_low)
     gain_shift = norm_sums(tensor.astype(jnp.int32)[None], tok_parts, normed_grad_low)
-    (gain_shift,) = advance(lines, gain_shift)
     (gain_shift,) = grad_sum.second(gain_shift)
     own = tokens.astype(F32)
     (output_rows,) = output_sum.result()
@@ -745,18 +745,21 @@
 
     shared = jnp.concatenate([gain_shift.reshape(-1), jnp.sum(own_grad, axis=0)])
     kept = jnp.concatenate([head_bias_grad] + up_bias_grads)
-    summed = all_sum(jnp.concatenate([shared, kept]).reshape(-1, LANES), "dp")
-    many = shared.shape[0] // LANES
-    shared = summed[:many]
+    shared = all_sum(shared.reshape(-1, LANES), "tensor")
     while not all(item.done() for item in lines):
         (shared,) = advance(lines, shared)
-    shared = all_sum(shared, "tensor")
+    many = shared.shape[0]
+    summed = jnp.concatenate([shared, kept.reshape(-1, LANES)])
     attn_shard = attn_line.total
     mlp_shards = [line.total, far_shard.astype(F32)]
-    own_normed_grad, shared = grad_sum.result(shared)
+    up_out = jnp.concatenate([item[:, : item.shape[1] // 2] for item in mlp_shards], axis=1)
+    down_out = jnp.concatenate([item[:, item.shape[1] // 2 :].T for item in mlp_shards], axis=0)
+    (own_normed_grad,) = grad_sum.result()
     _, norm_back = jax.vjp(lambda rows: layer_norm(rows, n_gain, n_shift), own)
     input_grad = own_grad + norm_back(own_normed_grad)[0]
-    shared = shared.reshape(3, dp_count, shard)
+    summed, input_grad, up_out, down_out = tie(summed, input_grad, up_out, down_out)
+    summed = all_sum(summed, "dp")
+    shared = summed[:many].reshape(3, dp_count, shard)
     gain_grad, shift_grad, out_bias = lax.dynamic_index_in_dim(shared, place, 1, keepdims=False)
     kept = summed[many:].reshape(-1)
     head_out = lax.dynamic_index_in_dim(
@@ -777,8 +780,6 @@
             [attn_shard[:, (3 * p + which) * LANES : (3 * p + which + 1) * LANES] for p in range(pairs)], axis=1
         )
 
-    up_out = jnp.concatenate([item[:, : item.shape[1] // 2] for item in mlp_shards], axis=1)
-    down_out = jnp.concatenate([item[:, item.shape[1] // 2 :].T for item in mlp_shards], axis=0)
     return (
         output,
         input_grad,

time: 555 us -> 538 us (0.969)
  other arithmetic: 71.4 us -> 62.6 us
    ppermute x8, waiting for transfers between devices: 48.5 us -> 18.3 us  [all_sum(): value = value + lax.ppermute(value, axis, swap_pairs(count, bit))]
    ppermute x12, waiting for transfers between devices: 25.6 us -> 52.7 us  [send(): lax.ppermute(item, 'dp', way)]
    unnamed x180 -> x194, local copies, waits for them, and re-layouts: 39.5 us -> 36.4 us
  transfers between devices with their start and end apart: 45 -> 45, of which waited for: 15 -> 20; matrix products, arithmetic and copies ran while one was open for 32% -> 31% of each run, Pallas kernels for 20% -> 21%
where the time goes in v3:
time: 538 us; the launch traced here: 529 us
  Pallas kernels  118 us (22%)
  matrix products  101 us (19%)
  waiting for transfers between devices  97.5 us (18%)
  starting transfers between devices  78.5 us (15%)
  other arithmetic  62.6 us (12%)
  local copies, waits for them, and re-layouts  55.6 us (10%)
  between operations  16.5 us (3%)
    ppermute x12, waiting for transfers between devices, send(): lax.ppermute(item, 'dp', way)  52.7 us
    dot_general x6, matrix products, times_trans(): lax.dot_general(left, right, (((1,), (1,)), ((), ())), preferred_element_...  52.7 us
    dot_general x6, matrix products, product(): return jnp.dot(left, right, preferred_element_type=F32)  48.1 us
    pallas_call x5, Pallas kernels, weight_grads(): pl.pallas_call(weight_kernel, grid_spec=pltpu.PrefetchScalarGridSpec(num_...  39 us
    unnamed x194, local copies, waits for them, and re-layouts  36.4 us
    ppermute x12, starting transfers between devices, send(): lax.ppermute(item, 'dp', way)  34.2 us
    pallas_call x1, Pallas kernels, attention_backward(): pl.pallas_call(attn_bwd_kernel, grid=(pairs,), in_specs=[pl.BlockSpec(mem...  26.6 us
    convert_element_type x6, other arithmetic, next_sends(): (sent if item is None else sent + item.astype(F32)).astype(BF16)  22.9 us
  transfers between devices with their start and end apart: 45, of which 20 were waited for; matrix products, arithmetic and copies ran while one was open for 31% of the time, Pallas kernels for 21%

profile of v3, /device:TPU:0, one launch (start us, length us, event | category | flops | bytes accessed | tf_op | source)
XLA Modules:
  0.0 529.2 jit_solution(10455545381548398846)
XLA Ops:
  29.9 10.9 %collective-permute-done.4 = bf16[8,1472]{1,0:T(8,128)(2,1)S(1)} collective-permute-done((bf16[8,1472]{1,0:T(8,128)(2,1)S(1)}, bf16[8,1472]{1,0:T(8,128)(2,1)S(1)}, u32[]{:S(2)}, u32[]{:S(2)}) %collective-permute-start.4) | collective-permute-done | bytes 23584 | tf_op jit(solution)/shard_map/ppermute | solution.py:556
  51.5 3.0 norm_rows.4.refs_3_
  54.5 3.0 norm_rows.5.refs_3_
  57.5 3.0 norm_rows.6.refs_4_
  60.5 7.7 %collective-permute-done.8.refs_0_ = bf16[256,2048]{1,0:T(8,128)(2,1)} collective-permute-done((bf16[256,2048]{1,0:T(8,128)(2,1)}, bf16[256,2048]{1,0:T(8,128)(2,1)}, u32[]{:S(2)}, u32[]{:S(2)}) %collective-permute-start.8) | collective-permute-done | bytes 1048608 | tf_op jit(solution)/shard_map/ppermute | solution.py:645
  86.3 3.1 norm_rows.7.left_a
  92.4 8.3 %all-gather.5.cloned.1.call-done = bf16[2048,2048]{0,1:T(8,128)(2,1)} async-done(((bf16[256,2048]{0,1:T(8,128)(2,1)}), bf16[2048,2048]{0,1:T(8,128)(2,1)}) %all-gather.5.cloned.1.call-update) | async-done | bytes 8388624 | tf_op jit(solution)/shard_map/all_gather | solution.py:639
  100.7 12.4 %fusion.4.qkv_ref = f32[1024,1536]{1,0:T(8,128)} fusion(bf16[1024,2048]{1,0:T(8,128)(2,1)} %norm_rows.7.left_a, bf16[2048,2048]{0,1:T(8,128)(2,1)} %all-gather.5.cloned.1.call-done, f32[1536]{0:T(1024)S(1)} %reshape.189), kind=kOutput, calls=%fused_computation.15 | convolution fusion | flops 6444023808 | bytes 16783360 | tf_op jit(solution)/shard_map/dot_general | solution.py:29
  113.1 16.6 %attn_fwd.1 = (bf16[1024,512]{1,0:T(8,128)(2,1)S(1)}, bf16[1024,512]{1,0:T(8,128)(2,1)S(1)}, bf16[1024,512]{1,0:T(8,128)(2,1)S(1)}, bf16[1024,512]{1,0:T(8,128)(2,1)S(1)}, f32[1024,512]{1,0:T(8,128)}) custom-call(s32[1]{0:T(128)} %copy.131.len_ref, f32[1024,1536]{1,0:T(8,128)} %fusion.4.qkv_ref, f32[1024,128]{1,0:T(8,128)S(1)} %get-tuple-element.369.keep_ref, ...), custom_call_target="tpu_custom_call" | custom-call | flops 6442450944 | bytes 12582912 | tf_op jit(solution)/shard_map/attn_fwd/pallas_call | solution.py:189
  129.7 4.4 fusion.44.grad_ref
  134.1 26.6 %attn_bwd.1.right_a = bf16[1024,1536]{1,0:T(8,128)(2,1)} custom-call(s32[1]{0:T(128)} %copy.131.len_ref, bf16[1024,512]{1,0:T(8,128)(2,1)S(1)} %get-tuple-element.147.q_ref, bf16[1024,512]{1,0:T(8,128)(2,1)S(1)} %get-tuple-element.148.k_ref, bf16[1024,512]{1,0:T(8,128)(2,1)S(1)} %get-tuple-element.149.v_ref, bf16[1024,512]{1,0:T(8,128)(2,1)S(1)} %fusion.44.grad_ref, ...), custom_call_target="tpu_custom_call" | custom-call | flops 16106127360 | bytes 12582912 | tf_op jit(solution)/shard_map/attn_bwd/pallas_call | solution.py:211
  163.9 6.8 %weight_grads.5 = bf16[1024,2048]{1,0:T(8,128)(2,1)} custom-call(s32[1]{0:T(128)} %bitcast.9.at_ref, bf16[1024,2048]{1,0:T(8,128)(2,1)S(1)} %copy-done.5, bf16[1024,1536]{1,0:T(8,128)(2,1)S(1)} %copy-done.12, bf16[1024,2048]{1,0:T(8,128)(2,1)S(1)} %copy-done, bf16[1024,512]{1,0:T(8,128)(2,1)S(1)} %copy-done.24), custom_call_target="tpu_custom_call" | custom-call | flops 4294967296 | bytes 12582912 | tf_op jit(solution)/shard_map/weight_grads/pallas_call | solution.py:330
  176.8 5.8 %weight_grads.6 = bf16[1024,2048]{1,0:T(8,128)(2,1)S(1)} custom-call(s32[1]{0:T(128)} %bitcast.5.at_ref, bf16[1024,2048]{1,0:T(8,128)(2,1)S(1)} %copy-done.6, bf16[1024,1536]{1,0:T(8,128)(2,1)S(1)} %copy-done.13, bf16[1024,2048]{1,0:T(8,128)(2,1)S(1)} %copy-done.1, bf16[1024,512]{1,0:T(8,128)(2,1)S(1)} %copy-done.25), custom_call_target="tpu_custom_call" | custom-call | flops 4294967296 | bytes 12582912 | tf_op jit(solution)/shard_map/weight_grads/pallas_call | solution.py:330
  185.9 5.5 %collective-permute-start.12 = (bf16[256,1792]{1,0:T(8,128)(2,1)}, bf16[256,1792]{1,0:T(8,128)(2,1)}, u32[]{:S(2)}, u32[]{:S(2)}) collective-permute-start(bf16[256,1792]{1,0:T(8,128)(2,1)} %pad_maximum_fusion.8), channel_id=1, source_target_pairs={{0,8},{4,12},{8,16},{12,20},{16,24},{20,28},{1,9},{5,13},{9,17},{1... | collective-permute-start | bytes 2752520 | tf_op jit(solution)/shard_map/ppermute | solution.py:439
  193.0 11.4 %add_convert_fusion.4 = (bf16[1024,1152]{1,0:T(8,128)(2,1)S(1)}, bf16[1024,1152]{1,0:T(8,128)(2,1)S(1)}) fusion(f32[1152]{0:T(1024)S(1)} %slice.228, bf16[1024,2048]{1,0:T(8,128)(2,1)} %norm_rows.7.left_a, bf16[2048,2304]{1,0:T(8,128)(2,1)} %all-gather.3.cloned.1.call-done), kind=kOutput, calls=%fused_computation.11 | convolution fusion | flops 4855431168 | bytes 13636096 | tf_op jit(solution)/shard_map/dot_general | solution.py:29
  204.4 5.8 %fusion.13.right_a = bf16[1024,1152]{1,0:T(8,128)(2,1)S(1)} fusion(bf16[1024,1152]{1,0:T(8,128)(2,1)S(1)} %get-tuple-element.162, bf16[1024,2048]{1,0:T(8,128)(2,1)S(1)} %copy-done.2, bf16[2048,2304]{1,0:T(8,128)(2,1)S(1)} %copy-done.74), kind=kOutput, calls=%fused_computation.22 | convolution fusion | flops 4835377152 | bytes 13631488 | tf_op jit(solution)/shard_map/dot_general | solution.py:29
  210.6 3.3 add_convert_fusion.11
  213.9 7.9 %weight_grads.7 = bf16[1024,2304]{1,0:T(8,128)(2,1)} custom-call(s32[1]{0:T(128)} %bitcast.9.at_ref, bf16[1024,2048]{1,0:T(8,128)(2,1)S(1)} %copy-done.7, bf16[1024,1152]{1,0:T(8,128)(2,1)S(1)} %fusion.13.right_a, bf16[1024,2048]{1,0:T(8,128)(2,1)S(1)} %copy-done.2, bf16[1024,1152]{1,0:T(8,128)(2,1)S(1)} %get-tuple-element.199.right_b), custom_call_target="tpu_custom_call" | custom-call | flops 4831838208 | bytes 13631488 | tf_op jit(solution)/shard_map/weight_grads/pallas_call | solution.py:330
  222.2 4.7 collective-permute-start.14
  237.5 6.9 %weight_grads.8 = bf16[1024,2304]{1,0:T(8,128)(2,1)S(1)} custom-call(s32[1]{0:T(128)} %bitcast.5.at_ref, bf16[1024,2048]{1,0:T(8,128)(2,1)S(1)} %copy-done.8, bf16[1024,1152]{1,0:T(8,128)(2,1)S(1)} %copy-done.28, bf16[1024,2048]{1,0:T(8,128)(2,1)S(1)} %copy-done.3, bf16[1024,1152]{1,0:T(8,128)(2,1)S(1)} %copy-done.35), custom_call_target="tpu_custom_call" | custom-call | flops 4831838208 | bytes 13631488 | tf_op jit(solution)/shard_map/weight_grads/pallas_call | solution.py:330
  244.4 8.7 %collective-permute-done.16 = bf16[256,1792]{1,0:T(8,128)(2,1)} collective-permute-done((bf16[256,1792]{1,0:T(8,128)(2,1)}, bf16[256,1792]{1,0:T(8,128)(2,1)}, u32[]{:S(2)}, u32[]{:S(2)}) %collective-permute-start.16) | collective-permute-done | bytes 917536 | tf_op jit(solution)/shard_map/ppermute | solution.py:439
  253.1 4.5 fusion.33
  260.6 11.4 %fusion.16 = bf16[1024,2048]{1,0:T(8,128)(2,1)} fusion(bf16[1024,1536]{1,0:T(8,128)(2,1)S(1)} %copy-done.13, bf16[2048,2048]{0,1:T(8,128)(2,1)} %all-gather.5.cloned.1.call-done), kind=kOutput, calls=%fused_computation.23 | convolution fusion | flops 6444548096 | bytes 13631488 | tf_op jit(solution)/shard_map/dot_general | solution.py:33
  272.0 5.9 %convolution_convert_fusion = bf16[1024,2048]{1,0:T(8,128)(2,1)} fusion(bf16[1024,512]{1,0:T(8,128)(2,1)S(1)} %copy-done.26, bf16[2048,2048]{0,1:T(8,128)(2,1)} %all-gather.5.cloned.1.call-done), kind=kOutput, calls=%fused_computation.24 | convolution fusion | flops 2149580800 | bytes 7340032 | tf_op jit(solution)/shard_map/dot_general | solution.py:33
  278.0 4.9 collective-permute-done.17
  286.8 3.2 pad_maximum_fusion.mine_ref
  293.5 3.5 collective-permute-start.24
  297.0 10.1 %add_convert_fusion.3 = bf16[1024,2048]{1,0:T(8,128)(2,1)} fusion(bf16[1024,2048]{1,0:T(8,128)(2,1)} %convolution_convert_fusion, bf16[1024,1152]{1,0:T(8,128)(2,1)S(1)} %copy-done.36, bf16[2048,2304]{1,0:T(8,128)(2,1)} %all-gather.3.cloned.1.call-done), kind=kOutput, calls=%fused_computation.3 | convolution fusion | flops 4838129664 | bytes 15466496 | tf_op jit(solution)/shard_map/dot_general | solution.py:33
  307.1 9.4 %collective-permute-done.20 = bf16[256,2048]{1,0:T(8,128)(2,1)S(1)} collective-permute-done((bf16[256,2048]{1,0:T(8,128)(2,1)}, bf16[256,2048]{1,0:T(8,128)(2,1)S(1)}, u32[]{:S(2)}, u32[]{:S(2)}) %collective-permute-start.20) | collective-permute-done | bytes 1048608 | tf_op jit(solution)/shard_map/ppermute | solution.py:401
  316.6 4.1 add_convert_fusion.9
  320.7 5.6 %collective-permute-start.22 = (bf16[256,2048]{1,0:T(8,128)(2,1)}, bf16[256,2048]{1,0:T(8,128)(2,1)S(1)}, u32[]{:S(2)}, u32[]{:S(2)}) collective-permute-start(bf16[256,2048]{1,0:T(8,128)(2,1)} %get-tuple-element.207), channel_id=1, source_target_pairs={{0,8},{4,12},{8,16},{12,20},{16,24},{20,28},{1,9},{5,13},{9,17},{1... | collective-permute-start | bytes 3145736 | tf_op jit(solution)/shard_map/ppermute | solution.py:401
  327.6 10.3 %weave.1 = bf16[2048,1792]{1,0:T(8,128)(2,1)} custom-call(s32[2]{0:T(128)} %pad_add_fusion.at_ref, bf16[1024,1792]{1,0:T(8,128)(2,1)} %pad_maximum_fusion.mine_ref, bf16[1024,1792]{1,0:T(8,128)(2,1)} %collective-permute-done.19.got_ref), custom_call_target="tpu_custom_call" | custom-call | bytes 22020096 | tf_op jit(solution)/shard_map/weave/pallas_call | solution.py:463
  337.9 9.8 %add_convert_fusion.5 = (bf16[1024,896]{1,0:T(8,128)(2,1)S(1)}, bf16[1024,896]{1,0:T(8,128)(2,1)S(1)}) fusion(f32[896]{0:T(1024)S(1)} %slice.233, bf16[1024,2048]{1,0:T(8,128)(2,1)} %norm_rows.7.left_a, bf16[2048,1792]{1,0:T(8,128)(2,1)} %weave.1), kind=kOutput, calls=%fused_computation.28 | convolution fusion | flops 3776446464 | bytes 11537920 | tf_op jit(solution)/shard_map/dot_general | solution.py:29
  347.7 4.5 multiply_convert_fusion.1.right_a
  352.2 11.6 %weight_grads.9 = bf16[2048,1792]{1,0:T(8,128)(2,1)S(1)} custom-call(s32[1]{0:T(128)} %constant.140.clone.1.at_ref, bf16[1024,2048]{1,0:T(8,128)(2,1)S(1)} %copy-done.9, bf16[1024,896]{1,0:T(8,128)(2,1)S(1)} %multiply_convert_fusion.1.right_a, bf16[1024,2048]{1,0:T(8,128)(2,1)S(1)} %copy-done.4, bf16[1024,896]{1,0:T(8,128)(2,1)S(1)} %get-tuple-element.221.right_b), custom_call_target="tpu_custom_call" | custom-call | flops 7516192768 | bytes 19398656 | tf_op jit(solution)/shard_map/weight_grads/pallas_call | solution.py:330
  363.8 3.0 copy-done.18
  366.9 5.2 fusion.31
  377.0 8.3 %add_convert_fusion.2 = bf16[1024,2048]{1,0:T(8,128)(2,1)S(1)} fusion(bf16[1024,2048]{1,0:T(8,128)(2,1)} %add_convert_fusion.3, bf16[1024,896]{1,0:T(8,128)(2,1)S(1)} %copy-done.38, bf16[2048,1792]{1,0:T(8,128)(2,1)} %weave.1), kind=kOutput, calls=%fused_computation.2 | convolution fusion | flops 3764387840 | bytes 13893632 | tf_op jit(solution)/shard_map/dot_general | solution.py:33
  385.3 5.6 %collective-permute-start.29 = (bf16[256,2304]{1,0:T(8,128)(2,1)}, bf16[256,2304]{1,0:T(8,128)(2,1)}, u32[]{:S(2)}, u32[]{:S(2)}) collective-permute-start(bf16[256,2304]{1,0:T(8,128)(2,1)} %get-tuple-element.230), channel_id=1, source_target_pairs={{0,8},{4,12},{8,16},{12,20},{1,9},{5,13},{9,17},{13,21},{2,10},{6,... | collective-permute-start | bytes 3538952 | tf_op jit(solution)/shard_map/ppermute | solution.py:401
  396.0 8.1 %fusion.10 = f32[1024,2048]{1,0:T(8,128)} fusion(bf16[1024,1152]{1,0:T(8,128)(2,1)S(1)} %copy-done.29, bf16[2048,2304]{1,0:T(8,128)(2,1)S(1)} %bitcast.100), kind=kOutput, calls=%fused_computation.19 | convolution fusion | flops 4831838208 | bytes 15466496 | tf_op jit(solution)/shard_map/dot_general | solution.py:33
  404.1 8.8 %add_convert_fusion.refs_5_ = bf16[1024,2048]{1,0:T(8,128)(2,1)S(1)} fusion(f32[1024,2048]{1,0:T(8,128)} %fusion.10, bf16[1024,2048]{1,0:T(8,128)(2,1)} %fusion.16, bf16[1024,896]{1,0:T(8,128)(2,1)S(1)} %multiply_convert_fusion.1.right_a, bf16[2048,1792]{1,0:T(8,128)(2,1)} %weave.1), kind=kOutput, calls=%fused_computation | convolution fusion | flops 3770679296 | bytes 22282240 | tf_op jit(solution)/shard_map/dot_general | solution.py:33
  425.7 15.5 %collective-permute-done.29 = bf16[256,2304]{1,0:T(8,128)(2,1)} collective-permute-done((bf16[256,2304]{1,0:T(8,128)(2,1)}, bf16[256,2304]{1,0:T(8,128)(2,1)}, u32[]{:S(2)}, u32[]{:S(2)}) %collective-permute-start.29) | collective-permute-done | bytes 1179680 | tf_op jit(solution)/shard_map/ppermute | solution.py:401
  442.9 3.2 add_convert_fusion.6
  446.1 4.1 norm_sums.1
  456.1 6.1 %collective-permute-start.31 = (bf16[256,2304]{1,0:T(8,128)(2,1)S(1)}, bf16[256,2304]{1,0:T(8,128)(2,1)S(1)}, u32[]{:S(2)}, u32[]{:S(2)}) collective-permute-start(bf16[256,2304]{1,0:T(8,128)(2,1)S(1)} %get-tuple-element.236), channel_id=1, source_target_pairs={{0,8},{4,12},{8,16},{12,20},{16,24},{20,28},{1,9},{5,13},{9,17},{1... | collective-permute-start | bytes 3538952 | tf_op jit(solution)/shard_map/ppermute | solution.py:401
  476.6 3.0 collective-permute-done.36
  479.6 18.3 %collective-permute-done.31 = bf16[256,2304]{1,0:T(8,128)(2,1)S(1)} collective-permute-done((bf16[256,2304]{1,0:T(8,128)(2,1)S(1)}, bf16[256,2304]{1,0:T(8,128)(2,1)S(1)}, u32[]{:S(2)}, u32[]{:S(2)}) %collective-permute-start.31) | collective-permute-done | bytes 1179680 | tf_op jit(solution)/shard_map/ppermute | solution.py:401
  507.6 3.8 collective-permute-start.40
  (381 shorter events, 155.3 us)
Async XLA Ops:
  7.2 93.5 %all-gather.5.cloned.1.call-start = ((), (), s32[]{:S(2)}) async-start(), calls=%async_computation.2 | async-start | bytes 9437184 | tf_op jit(solution)/shard_map/all_gather | solution.py:639
  12.8 180.1 %all-gather.3.cloned.1.call-start = ((), (), s32[]{:S(2)}) async-start(), calls=%async_computation.1 | async-start | bytes 10616832 | tf_op jit(solution)/shard_map/all_gather | solution.py:652
  13.4 4.6 collective-permute-start.2
  13.9 27.0 %collective-permute-start.1 = (bf16[256,2048]{1,0:T(8,128)(2,1)S(1)}, bf16[256,2048]{1,0:T(8,128)(2,1)S(1)}, u32[]{:S(2)}, u32[]{:S(2)}) collective-permute-start(bf16[256,2048]{1,0:T(8,128)(2,1)S(1)} %copy-done.10), channel_id=1, source_target_pairs={{0,2},{1,3},{2,0},{3,1},{4,6},{5,7},{6,4},{7,5},{8,10},{9,11},{10,... | collective-permute-start | bytes 3145736 | tf_op jit(solution)/shard_map/ppermute | solution.py:645
  16.5 25.2 %collective-permute-start = (bf16[256,2048]{1,0:T(8,128)(2,1)S(1)}, bf16[256,2048]{1,0:T(8,128)(2,1)S(1)}, u32[]{:S(2)}, u32[]{:S(2)}) collective-permute-start(bf16[256,2048]{1,0:T(8,128)(2,1)S(1)} %copy-done.10), channel_id=1, source_target_pairs={{0,1},{1,0},{2,3},{3,2},{4,5},{5,4},{6,7},{7,6},{8,9},{9,8},{10,11... | collective-permute-start | bytes 3145736 | tf_op jit(solution)/shard_map/ppermute | solution.py:645
  18.1 7.0 %collective-permute-start.3 = (bf16[8,1472]{1,0:T(8,128)(2,1)S(1)}, bf16[8,1472]{1,0:T(8,128)(2,1)S(1)}, u32[]{:S(2)}, u32[]{:S(2)}) collective-permute-start(bf16[8,1472]{1,0:T(8,128)(2,1)S(1)} %fusion.57), channel_id=1, source_target_pairs={{0,8},{4,12},{8,0},{12,4},{16,24},{20,28},{24,16},{28,20},{1,9},{5... | collective-permute-start | bytes 70664 | tf_op jit(solution)/shard_map/ppermute | solution.py:556
  25.2 15.7 %collective-permute-start.4 = (bf16[8,1472]{1,0:T(8,128)(2,1)S(1)}, bf16[8,1472]{1,0:T(8,128)(2,1)S(1)}, u32[]{:S(2)}, u32[]{:S(2)}) collective-permute-start(bf16[8,1472]{1,0:T(8,128)(2,1)S(1)} %fusion.83), channel_id=1, source_target_pairs={{0,16},{4,20},{8,24},{12,28},{16,0},{20,4},{24,8},{28,12},{1,17},{... | collective-permute-start | bytes 70664 | tf_op jit(solution)/shard_map/ppermute | solution.py:556
  40.9 129.9 %copy-start.65 = (bf16[8,1472]{1,0:T(8,128)(2,1)}, bf16[8,1472]{1,0:T(8,128)(2,1)S(1)}, u32[]{:S(2)}) copy-start(bf16[8,1472]{1,0:T(8,128)(2,1)S(1)} %add.390) | copy-start | bytes 70660
  41.7 460.2 %reduce-scatter.2.cloned.1.call-start = ((), (), s32[]{:S(2)}) async-start(), calls=%async_computation.3 | async-start | bytes 8257536 | tf_op jit(solution)/shard_map/reduce_scatter | solution.py:728
  41.8 26.4 %collective-permute-start.8 = (bf16[256,2048]{1,0:T(8,128)(2,1)}, bf16[256,2048]{1,0:T(8,128)(2,1)}, u32[]{:S(2)}, u32[]{:S(2)}) collective-permute-start(bf16[256,2048]{1,0:T(8,128)(2,1)} %refs_1_.1), channel_id=1, source_target_pairs={{0,2},{1,3},{2,0},{3,1},{4,6},{5,7},{6,4},{7,5},{8,10},{9,11},{10,... | collective-permute-start | bytes 3145736 | tf_op jit(solution)/shard_map/ppermute | solution.py:645
  42.5 26.3 %collective-permute-start.7 = (bf16[256,2048]{1,0:T(8,128)(2,1)}, bf16[256,2048]{1,0:T(8,128)(2,1)}, u32[]{:S(2)}, u32[]{:S(2)}) collective-permute-start(bf16[256,2048]{1,0:T(8,128)(2,1)} %refs_1_.1), channel_id=1, source_target_pairs={{0,1},{1,0},{2,3},{3,2},{4,5},{5,4},{6,7},{7,6},{8,9},{9,8},{10,11... | collective-permute-start | bytes 3145736 | tf_op jit(solution)/shard_map/ppermute | solution.py:645
  49.5 35.8 %collective-permute-start.6 = (bf16[256,1024]{1,0:T(8,128)(2,1)}, bf16[256,1024]{1,0:T(8,128)(2,1)S(1)}, u32[]{:S(2)}, u32[]{:S(2)}) collective-permute-start(bf16[256,1024]{1,0:T(8,128)(2,1)} %slice.203), channel_id=1, source_target_pairs={{0,1},{1,0},{2,3},{3,2},{4,5},{5,4},{6,7},{7,6},{8,9},{9,8},{10,11... | collective-permute-start | bytes 1572872 | tf_op jit(solution)/shard_map/ppermute | solution.py:645
  50.1 35.2 %collective-permute-start.5 = (bf16[256,1024]{1,0:T(8,128)(2,1)}, bf16[256,1024]{1,0:T(8,128)(2,1)S(1)}, u32[]{:S(2)}, u32[]{:S(2)}) collective-permute-start(bf16[256,1024]{1,0:T(8,128)(2,1)} %slice.202), channel_id=1, source_target_pairs={{0,2},{1,3},{2,0},{3,1},{4,6},{5,7},{6,4},{7,5},{8,10},{9,11},{10,... | collective-permute-start | bytes 1572872 | tf_op jit(solution)/shard_map/ppermute | solution.py:645
  72.5 16.8 %collective-permute-start.10 = (bf16[256,1024]{1,0:T(8,128)(2,1)}, bf16[256,1024]{1,0:T(8,128)(2,1)S(1)}, u32[]{:S(2)}, u32[]{:S(2)}) collective-permute-start(bf16[256,1024]{1,0:T(8,128)(2,1)} %slice.207), channel_id=1, source_target_pairs={{0,1},{1,0},{2,3},{3,2},{4,5},{5,4},{6,7},{7,6},{8,9},{9,8},{10,11... | collective-permute-start | bytes 1572872 | tf_op jit(solution)/shard_map/ppermute | solution.py:645
  73.9 15.4 %collective-permute-start.9 = (bf16[256,1024]{1,0:T(8,128)(2,1)}, bf16[256,1024]{1,0:T(8,128)(2,1)}, u32[]{:S(2)}, u32[]{:S(2)}) collective-permute-start(bf16[256,1024]{1,0:T(8,128)(2,1)} %slice.206), channel_id=1, source_target_pairs={{0,2},{1,3},{2,0},{3,1},{4,6},{5,7},{6,4},{7,5},{8,10},{9,11},{10,... | collective-permute-start | bytes 1572872 | tf_op jit(solution)/shard_map/ppermute | solution.py:645
  134.1 26.6 %copy-start.5 = (bf16[1024,2048]{1,0:T(8,128)(2,1)S(1)}, bf16[1024,2048]{1,0:T(8,128)(2,1)}, u32[]{:S(2)}) copy-start(bf16[1024,2048]{1,0:T(8,128)(2,1)} %norm_rows.7.left_a) | copy-start | bytes 12582916
  170.7 40.0 %collective-permute-start.11 = (bf16[1024,2048]{1,0:T(8,128)(2,1)}, bf16[1024,2048]{1,0:T(8,128)(2,1)}, u32[]{:S(2)}, u32[]{:S(2)}) collective-permute-start(bf16[1024,2048]{1,0:T(8,128)(2,1)} %weight_grads.5), channel_id=1, source_target_pairs={{0,4},{4,0},{8,12},{12,8},{16,20},{20,16},{24,28},{28,24},{1,5},{5... | collective-permute-start | bytes 12582920 | tf_op jit(solution)/shard_map/ppermute | solution.py:369
  184.6 26.0 %collective-permute-start.13 = (bf16[256,1792]{1,0:T(8,128)(2,1)}, bf16[256,1792]{1,0:T(8,128)(2,1)}, u32[]{:S(2)}, u32[]{:S(2)}) collective-permute-start(bf16[256,1792]{1,0:T(8,128)(2,1)} %pad_maximum_fusion.8), channel_id=1, source_target_pairs={{28,20},{24,16},{20,12},{16,8},{12,4},{8,0},{29,21},{25,17},{21,13... | collective-permute-start | bytes 2752520 | tf_op jit(solution)/shard_map/ppermute | solution.py:439
  185.9 24.8 %collective-permute-start.12 = (bf16[256,1792]{1,0:T(8,128)(2,1)}, bf16[256,1792]{1,0:T(8,128)(2,1)}, u32[]{:S(2)}, u32[]{:S(2)}) collective-permute-start(bf16[256,1792]{1,0:T(8,128)(2,1)} %pad_maximum_fusion.8), channel_id=1, source_target_pairs={{0,8},{4,12},{8,16},{12,20},{16,24},{20,28},{1,9},{5,13},{9,17},{1... | collective-permute-start | bytes 2752520 | tf_op jit(solution)/shard_map/ppermute | solution.py:439
  221.9 61.0 %collective-permute-start.18 = (bf16[1024,2304]{1,0:T(8,128)(2,1)}, bf16[1024,2304]{1,0:T(8,128)(2,1)}, u32[]{:S(2)}, u32[]{:S(2)}) collective-permute-start(bf16[1024,2304]{1,0:T(8,128)(2,1)} %weight_grads.7), channel_id=1, source_target_pairs={{0,4},{4,0},{8,12},{12,8},{16,20},{20,16},{24,28},{28,24},{1,5},{5... | collective-permute-start | bytes 14155784 | tf_op jit(solution)/shard_map/ppermute | solution.py:369
  222.2 31.0 %collective-permute-start.14 = (bf16[256,2048]{1,0:T(8,128)(2,1)}, bf16[256,2048]{1,0:T(8,128)(2,1)}, u32[]{:S(2)}, u32[]{:S(2)}) collective-permute-start(bf16[256,2048]{1,0:T(8,128)(2,1)} %add_convert_fusion.11), channel_id=1, source_target_pairs={{0,8},{4,12},{28,20},{24,16},{1,9},{5,13},{29,21},{25,17},{2,10},{... | collective-permute-start | bytes 3145736 | tf_op jit(solution)/shard_map/ppermute | solution.py:399
  226.9 17.6 %collective-permute-start.15 = (bf16[256,1792]{1,0:T(8,128)(2,1)}, bf16[256,1792]{1,0:T(8,128)(2,1)}, u32[]{:S(2)}, u32[]{:S(2)}) collective-permute-start(bf16[256,1792]{1,0:T(8,128)(2,1)} %collective-permute-done.12), channel_id=1, source_target_pairs={{8,16},{12,20},{16,24},{20,28},{9,17},{13,21},{17,25},{21,29},{10,... | collective-permute-start | bytes 2752520 | tf_op jit(solution)/shard_map/ppermute | solution.py:439
  228.4 24.7 %collective-permute-start.16 = (bf16[256,1792]{1,0:T(8,128)(2,1)}, bf16[256,1792]{1,0:T(8,128)(2,1)}, u32[]{:S(2)}, u32[]{:S(2)}) collective-permute-start(bf16[256,1792]{1,0:T(8,128)(2,1)} %collective-permute-done.13), channel_id=1, source_target_pairs={{20,12},{16,8},{12,4},{8,0},{21,13},{17,9},{13,5},{9,1},{22,14},{1... | collective-permute-start | bytes 2752520 | tf_op jit(solution)/shard_map/ppermute | solution.py:439
  244.4 38.5 %copy-start.17 = (bf16[1024,2304]{1,0:T(8,128)(2,1)}, bf16[1024,2304]{1,0:T(8,128)(2,1)S(1)}, u32[]{:S(2)}) copy-start(bf16[1024,2304]{1,0:T(8,128)(2,1)S(1)} %weight_grads.8) | copy-start | bytes 14155780
  259.2 23.6 %collective-permute-start.17 = (bf16[256,1792]{1,0:T(8,128)(2,1)S(1)}, bf16[256,1792]{1,0:T(8,128)(2,1)S(1)}, u32[]{:S(2)}, u32[]{:S(2)}) collective-permute-start(bf16[256,1792]{1,0:T(8,128)(2,1)S(1)} %get-tuple-element.184), channel_id=1, source_target_pairs={{16,24},{20,28},{12,4},{8,0},{17,25},{21,29},{13,5},{9,1},{18,26},... | collective-permute-start | bytes 2752520 | tf_op jit(solution)/shard_map/ppermute | solution.py:437
  290.0 26.6 %collective-permute-start.19 = (bf16[1024,1792]{1,0:T(8,128)(2,1)}, bf16[1024,1792]{1,0:T(8,128)(2,1)}, u32[]{:S(2)}, u32[]{:S(2)}) collective-permute-start(bf16[1024,1792]{1,0:T(8,128)(2,1)} %pad_maximum_fusion.mine_ref), channel_id=1, source_target_pairs={{0,4},{4,0},{8,12},{12,8},{16,20},{20,16},{24,28},{28,24},{1,5},{5... | collective-permute-start | bytes 11010056 | tf_op jit(solution)/shard_map/ppermute | solution.py:432
  290.7 25.8 %collective-permute-start.20 = (bf16[256,2048]{1,0:T(8,128)(2,1)}, bf16[256,2048]{1,0:T(8,128)(2,1)S(1)}, u32[]{:S(2)}, u32[]{:S(2)}) collective-permute-start(bf16[256,2048]{1,0:T(8,128)(2,1)} %get-tuple-element.196), channel_id=1, source_target_pairs={{0,8},{4,12},{8,16},{12,20},{1,9},{5,13},{9,17},{13,21},{2,10},{6,... | collective-permute-start | bytes 3145736 | tf_op jit(solution)/shard_map/ppermute | solution.py:401
  292.8 23.8 %collective-permute-start.21 = (bf16[256,2048]{1,0:T(8,128)(2,1)S(1)}, bf16[256,2048]{1,0:T(8,128)(2,1)S(1)}, u32[]{:S(2)}, u32[]{:S(2)}) collective-permute-start(bf16[256,2048]{1,0:T(8,128)(2,1)S(1)} %copy-done.50), channel_id=1, source_target_pairs={{28,20},{24,16},{20,12},{16,8},{29,21},{25,17},{21,13},{17,9},{30,... | collective-permute-start | bytes 3145736 | tf_op jit(solution)/shard_map/ppermute | solution.py:401
  293.5 73.3 %collective-permute-start.24 = (bf16[256,2304]{1,0:T(8,128)(2,1)}, bf16[256,2304]{1,0:T(8,128)(2,1)}, u32[]{:S(2)}, u32[]{:S(2)}) collective-permute-start(bf16[256,2304]{1,0:T(8,128)(2,1)} %add_convert_fusion.8), channel_id=1, source_target_pairs={{0,8},{4,12},{28,20},{24,16},{1,9},{5,13},{29,21},{25,17},{2,10},{... | collective-permute-start | bytes 3538952 | tf_op jit(solution)/shard_map/ppermute | solution.py:399
  320.7 46.1 %collective-permute-start.22 = (bf16[256,2048]{1,0:T(8,128)(2,1)}, bf16[256,2048]{1,0:T(8,128)(2,1)S(1)}, u32[]{:S(2)}, u32[]{:S(2)}) collective-permute-start(bf16[256,2048]{1,0:T(8,128)(2,1)} %get-tuple-element.207), channel_id=1, source_target_pairs={{0,8},{4,12},{8,16},{12,20},{16,24},{20,28},{1,9},{5,13},{9,17},{1... | collective-permute-start | bytes 3145736 | tf_op jit(solution)/shard_map/ppermute | solution.py:401
  326.3 40.5 %collective-permute-start.23 = (bf16[256,2048]{1,0:T(8,128)(2,1)}, bf16[256,2048]{1,0:T(8,128)(2,1)}, u32[]{:S(2)}, u32[]{:S(2)}) collective-permute-start(bf16[256,2048]{1,0:T(8,128)(2,1)} %get-tuple-element.208), channel_id=1, source_target_pairs={{28,20},{24,16},{20,12},{16,8},{12,4},{8,0},{29,21},{25,17},{21,13... | collective-permute-start | bytes 3145736 | tf_op jit(solution)/shard_map/ppermute | solution.py:401
  385.3 55.9 %collective-permute-start.29 = (bf16[256,2304]{1,0:T(8,128)(2,1)}, bf16[256,2304]{1,0:T(8,128)(2,1)}, u32[]{:S(2)}, u32[]{:S(2)}) collective-permute-start(bf16[256,2304]{1,0:T(8,128)(2,1)} %get-tuple-element.230), channel_id=1, source_target_pairs={{0,8},{4,12},{8,16},{12,20},{1,9},{5,13},{9,17},{13,21},{2,10},{6,... | collective-permute-start | bytes 3538952 | tf_op jit(solution)/shard_map/ppermute | solution.py:401
  390.8 52.0 %collective-permute-start.30 = (bf16[256,2304]{1,0:T(8,128)(2,1)}, bf16[256,2304]{1,0:T(8,128)(2,1)}, u32[]{:S(2)}, u32[]{:S(2)}) collective-permute-start(bf16[256,2304]{1,0:T(8,128)(2,1)} %get-tuple-element.231), channel_id=1, source_target_pairs={{28,20},{24,16},{20,12},{16,8},{29,21},{25,17},{21,13},{17,9},{30,... | collective-permute-start | bytes 3538952 | tf_op jit(solution)/shard_map/ppermute | solution.py:401
  392.8 24.6 %collective-permute-start.25 = (bf16[512,1024]{1,0:T(8,128)(2,1)S(1)}, bf16[512,1024]{1,0:T(8,128)(2,1)S(1)}, u32[]{:S(2)}, u32[]{:S(2)}) collective-permute-start(bf16[512,1024]{1,0:T(8,128)(2,1)S(1)} %pad_maximum_fusion.4), channel_id=1, source_target_pairs={{0,1},{1,0},{2,3},{3,2},{4,5},{5,4},{6,7},{7,6},{8,9},{9,8},{10,11... | collective-permute-start | bytes 3145736 | tf_op jit(solution)/shard_map/ppermute | solution.py:524
  394.5 24.1 %collective-permute-start.26 = (bf16[512,1024]{1,0:T(8,128)(2,1)S(1)}, bf16[512,1024]{1,0:T(8,128)(2,1)}, u32[]{:S(2)}, u32[]{:S(2)}) collective-permute-start(bf16[512,1024]{1,0:T(8,128)(2,1)S(1)} %pad_maximum_fusion.5), channel_id=1, source_target_pairs={{0,2},{1,3},{2,0},{3,1},{4,6},{5,7},{6,4},{7,5},{8,10},{9,11},{10,... | collective-permute-start | bytes 3145736 | tf_op jit(solution)/shard_map/ppermute | solution.py:524
  419.1 31.1 %collective-permute-start.33 = (bf16[512,1024]{1,0:T(8,128)(2,1)S(1)}, bf16[512,1024]{1,0:T(8,128)(2,1)S(1)}, u32[]{:S(2)}, u32[]{:S(2)}) collective-permute-start(bf16[512,1024]{1,0:T(8,128)(2,1)S(1)} %pad_maximum_fusion.6), channel_id=1, source_target_pairs={{0,1},{1,0},{2,3},{3,2},{4,5},{5,4},{6,7},{7,6},{8,9},{9,8},{10,11... | collective-permute-start | bytes 3145736 | tf_op jit(solution)/shard_map/ppermute | solution.py:524
  419.6 30.6 %collective-permute-start.34 = (bf16[512,1024]{1,0:T(8,128)(2,1)S(1)}, bf16[512,1024]{1,0:T(8,128)(2,1)S(1)}, u32[]{:S(2)}, u32[]{:S(2)}) collective-permute-start(bf16[512,1024]{1,0:T(8,128)(2,1)S(1)} %pad_maximum_fusion.7), channel_id=1, source_target_pairs={{0,2},{1,3},{2,0},{3,1},{4,6},{5,7},{6,4},{7,5},{8,10},{9,11},{10,... | collective-permute-start | bytes 3145736 | tf_op jit(solution)/shard_map/ppermute | solution.py:524
  424.4 37.9 %collective-permute-start.28 = (bf16[256,1024]{1,0:T(8,128)(2,1)}, bf16[256,1024]{1,0:T(8,128)(2,1)S(1)}, u32[]{:S(2)}, u32[]{:S(2)}) collective-permute-start(bf16[256,1024]{1,0:T(8,128)(2,1)} %get-tuple-element.318), channel_id=1, source_target_pairs={{0,1},{1,0},{2,3},{3,2},{4,5},{5,4},{6,7},{7,6},{8,9},{9,8},{10,11... | collective-permute-start | bytes 1572872 | tf_op jit(solution)/shard_map/ppermute | solution.py:536
  441.2 22.6 %collective-permute-start.27 = (bf16[256,1024]{1,0:T(8,128)(2,1)}, bf16[256,1024]{1,0:T(8,128)(2,1)}, u32[]{:S(2)}, u32[]{:S(2)}) collective-permute-start(bf16[256,1024]{1,0:T(8,128)(2,1)} %get-tuple-element.319), channel_id=1, source_target_pairs={{0,2},{1,3},{2,0},{3,1},{4,6},{5,7},{6,4},{7,5},{8,10},{9,11},{10,... | collective-permute-start | bytes 1572872 | tf_op jit(solution)/shard_map/ppermute | solution.py:536
  453.3 12.3 %collective-permute-start.38 = (bf16[256,1024]{1,0:T(8,128)(2,1)S(1)}, bf16[256,1024]{1,0:T(8,128)(2,1)S(1)}, u32[]{:S(2)}, u32[]{:S(2)}) collective-permute-start(bf16[256,1024]{1,0:T(8,128)(2,1)S(1)} %get-tuple-element.310), channel_id=1, source_target_pairs={{0,1},{1,0},{2,3},{3,2},{4,5},{5,4},{6,7},{7,6},{8,9},{9,8},{10,11... | collective-permute-start | bytes 1572872 | tf_op jit(solution)/shard_map/ppermute | solution.py:536
  454.8 12.0 %collective-permute-start.37 = (bf16[256,1024]{1,0:T(8,128)(2,1)S(1)}, bf16[256,1024]{1,0:T(8,128)(2,1)S(1)}, u32[]{:S(2)}, u32[]{:S(2)}) collective-permute-start(bf16[256,1024]{1,0:T(8,128)(2,1)S(1)} %get-tuple-element.311), channel_id=1, source_target_pairs={{0,2},{1,3},{2,0},{3,1},{4,6},{5,7},{6,4},{7,5},{8,10},{9,11},{10,... | collective-permute-start | bytes 1572872 | tf_op jit(solution)/shard_map/ppermute | solution.py:536
  456.1 41.8 %collective-permute-start.31 = (bf16[256,2304]{1,0:T(8,128)(2,1)S(1)}, bf16[256,2304]{1,0:T(8,128)(2,1)S(1)}, u32[]{:S(2)}, u32[]{:S(2)}) collective-permute-start(bf16[256,2304]{1,0:T(8,128)(2,1)S(1)} %get-tuple-element.236), channel_id=1, source_target_pairs={{0,8},{4,12},{8,16},{12,20},{16,24},{20,28},{1,9},{5,13},{9,17},{1... | collective-permute-start | bytes 3538952 | tf_op jit(solution)/shard_map/ppermute | solution.py:401
  462.3 36.0 %collective-permute-start.32 = (bf16[256,2304]{1,0:T(8,128)(2,1)S(1)}, bf16[256,2304]{1,0:T(8,128)(2,1)S(1)}, u32[]{:S(2)}, u32[]{:S(2)}) collective-permute-start(bf16[256,2304]{1,0:T(8,128)(2,1)S(1)} %get-tuple-element.237), channel_id=1, source_target_pairs={{28,20},{24,16},{20,12},{16,8},{12,4},{8,0},{29,21},{25,17},{21,13... | collective-permute-start | bytes 3538952 | tf_op jit(solution)/shard_map/ppermute | solution.py:401
  471.9 3.8 collective-permute-start.35
  475.8 3.8 collective-permute-start.36
  506.3 1.2 collective-permute-start.39
  507.6 5.8 %collective-permute-start.40 = (f32[76,128]{1,0:T(8,128)S(1)}, f32[76,128]{1,0:T(8,128)S(1)}, u32[]{:S(2)}, u32[]{:S(2)}) collective-permute-start(f32[76,128]{1,0:T(8,128)S(1)} %add.470), channel_id=1, source_target_pairs={{0,8},{4,12},{8,0},{12,4},{16,24},{20,28},{24,16},{28,20},{1,9},{5... | collective-permute-start | bytes 116744 | tf_op jit(solution)/shard_map/ppermute | solution.py:556
  513.3 6.2 %collective-permute-start.41 = (f32[76,128]{1,0:T(8,128)S(1)}, f32[76,128]{1,0:T(8,128)S(1)}, u32[]{:S(2)}, u32[]{:S(2)}) collective-permute-start(f32[76,128]{1,0:T(8,128)S(1)} %add.471), channel_id=1, source_target_pairs={{0,16},{4,20},{8,24},{12,28},{16,0},{20,4},{24,8},{28,12},{1,17},{... | collective-permute-start | bytes 116744 | tf_op jit(solution)/shard_map/ppermute | solution.py:556
  (78 other events, 499.1 us)
Sparse Core Ops, SparseCore 0:
  13.0 87.7 all-gather.4
  102.9 89.9 all-gather.2
  372.3 117.9 reduce-scatter.1

commit v4 on v3

--- a/solution.py
+++ b/solution.py
@@ -723,13 +723,14 @@
         normed, grad_all = advance([gather], normed, grad_all)
     w_up, w_down_t, act, back = forward(gather.full, edges[1], edges[2])
     up_pre_grad = (product(grad_all, w_down_t) * back.astype(F32)).astype(BF16)
+    up_pre_grad, act, grad_all = advance([line], up_pre_grad, act, grad_all)
     far_grad = natural_grads(normed, up_pre_grad, grad_all, act)
-    far_grad, act, up_pre_grad, near_grad = advance(lines, far_grad, act, up_pre_grad, near_grad)
+    far_grad, act, up_pre_grad, near_grad = advance([attn_line], far_grad, act, up_pre_grad, near_grad)
     far_shard = lax.psum_scatter(far_grad, "dp", scatter_dimension=0, tiled=True)
     branch_low = plus(branch, act, w_down_t)
 
     output_sum = TensorScatter(branch_low, tok_rows)
-    near_grad, branch_low = tie(near_grad, branch_low)
+    near_grad, branch_low = advance([line], near_grad, branch_low)
     normed_grad_low = plus(plus(normed_grad, near_grad, near_up), up_pre_grad, w_up)
     (normed_grad_low,) = output_sum.second(normed_grad_low)
     up_bias_grads = [jnp.sum(item, axis=0, dtype=F32) for item in (near_grad, up_pre_grad)]

time: 538 us -> 565 us (1.050)
  waiting for transfers between devices: 97.5 us -> 118 us
    ppermute x12, waiting for transfers between devices: 52.7 us -> 70.9 us  [send(): lax.ppermute(item, 'dp', way)]
    ppermute x4, waiting for transfers between devices: 1.37 us -> 8.63 us  [second(): lax.ppermute(far, 'tensor', swap_pairs(self.count, 3 - flip))]
    unnamed x194 -> x190, local copies, waits for them, and re-layouts: 36.4 us -> 36 us
  transfers between devices with their start and end apart: 45 -> 45, of which waited for: 20 -> 18; matrix products, arithmetic and copies ran while one was open for 31% -> 31% of each run, Pallas kernels for 21% -> 20%
where the time goes in v4:
time: 565 us; the launch traced here: 556 us
  waiting for transfers between devices  118 us (21%)
  Pallas kernels  118 us (21%)
  matrix products  102 us (18%)
  starting transfers between devices  80.8 us (14%)
  other arithmetic  65.3 us (12%)
  local copies, waits for them, and re-layouts  55.1 us (10%)
  between operations  16.3 us (3%)
    ppermute x12, waiting for transfers between devices, send(): lax.ppermute(item, 'dp', way)  70.9 us
    dot_general x6, matrix products, times_trans(): lax.dot_general(left, right, (((1,), (1,)), ((), ())), preferred_element_...  54 us
    dot_general x6, matrix products, product(): return jnp.dot(left, right, preferred_element_type=F32)  48.1 us
    pallas_call x5, Pallas kernels, weight_grads(): pl.pallas_call(weight_kernel, grid_spec=pltpu.PrefetchScalarGridSpec(num_...  38.9 us
    unnamed x190, local copies, waits for them, and re-layouts  36 us
    ppermute x12, starting transfers between devices, send(): lax.ppermute(item, 'dp', way)  35.8 us
    pallas_call x1, Pallas kernels, attention_backward(): pl.pallas_call(attn_bwd_kernel, grid=(pairs,), in_specs=[pl.BlockSpec(mem...  26.7 us
    convert_element_type x6, other arithmetic, next_sends(): (sent if item is None else sent + item.astype(F32)).astype(BF16)  22.2 us
  transfers between devices with their start and end apart: 45, of which 18 were waited for; matrix products, arithmetic and copies ran while one was open for 31% of the time, Pallas kernels for 20%

profile of v4, /device:TPU:0, one launch (start us, length us, event | category | flops | bytes accessed | tf_op | source)
XLA Modules:
  0.0 555.5 jit_solution(1904807638015284680)
XLA Ops:
  29.9 10.9 %collective-permute-done.4 = bf16[8,1472]{1,0:T(8,128)(2,1)S(1)} collective-permute-done((bf16[8,1472]{1,0:T(8,128)(2,1)S(1)}, bf16[8,1472]{1,0:T(8,128)(2,1)S(1)}, u32[]{:S(2)}, u32[]{:S(2)}) %collective-permute-start.4) | collective-permute-done | bytes 23584 | tf_op jit(solution)/shard_map/ppermute | solution.py:556
  51.5 3.0 norm_rows.4.refs_3_
  54.5 3.0 norm_rows.5.refs_3_
  57.5 3.0 norm_rows.6.refs_4_
  60.4 7.7 %collective-permute-done.8.refs_0_ = bf16[256,2048]{1,0:T(8,128)(2,1)} collective-permute-done((bf16[256,2048]{1,0:T(8,128)(2,1)}, bf16[256,2048]{1,0:T(8,128)(2,1)}, u32[]{:S(2)}, u32[]{:S(2)}) %collective-permute-start.8) | collective-permute-done | bytes 1048608 | tf_op jit(solution)/shard_map/ppermute | solution.py:645
  86.2 3.0 norm_rows.7.left_a
  92.4 8.3 %all-gather.5.cloned.1.call-done = bf16[2048,2048]{0,1:T(8,128)(2,1)} async-done(((bf16[256,2048]{0,1:T(8,128)(2,1)}), bf16[2048,2048]{0,1:T(8,128)(2,1)}) %all-gather.5.cloned.1.call-update) | async-done | bytes 8388624 | tf_op jit(solution)/shard_map/all_gather | solution.py:639
  100.7 12.0 %fusion.4.qkv_ref = f32[1024,1536]{1,0:T(8,128)} fusion(bf16[1024,2048]{1,0:T(8,128)(2,1)} %norm_rows.7.left_a, bf16[2048,2048]{0,1:T(8,128)(2,1)} %all-gather.5.cloned.1.call-done, f32[1536]{0:T(1024)S(1)} %reshape.189), kind=kOutput, calls=%fused_computation.15 | convolution fusion | flops 6444023808 | bytes 16783360 | tf_op jit(solution)/shard_map/dot_general | solution.py:29
  112.7 16.6 %attn_fwd.1 = (bf16[1024,512]{1,0:T(8,128)(2,1)S(1)}, bf16[1024,512]{1,0:T(8,128)(2,1)S(1)}, bf16[1024,512]{1,0:T(8,128)(2,1)S(1)}, bf16[1024,512]{1,0:T(8,128)(2,1)S(1)}, f32[1024,512]{1,0:T(8,128)}) custom-call(s32[1]{0:T(128)} %copy.131.len_ref, f32[1024,1536]{1,0:T(8,128)} %fusion.4.qkv_ref, f32[1024,128]{1,0:T(8,128)S(1)} %get-tuple-element.379.keep_ref, ...), custom_call_target="tpu_custom_call" | custom-call | flops 6442450944 | bytes 12582912 | tf_op jit(solution)/shard_map/attn_fwd/pallas_call | solution.py:189
  129.3 4.4 fusion.44.grad_ref
  133.7 26.7 %attn_bwd.1.right_a = bf16[1024,1536]{1,0:T(8,128)(2,1)} custom-call(s32[1]{0:T(128)} %copy.131.len_ref, bf16[1024,512]{1,0:T(8,128)(2,1)S(1)} %get-tuple-element.152.q_ref, bf16[1024,512]{1,0:T(8,128)(2,1)S(1)} %get-tuple-element.153.k_ref, bf16[1024,512]{1,0:T(8,128)(2,1)S(1)} %get-tuple-element.154.v_ref, bf16[1024,512]{1,0:T(8,128)(2,1)S(1)} %fusion.44.grad_ref, ...), custom_call_target="tpu_custom_call" | custom-call | flops 16106127360 | bytes 12582912 | tf_op jit(solution)/shard_map/attn_bwd/pallas_call | solution.py:211
  163.6 6.8 %weight_grads.5 = bf16[1024,2048]{1,0:T(8,128)(2,1)} custom-call(s32[1]{0:T(128)} %bitcast.9.at_ref, bf16[1024,2048]{1,0:T(8,128)(2,1)S(1)} %copy-done.5, bf16[1024,1536]{1,0:T(8,128)(2,1)S(1)} %copy-done.12, bf16[1024,2048]{1,0:T(8,128)(2,1)S(1)} %copy-done, bf16[1024,512]{1,0:T(8,128)(2,1)S(1)} %copy-done.24), custom_call_target="tpu_custom_call" | custom-call | flops 4294967296 | bytes 12582912 | tf_op jit(solution)/shard_map/weight_grads/pallas_call | solution.py:330
  176.6 5.8 %weight_grads.6 = bf16[1024,2048]{1,0:T(8,128)(2,1)S(1)} custom-call(s32[1]{0:T(128)} %bitcast.5.at_ref, bf16[1024,2048]{1,0:T(8,128)(2,1)S(1)} %copy-done.6, bf16[1024,1536]{1,0:T(8,128)(2,1)S(1)} %copy-done.13, bf16[1024,2048]{1,0:T(8,128)(2,1)S(1)} %copy-done.1, bf16[1024,512]{1,0:T(8,128)(2,1)S(1)} %copy-done.25), custom_call_target="tpu_custom_call" | custom-call | flops 4294967296 | bytes 12582912 | tf_op jit(solution)/shard_map/weight_grads/pallas_call | solution.py:330
  185.7 5.5 collective-permute-start.12
  193.3 11.7 %add_convert_fusion.4 = (bf16[1024,1152]{1,0:T(8,128)(2,1)S(1)}, bf16[1024,1152]{1,0:T(8,128)(2,1)S(1)}) fusion(f32[1152]{0:T(1024)S(1)} %slice.228, bf16[1024,2048]{1,0:T(8,128)(2,1)} %norm_rows.7.left_a, bf16[2048,2304]{1,0:T(8,128)(2,1)} %all-gather.3.cloned.1.call-done), kind=kOutput, calls=%fused_computation.11 | convolution fusion | flops 4855431168 | bytes 13636096 | tf_op jit(solution)/shard_map/dot_general | solution.py:29
  205.1 5.8 %fusion.13.right_a = bf16[1024,1152]{1,0:T(8,128)(2,1)S(1)} fusion(bf16[1024,1152]{1,0:T(8,128)(2,1)S(1)} %get-tuple-element.167, bf16[1024,2048]{1,0:T(8,128)(2,1)S(1)} %copy-done.2, bf16[2048,2304]{1,0:T(8,128)(2,1)S(1)} %copy-done.73), kind=kOutput, calls=%fused_computation.22 | convolution fusion | flops 4835377152 | bytes 13631488 | tf_op jit(solution)/shard_map/dot_general | solution.py:29
  210.9 3.7 add_convert_fusion.11
  214.7 7.9 %weight_grads.7 = bf16[1024,2304]{1,0:T(8,128)(2,1)} custom-call(s32[1]{0:T(128)} %bitcast.9.at_ref, bf16[1024,2048]{1,0:T(8,128)(2,1)S(1)} %copy-done.7, bf16[1024,1152]{1,0:T(8,128)(2,1)S(1)} %fusion.13.right_a, bf16[1024,2048]{1,0:T(8,128)(2,1)S(1)} %copy-done.2, bf16[1024,1152]{1,0:T(8,128)(2,1)S(1)} %get-tuple-element.204.right_b), custom_call_target="tpu_custom_call" | custom-call | flops 4831838208 | bytes 13631488 | tf_op jit(solution)/shard_map/weight_grads/pallas_call | solution.py:330
  222.9 3.7 collective-permute-start.14
  237.2 6.9 %weight_grads.8 = bf16[1024,2304]{1,0:T(8,128)(2,1)S(1)} custom-call(s32[1]{0:T(128)} %bitcast.5.at_ref, bf16[1024,2048]{1,0:T(8,128)(2,1)S(1)} %copy-done.8, bf16[1024,1152]{1,0:T(8,128)(2,1)S(1)} %copy-done.28, bf16[1024,2048]{1,0:T(8,128)(2,1)S(1)} %copy-done.3, bf16[1024,1152]{1,0:T(8,128)(2,1)S(1)} %copy-done.37), custom_call_target="tpu_custom_call" | custom-call | flops 4831838208 | bytes 13631488 | tf_op jit(solution)/shard_map/weight_grads/pallas_call | solution.py:330
  244.1 8.7 %collective-permute-done.16 = bf16[256,1792]{1,0:T(8,128)(2,1)} collective-permute-done((bf16[256,1792]{1,0:T(8,128)(2,1)}, bf16[256,1792]{1,0:T(8,128)(2,1)}, u32[]{:S(2)}, u32[]{:S(2)}) %collective-permute-start.16) | collective-permute-done | bytes 917536 | tf_op jit(solution)/shard_map/ppermute | solution.py:439
  252.9 4.4 fusion.33
  260.3 11.1 %fusion.16 = bf16[1024,2048]{1,0:T(8,128)(2,1)} fusion(bf16[1024,1536]{1,0:T(8,128)(2,1)S(1)} %copy-done.13, bf16[2048,2048]{0,1:T(8,128)(2,1)} %all-gather.5.cloned.1.call-done), kind=kOutput, calls=%fused_computation.23 | convolution fusion | flops 6444548096 | bytes 13631488 | tf_op jit(solution)/shard_map/dot_general | solution.py:33
  271.4 5.9 %convolution_convert_fusion = bf16[1024,2048]{1,0:T(8,128)(2,1)} fusion(bf16[1024,512]{1,0:T(8,128)(2,1)S(1)} %copy-done.26, bf16[2048,2048]{0,1:T(8,128)(2,1)} %all-gather.5.cloned.1.call-done), kind=kOutput, calls=%fused_computation.24 | convolution fusion | flops 2149580800 | bytes 7340032 | tf_op jit(solution)/shard_map/dot_general | solution.py:33
  277.3 5.2 collective-permute-done.17
  286.4 3.2 pad_maximum_fusion.mine_ref
  293.2 3.4 collective-permute-start.24
  296.6 10.1 %add_convert_fusion.3 = bf16[1024,2048]{1,0:T(8,128)(2,1)} fusion(bf16[1024,2048]{1,0:T(8,128)(2,1)} %convolution_convert_fusion, bf16[1024,1152]{1,0:T(8,128)(2,1)S(1)} %copy-done.38, bf16[2048,2304]{1,0:T(8,128)(2,1)} %all-gather.3.cloned.1.call-done), kind=kOutput, calls=%fused_computation.3 | convolution fusion | flops 4838129664 | bytes 15466496 | tf_op jit(solution)/shard_map/dot_general | solution.py:33
  306.7 9.5 %collective-permute-done.20 = bf16[256,2048]{1,0:T(8,128)(2,1)S(1)} collective-permute-done((bf16[256,2048]{1,0:T(8,128)(2,1)}, bf16[256,2048]{1,0:T(8,128)(2,1)S(1)}, u32[]{:S(2)}, u32[]{:S(2)}) %collective-permute-start.20) | collective-permute-done | bytes 1048608 | tf_op jit(solution)/shard_map/ppermute | solution.py:401
  316.2 4.1 add_convert_fusion.9
  320.3 6.5 %collective-permute-start.22 = (bf16[256,2048]{1,0:T(8,128)(2,1)}, bf16[256,2048]{1,0:T(8,128)(2,1)}, u32[]{:S(2)}, u32[]{:S(2)}) collective-permute-start(bf16[256,2048]{1,0:T(8,128)(2,1)} %get-tuple-element.212), channel_id=1, source_target_pairs={{0,8},{4,12},{8,16},{12,20},{16,24},{20,28},{1,9},{5,13},{9,17},{1... | collective-permute-start | bytes 3145736 | tf_op jit(solution)/shard_map/ppermute | solution.py:401
  328.1 10.4 %weave.1 = bf16[2048,1792]{1,0:T(8,128)(2,1)} custom-call(s32[2]{0:T(128)} %pad_add_fusion.at_ref, bf16[1024,1792]{1,0:T(8,128)(2,1)} %pad_maximum_fusion.mine_ref, bf16[1024,1792]{1,0:T(8,128)(2,1)} %collective-permute-done.19.got_ref), custom_call_target="tpu_custom_call" | custom-call | bytes 22020096 | tf_op jit(solution)/shard_map/weave/pallas_call | solution.py:463
  338.5 9.7 %add_convert_fusion.5 = (bf16[1024,896]{1,0:T(8,128)(2,1)S(1)}, bf16[1024,896]{1,0:T(8,128)(2,1)S(1)}) fusion(f32[896]{0:T(1024)S(1)} %slice.233, bf16[1024,2048]{1,0:T(8,128)(2,1)} %norm_rows.7.left_a, bf16[2048,1792]{1,0:T(8,128)(2,1)} %weave.1), kind=kOutput, calls=%fused_computation.28 | convolution fusion | flops 3776446464 | bytes 11537920 | tf_op jit(solution)/shard_map/dot_general | solution.py:29
  348.3 4.5 multiply_convert_fusion.1.right_a
  352.9 4.9 fusion.31
  357.7 11.6 %weight_grads.9 = bf16[2048,1792]{1,0:T(8,128)(2,1)S(1)} custom-call(s32[1]{0:T(128)} %constant.140.clone.1.at_ref, bf16[1024,2048]{1,0:T(8,128)(2,1)S(1)} %copy-done.9, bf16[1024,896]{1,0:T(8,128)(2,1)S(1)} %multiply_convert_fusion.1.right_a, bf16[1024,2048]{1,0:T(8,128)(2,1)S(1)} %copy-done.4, bf16[1024,896]{1,0:T(8,128)(2,1)S(1)} %get-tuple-element.232.right_b), custom_call_target="tpu_custom_call" | custom-call | flops 7516192768 | bytes 19398656 | tf_op jit(solution)/shard_map/weight_grads/pallas_call | solution.py:330
  369.3 3.0 copy-done.18
  377.0 4.8 collective-permute-start.27
  382.9 7.4 %add_convert_fusion.2 = bf16[1024,2048]{1,0:T(8,128)(2,1)S(1)} fusion(bf16[1024,2048]{1,0:T(8,128)(2,1)} %add_convert_fusion.3, bf16[1024,896]{1,0:T(8,128)(2,1)S(1)} %get-tuple-element.232.right_b, bf16[2048,1792]{1,0:T(8,128)(2,1)} %weave.1), kind=kOutput, calls=%fused_computation.2 | convolution fusion | flops 3764387840 | bytes 13893632 | tf_op jit(solution)/shard_map/dot_general | solution.py:33
  396.9 35.9 %collective-permute-done.27 = bf16[256,2304]{1,0:T(8,128)(2,1)S(1)} collective-permute-done((bf16[256,2304]{1,0:T(8,128)(2,1)S(1)}, bf16[256,2304]{1,0:T(8,128)(2,1)S(1)}, u32[]{:S(2)}, u32[]{:S(2)}) %collective-permute-start.27) | collective-permute-done | bytes 1179680 | tf_op jit(solution)/shard_map/ppermute | solution.py:401
  435.4 8.4 %collective-permute-start.33 = (bf16[256,2304]{1,0:T(8,128)(2,1)S(1)}, bf16[256,2304]{1,0:T(8,128)(2,1)}, u32[]{:S(2)}, u32[]{:S(2)}) collective-permute-start(bf16[256,2304]{1,0:T(8,128)(2,1)S(1)} %get-tuple-element.247), channel_id=1, source_target_pairs={{0,8},{4,12},{8,16},{12,20},{16,24},{20,28},{1,9},{5,13},{9,17},{1... | collective-permute-start | bytes 3538952 | tf_op jit(solution)/shard_map/ppermute | solution.py:401
  445.1 10.3 %fusion.10 = f32[1024,2048]{1,0:T(8,128)} fusion(bf16[1024,1152]{1,0:T(8,128)(2,1)S(1)} %copy-done.29, bf16[2048,2304]{1,0:T(8,128)(2,1)} %all-gather.3.cloned.1.call-done), kind=kOutput, calls=%fused_computation.19 | convolution fusion | flops 4831838208 | bytes 15466496 | tf_op jit(solution)/shard_map/dot_general | solution.py:33
  455.4 9.1 %add_convert_fusion.refs_5_ = bf16[1024,2048]{1,0:T(8,128)(2,1)S(1)} fusion(f32[1024,2048]{1,0:T(8,128)} %fusion.10, bf16[1024,2048]{1,0:T(8,128)(2,1)} %fusion.16, bf16[1024,896]{1,0:T(8,128)(2,1)S(1)} %copy-done.35, bf16[2048,1792]{1,0:T(8,128)(2,1)} %weave.1), kind=kOutput, calls=%fused_computation | convolution fusion | flops 3770679296 | bytes 22282240 | tf_op jit(solution)/shard_map/dot_general | solution.py:33
  468.2 2.9 convert_add_fusion.6
  477.5 15.9 %collective-permute-done.33 = bf16[256,2304]{1,0:T(8,128)(2,1)} collective-permute-done((bf16[256,2304]{1,0:T(8,128)(2,1)S(1)}, bf16[256,2304]{1,0:T(8,128)(2,1)}, u32[]{:S(2)}, u32[]{:S(2)}) %collective-permute-start.33) | collective-permute-done | bytes 1179680 | tf_op jit(solution)/shard_map/ppermute | solution.py:401
  496.0 4.1 norm_sums.1
  507.5 5.0 collective-permute-done.38
  512.4 3.0 collective-permute-done.37
  (377 shorter events, 160.0 us)
Async XLA Ops:
  7.2 93.5 %all-gather.5.cloned.1.call-start = ((), (), s32[]{:S(2)}) async-start(), calls=%async_computation.2 | async-start | bytes 9437184 | tf_op jit(solution)/shard_map/all_gather | solution.py:639
  12.8 180.5 %all-gather.3.cloned.1.call-start = ((), (), s32[]{:S(2)}) async-start(), calls=%async_computation.1 | async-start | bytes 10616832 | tf_op jit(solution)/shard_map/all_gather | solution.py:652
  13.4 4.6 collective-permute-start.2
  13.9 27.0 %collective-permute-start.1 = (bf16[256,2048]{1,0:T(8,128)(2,1)S(1)}, bf16[256,2048]{1,0:T(8,128)(2,1)S(1)}, u32[]{:S(2)}, u32[]{:S(2)}) collective-permute-start(bf16[256,2048]{1,0:T(8,128)(2,1)S(1)} %copy-done.10), channel_id=1, source_target_pairs={{0,2},{1,3},{2,0},{3,1},{4,6},{5,7},{6,4},{7,5},{8,10},{9,11},{10,... | collective-permute-start | bytes 3145736 | tf_op jit(solution)/shard_map/ppermute | solution.py:645
  16.5 25.2 %collective-permute-start = (bf16[256,2048]{1,0:T(8,128)(2,1)S(1)}, bf16[256,2048]{1,0:T(8,128)(2,1)S(1)}, u32[]{:S(2)}, u32[]{:S(2)}) collective-permute-start(bf16[256,2048]{1,0:T(8,128)(2,1)S(1)} %copy-done.10), channel_id=1, source_target_pairs={{0,1},{1,0},{2,3},{3,2},{4,5},{5,4},{6,7},{7,6},{8,9},{9,8},{10,11... | collective-permute-start | bytes 3145736 | tf_op jit(solution)/shard_map/ppermute | solution.py:645
  18.1 7.0 %collective-permute-start.3 = (bf16[8,1472]{1,0:T(8,128)(2,1)S(1)}, bf16[8,1472]{1,0:T(8,128)(2,1)S(1)}, u32[]{:S(2)}, u32[]{:S(2)}) collective-permute-start(bf16[8,1472]{1,0:T(8,128)(2,1)S(1)} %fusion.57), channel_id=1, source_target_pairs={{0,8},{4,12},{8,0},{12,4},{16,24},{20,28},{24,16},{28,20},{1,9},{5... | collective-permute-start | bytes 70664 | tf_op jit(solution)/shard_map/ppermute | solution.py:556
  25.2 15.7 %collective-permute-start.4 = (bf16[8,1472]{1,0:T(8,128)(2,1)S(1)}, bf16[8,1472]{1,0:T(8,128)(2,1)S(1)}, u32[]{:S(2)}, u32[]{:S(2)}) collective-permute-start(bf16[8,1472]{1,0:T(8,128)(2,1)S(1)} %fusion.83), channel_id=1, source_target_pairs={{0,16},{4,20},{8,24},{12,28},{16,0},{20,4},{24,8},{28,12},{1,17},{... | collective-permute-start | bytes 70664 | tf_op jit(solution)/shard_map/ppermute | solution.py:556
  40.9 129.7 %copy-start.64 = (bf16[8,1472]{1,0:T(8,128)(2,1)}, bf16[8,1472]{1,0:T(8,128)(2,1)S(1)}, u32[]{:S(2)}) copy-start(bf16[8,1472]{1,0:T(8,128)(2,1)S(1)} %add.390) | copy-start | bytes 70660
  41.7 487.7 %reduce-scatter.2.cloned.1.call-start = ((), (), s32[]{:S(2)}) async-start(), calls=%async_computation.3 | async-start | bytes 8257536 | tf_op jit(solution)/shard_map/reduce_scatter | solution.py:729
  41.8 26.4 %collective-permute-start.8 = (bf16[256,2048]{1,0:T(8,128)(2,1)}, bf16[256,2048]{1,0:T(8,128)(2,1)}, u32[]{:S(2)}, u32[]{:S(2)}) collective-permute-start(bf16[256,2048]{1,0:T(8,128)(2,1)} %refs_1_.1), channel_id=1, source_target_pairs={{0,2},{1,3},{2,0},{3,1},{4,6},{5,7},{6,4},{7,5},{8,10},{9,11},{10,... | collective-permute-start | bytes 3145736 | tf_op jit(solution)/shard_map/ppermute | solution.py:645
  42.5 26.3 %collective-permute-start.7 = (bf16[256,2048]{1,0:T(8,128)(2,1)}, bf16[256,2048]{1,0:T(8,128)(2,1)}, u32[]{:S(2)}, u32[]{:S(2)}) collective-permute-start(bf16[256,2048]{1,0:T(8,128)(2,1)} %refs_1_.1), channel_id=1, source_target_pairs={{0,1},{1,0},{2,3},{3,2},{4,5},{5,4},{6,7},{7,6},{8,9},{9,8},{10,11... | collective-permute-start | bytes 3145736 | tf_op jit(solution)/shard_map/ppermute | solution.py:645
  49.4 35.8 %collective-permute-start.6 = (bf16[256,1024]{1,0:T(8,128)(2,1)}, bf16[256,1024]{1,0:T(8,128)(2,1)S(1)}, u32[]{:S(2)}, u32[]{:S(2)}) collective-permute-start(bf16[256,1024]{1,0:T(8,128)(2,1)} %slice.203), channel_id=1, source_target_pairs={{0,1},{1,0},{2,3},{3,2},{4,5},{5,4},{6,7},{7,6},{8,9},{9,8},{10,11... | collective-permute-start | bytes 1572872 | tf_op jit(solution)/shard_map/ppermute | solution.py:645
  50.1 35.2 %collective-permute-start.5 = (bf16[256,1024]{1,0:T(8,128)(2,1)}, bf16[256,1024]{1,0:T(8,128)(2,1)S(1)}, u32[]{:S(2)}, u32[]{:S(2)}) collective-permute-start(bf16[256,1024]{1,0:T(8,128)(2,1)} %slice.202), channel_id=1, source_target_pairs={{0,2},{1,3},{2,0},{3,1},{4,6},{5,7},{6,4},{7,5},{8,10},{9,11},{10,... | collective-permute-start | bytes 1572872 | tf_op jit(solution)/shard_map/ppermute | solution.py:645
  72.5 16.7 %collective-permute-start.10 = (bf16[256,1024]{1,0:T(8,128)(2,1)}, bf16[256,1024]{1,0:T(8,128)(2,1)S(1)}, u32[]{:S(2)}, u32[]{:S(2)}) collective-permute-start(bf16[256,1024]{1,0:T(8,128)(2,1)} %slice.207), channel_id=1, source_target_pairs={{0,1},{1,0},{2,3},{3,2},{4,5},{5,4},{6,7},{7,6},{8,9},{9,8},{10,11... | collective-permute-start | bytes 1572872 | tf_op jit(solution)/shard_map/ppermute | solution.py:645
  73.9 15.3 %collective-permute-start.9 = (bf16[256,1024]{1,0:T(8,128)(2,1)}, bf16[256,1024]{1,0:T(8,128)(2,1)}, u32[]{:S(2)}, u32[]{:S(2)}) collective-permute-start(bf16[256,1024]{1,0:T(8,128)(2,1)} %slice.206), channel_id=1, source_target_pairs={{0,2},{1,3},{2,0},{3,1},{4,6},{5,7},{6,4},{7,5},{8,10},{9,11},{10,... | collective-permute-start | bytes 1572872 | tf_op jit(solution)/shard_map/ppermute | solution.py:645
  170.3 40.6 %collective-permute-start.11 = (bf16[1024,2048]{1,0:T(8,128)(2,1)}, bf16[1024,2048]{1,0:T(8,128)(2,1)}, u32[]{:S(2)}, u32[]{:S(2)}) collective-permute-start(bf16[1024,2048]{1,0:T(8,128)(2,1)} %weight_grads.5), channel_id=1, source_target_pairs={{0,4},{4,0},{8,12},{12,8},{16,20},{20,16},{24,28},{28,24},{1,5},{5... | collective-permute-start | bytes 12582920 | tf_op jit(solution)/shard_map/ppermute | solution.py:369
  184.4 26.5 %collective-permute-start.13 = (bf16[256,1792]{1,0:T(8,128)(2,1)}, bf16[256,1792]{1,0:T(8,128)(2,1)}, u32[]{:S(2)}, u32[]{:S(2)}) collective-permute-start(bf16[256,1792]{1,0:T(8,128)(2,1)} %pad_maximum_fusion.8), channel_id=1, source_target_pairs={{28,20},{24,16},{20,12},{16,8},{12,4},{8,0},{29,21},{25,17},{21,13... | collective-permute-start | bytes 2752520 | tf_op jit(solution)/shard_map/ppermute | solution.py:439
  185.7 25.2 %collective-permute-start.12 = (bf16[256,1792]{1,0:T(8,128)(2,1)}, bf16[256,1792]{1,0:T(8,128)(2,1)}, u32[]{:S(2)}, u32[]{:S(2)}) collective-permute-start(bf16[256,1792]{1,0:T(8,128)(2,1)} %pad_maximum_fusion.8), channel_id=1, source_target_pairs={{0,8},{4,12},{8,16},{12,20},{16,24},{20,28},{1,9},{5,13},{9,17},{1... | collective-permute-start | bytes 2752520 | tf_op jit(solution)/shard_map/ppermute | solution.py:439
  222.6 59.8 %collective-permute-start.18 = (bf16[1024,2304]{1,0:T(8,128)(2,1)}, bf16[1024,2304]{1,0:T(8,128)(2,1)}, u32[]{:S(2)}, u32[]{:S(2)}) collective-permute-start(bf16[1024,2304]{1,0:T(8,128)(2,1)} %weight_grads.7), channel_id=1, source_target_pairs={{0,4},{4,0},{8,12},{12,8},{16,20},{20,16},{24,28},{28,24},{1,5},{5... | collective-permute-start | bytes 14155784 | tf_op jit(solution)/shard_map/ppermute | solution.py:369
  222.9 30.0 %collective-permute-start.14 = (bf16[256,2048]{1,0:T(8,128)(2,1)}, bf16[256,2048]{1,0:T(8,128)(2,1)}, u32[]{:S(2)}, u32[]{:S(2)}) collective-permute-start(bf16[256,2048]{1,0:T(8,128)(2,1)} %add_convert_fusion.11), channel_id=1, source_target_pairs={{0,8},{4,12},{28,20},{24,16},{1,9},{5,13},{29,21},{25,17},{2,10},{... | collective-permute-start | bytes 3145736 | tf_op jit(solution)/shard_map/ppermute | solution.py:399
  226.6 17.6 %collective-permute-start.15 = (bf16[256,1792]{1,0:T(8,128)(2,1)}, bf16[256,1792]{1,0:T(8,128)(2,1)}, u32[]{:S(2)}, u32[]{:S(2)}) collective-permute-start(bf16[256,1792]{1,0:T(8,128)(2,1)} %collective-permute-done.12), channel_id=1, source_target_pairs={{8,16},{12,20},{16,24},{20,28},{9,17},{13,21},{17,25},{21,29},{10,... | collective-permute-start | bytes 2752520 | tf_op jit(solution)/shard_map/ppermute | solution.py:439
  228.2 24.7 %collective-permute-start.16 = (bf16[256,1792]{1,0:T(8,128)(2,1)}, bf16[256,1792]{1,0:T(8,128)(2,1)}, u32[]{:S(2)}, u32[]{:S(2)}) collective-permute-start(bf16[256,1792]{1,0:T(8,128)(2,1)} %collective-permute-done.13), channel_id=1, source_target_pairs={{20,12},{16,8},{12,4},{8,0},{21,13},{17,9},{13,5},{9,1},{22,14},{1... | collective-permute-start | bytes 2752520 | tf_op jit(solution)/shard_map/ppermute | solution.py:439
  258.8 23.6 %collective-permute-start.17 = (bf16[256,1792]{1,0:T(8,128)(2,1)S(1)}, bf16[256,1792]{1,0:T(8,128)(2,1)S(1)}, u32[]{:S(2)}, u32[]{:S(2)}) collective-permute-start(bf16[256,1792]{1,0:T(8,128)(2,1)S(1)} %get-tuple-element.189), channel_id=1, source_target_pairs={{16,24},{20,28},{12,4},{8,0},{17,25},{21,29},{13,5},{9,1},{18,26},... | collective-permute-start | bytes 2752520 | tf_op jit(solution)/shard_map/ppermute | solution.py:437
  289.6 26.6 %collective-permute-start.19 = (bf16[1024,1792]{1,0:T(8,128)(2,1)}, bf16[1024,1792]{1,0:T(8,128)(2,1)}, u32[]{:S(2)}, u32[]{:S(2)}) collective-permute-start(bf16[1024,1792]{1,0:T(8,128)(2,1)} %pad_maximum_fusion.mine_ref), channel_id=1, source_target_pairs={{0,4},{4,0},{8,12},{12,8},{16,20},{20,16},{24,28},{28,24},{1,5},{5... | collective-permute-start | bytes 11010056 | tf_op jit(solution)/shard_map/ppermute | solution.py:432
  290.4 25.8 %collective-permute-start.20 = (bf16[256,2048]{1,0:T(8,128)(2,1)}, bf16[256,2048]{1,0:T(8,128)(2,1)S(1)}, u32[]{:S(2)}, u32[]{:S(2)}) collective-permute-start(bf16[256,2048]{1,0:T(8,128)(2,1)} %get-tuple-element.201), channel_id=1, source_target_pairs={{0,8},{4,12},{8,16},{12,20},{1,9},{5,13},{9,17},{13,21},{2,10},{6,... | collective-permute-start | bytes 3145736 | tf_op jit(solution)/shard_map/ppermute | solution.py:401
  292.4 23.8 %collective-permute-start.21 = (bf16[256,2048]{1,0:T(8,128)(2,1)S(1)}, bf16[256,2048]{1,0:T(8,128)(2,1)S(1)}, u32[]{:S(2)}, u32[]{:S(2)}) collective-permute-start(bf16[256,2048]{1,0:T(8,128)(2,1)S(1)} %copy-done.48), channel_id=1, source_target_pairs={{28,20},{24,16},{20,12},{16,8},{29,21},{25,17},{21,13},{17,9},{30,... | collective-permute-start | bytes 3145736 | tf_op jit(solution)/shard_map/ppermute | solution.py:401
  293.2 59.7 %collective-permute-start.24 = (bf16[256,2304]{1,0:T(8,128)(2,1)}, bf16[256,2304]{1,0:T(8,128)(2,1)}, u32[]{:S(2)}, u32[]{:S(2)}) collective-permute-start(bf16[256,2304]{1,0:T(8,128)(2,1)} %add_convert_fusion.8), channel_id=1, source_target_pairs={{0,8},{4,12},{28,20},{24,16},{1,9},{5,13},{29,21},{25,17},{2,10},{... | collective-permute-start | bytes 3538952 | tf_op jit(solution)/shard_map/ppermute | solution.py:399
  320.3 52.0 %collective-permute-start.22 = (bf16[256,2048]{1,0:T(8,128)(2,1)}, bf16[256,2048]{1,0:T(8,128)(2,1)}, u32[]{:S(2)}, u32[]{:S(2)}) collective-permute-start(bf16[256,2048]{1,0:T(8,128)(2,1)} %get-tuple-element.212), channel_id=1, source_target_pairs={{0,8},{4,12},{8,16},{12,20},{16,24},{20,28},{1,9},{5,13},{9,17},{1... | collective-permute-start | bytes 3145736 | tf_op jit(solution)/shard_map/ppermute | solution.py:401
  326.8 45.5 %collective-permute-start.23 = (bf16[256,2048]{1,0:T(8,128)(2,1)}, bf16[256,2048]{1,0:T(8,128)(2,1)}, u32[]{:S(2)}, u32[]{:S(2)}) collective-permute-start(bf16[256,2048]{1,0:T(8,128)(2,1)} %get-tuple-element.213), channel_id=1, source_target_pairs={{28,20},{24,16},{20,12},{16,8},{12,4},{8,0},{29,21},{25,17},{21,13... | collective-permute-start | bytes 3145736 | tf_op jit(solution)/shard_map/ppermute | solution.py:401
  374.5 58.3 %slice-start.2 = ((s8[4718592]{0:T(1024)(128)(4,1)}), s8[4194304]{0:T(1024)(128)(4,1)S(1)}, s32[]{:S(2)}) async-start(s8[4718592]{0:T(1024)(128)(4,1)} %bitcast.69), calls=%async_computation.6 | async-start | bytes 8388608
  377.0 55.8 %slice-start.3 = ((s8[4718592]{0:T(1024)(128)(4,1)}), s8[524288]{0:T(1024)(128)(4,1)S(1)}, s32[]{:S(2)}) async-start(s8[4718592]{0:T(1024)(128)(4,1)} %bitcast.69), calls=%async_computation.7 | async-start | bytes 1048576
  377.0 55.8 %collective-permute-start.27 = (bf16[256,2304]{1,0:T(8,128)(2,1)S(1)}, bf16[256,2304]{1,0:T(8,128)(2,1)S(1)}, u32[]{:S(2)}, u32[]{:S(2)}) collective-permute-start(bf16[256,2304]{1,0:T(8,128)(2,1)S(1)} %copy-done.47), channel_id=1, source_target_pairs={{0,8},{4,12},{8,16},{12,20},{1,9},{5,13},{9,17},{13,21},{2,10},{6,... | collective-permute-start | bytes 3538952 | tf_op jit(solution)/shard_map/ppermute | solution.py:401
  381.8 51.0 %collective-permute-start.28 = (bf16[256,2304]{1,0:T(8,128)(2,1)S(1)}, bf16[256,2304]{1,0:T(8,128)(2,1)S(1)}, u32[]{:S(2)}, u32[]{:S(2)}) collective-permute-start(bf16[256,2304]{1,0:T(8,128)(2,1)S(1)} %copy-done.46), channel_id=1, source_target_pairs={{28,20},{24,16},{20,12},{16,8},{29,21},{25,17},{21,13},{17,9},{30,... | collective-permute-start | bytes 3538952 | tf_op jit(solution)/shard_map/ppermute | solution.py:401
  392.7 71.8 %collective-permute-start.25 = (bf16[512,1024]{1,0:T(8,128)(2,1)}, bf16[512,1024]{1,0:T(8,128)(2,1)}, u32[]{:S(2)}, u32[]{:S(2)}) collective-permute-start(bf16[512,1024]{1,0:T(8,128)(2,1)} %pad_maximum_fusion.4), channel_id=1, source_target_pairs={{0,1},{1,0},{2,3},{3,2},{4,5},{5,4},{6,7},{7,6},{8,9},{9,8},{10,11... | collective-permute-start | bytes 3145736 | tf_op jit(solution)/shard_map/ppermute | solution.py:524
  395.5 69.0 %collective-permute-start.26 = (bf16[512,1024]{1,0:T(8,128)(2,1)}, bf16[512,1024]{1,0:T(8,128)(2,1)}, u32[]{:S(2)}, u32[]{:S(2)}) collective-permute-start(bf16[512,1024]{1,0:T(8,128)(2,1)} %pad_maximum_fusion.5), channel_id=1, source_target_pairs={{0,2},{1,3},{2,0},{3,1},{4,6},{5,7},{6,4},{7,5},{8,10},{9,11},{10,... | collective-permute-start | bytes 3145736 | tf_op jit(solution)/shard_map/ppermute | solution.py:524
  435.4 57.9 %collective-permute-start.33 = (bf16[256,2304]{1,0:T(8,128)(2,1)S(1)}, bf16[256,2304]{1,0:T(8,128)(2,1)}, u32[]{:S(2)}, u32[]{:S(2)}) collective-permute-start(bf16[256,2304]{1,0:T(8,128)(2,1)S(1)} %get-tuple-element.247), channel_id=1, source_target_pairs={{0,8},{4,12},{8,16},{12,20},{16,24},{20,28},{1,9},{5,13},{9,17},{1... | collective-permute-start | bytes 3538952 | tf_op jit(solution)/shard_map/ppermute | solution.py:401
  443.8 52.2 %collective-permute-start.34 = (bf16[256,2304]{1,0:T(8,128)(2,1)S(1)}, bf16[256,2304]{1,0:T(8,128)(2,1)}, u32[]{:S(2)}, u32[]{:S(2)}) collective-permute-start(bf16[256,2304]{1,0:T(8,128)(2,1)S(1)} %get-tuple-element.248), channel_id=1, source_target_pairs={{28,20},{24,16},{20,12},{16,8},{12,4},{8,0},{29,21},{25,17},{21,13... | collective-permute-start | bytes 3538952 | tf_op jit(solution)/shard_map/ppermute | solution.py:401
  464.8 35.3 %collective-permute-start.31 = (bf16[512,1024]{1,0:T(8,128)(2,1)S(1)}, bf16[512,1024]{1,0:T(8,128)(2,1)S(1)}, u32[]{:S(2)}, u32[]{:S(2)}) collective-permute-start(bf16[512,1024]{1,0:T(8,128)(2,1)S(1)} %pad_maximum_fusion.6), channel_id=1, source_target_pairs={{0,1},{1,0},{2,3},{3,2},{4,5},{5,4},{6,7},{7,6},{8,9},{9,8},{10,11... | collective-permute-start | bytes 3145736 | tf_op jit(solution)/shard_map/ppermute | solution.py:524
  466.7 33.4 %collective-permute-start.32 = (bf16[512,1024]{1,0:T(8,128)(2,1)S(1)}, bf16[512,1024]{1,0:T(8,128)(2,1)S(1)}, u32[]{:S(2)}, u32[]{:S(2)}) collective-permute-start(bf16[512,1024]{1,0:T(8,128)(2,1)S(1)} %pad_maximum_fusion.7), channel_id=1, source_target_pairs={{0,2},{1,3},{2,0},{3,1},{4,6},{5,7},{6,4},{7,5},{8,10},{9,11},{10,... | collective-permute-start | bytes 3145736 | tf_op jit(solution)/shard_map/ppermute | solution.py:524
  476.8 27.5 %collective-permute-start.30 = (bf16[256,1024]{1,0:T(8,128)(2,1)S(1)}, bf16[256,1024]{1,0:T(8,128)(2,1)S(1)}, u32[]{:S(2)}, u32[]{:S(2)}) collective-permute-start(bf16[256,1024]{1,0:T(8,128)(2,1)S(1)} %get-tuple-element.328), channel_id=1, source_target_pairs={{0,1},{1,0},{2,3},{3,2},{4,5},{5,4},{6,7},{7,6},{8,9},{9,8},{10,11... | collective-permute-start | bytes 1572872 | tf_op jit(solution)/shard_map/ppermute | solution.py:536
  493.3 12.5 %collective-permute-start.29 = (bf16[256,1024]{1,0:T(8,128)(2,1)S(1)}, bf16[256,1024]{1,0:T(8,128)(2,1)S(1)}, u32[]{:S(2)}, u32[]{:S(2)}) collective-permute-start(bf16[256,1024]{1,0:T(8,128)(2,1)S(1)} %get-tuple-element.329), channel_id=1, source_target_pairs={{0,2},{1,3},{2,0},{3,1},{4,6},{5,7},{6,4},{7,5},{8,10},{9,11},{10,... | collective-permute-start | bytes 1572872 | tf_op jit(solution)/shard_map/ppermute | solution.py:536
  501.0 11.4 %collective-permute-start.38 = (bf16[256,1024]{1,0:T(8,128)(2,1)S(1)}, bf16[256,1024]{1,0:T(8,128)(2,1)S(1)}, u32[]{:S(2)}, u32[]{:S(2)}) collective-permute-start(bf16[256,1024]{1,0:T(8,128)(2,1)S(1)} %get-tuple-element.320), channel_id=1, source_target_pairs={{0,1},{1,0},{2,3},{3,2},{4,5},{5,4},{6,7},{7,6},{8,9},{9,8},{10,11... | collective-permute-start | bytes 1572872 | tf_op jit(solution)/shard_map/ppermute | solution.py:536
  502.4 12.9 %collective-permute-start.37 = (bf16[256,1024]{1,0:T(8,128)(2,1)S(1)}, bf16[256,1024]{1,0:T(8,128)(2,1)S(1)}, u32[]{:S(2)}, u32[]{:S(2)}) collective-permute-start(bf16[256,1024]{1,0:T(8,128)(2,1)S(1)} %get-tuple-element.321), channel_id=1, source_target_pairs={{0,2},{1,3},{2,0},{3,1},{4,6},{5,7},{6,4},{7,5},{8,10},{9,11},{10,... | collective-permute-start | bytes 1572872 | tf_op jit(solution)/shard_map/ppermute | solution.py:536
  520.7 4.2 collective-permute-start.35
  524.9 3.9 collective-permute-start.36
  534.2 1.2 collective-permute-start.39
  535.4 4.6 collective-permute-start.40
  540.0 6.0 %collective-permute-start.41 = (f32[76,128]{1,0:T(8,128)S(1)}, f32[76,128]{1,0:T(8,128)S(1)}, u32[]{:S(2)}, u32[]{:S(2)}) collective-permute-start(f32[76,128]{1,0:T(8,128)S(1)} %add.471), channel_id=1, source_target_pairs={{0,16},{4,20},{8,24},{12,28},{16,0},{20,4},{24,8},{28,12},{1,17},{... | collective-permute-start | bytes 116744 | tf_op jit(solution)/shard_map/ppermute | solution.py:556
  (76 other events, 599.4 us)
Sparse Core Ops, SparseCore 0:
  13.0 87.7 all-gather.4
  102.9 90.3 all-gather.2
  372.4 130.7 reduce-scatter.1
